TPU v7x, 32 devices: a whole 2x2x4 slice. The times are simulated.
32 devices in a mesh: grp: 2 (over y), gx: 4 (over z), gy: 2 (over x), gz: 2 (over core).
Axes of the slice: x: 2, y: 2, z: 4, core: 2. Of those that a mesh axis runs over, the one named last changes fastest.
Arguments:
- basis_modes: float32 [128, 64, 16, 256], P(None, ('grp', 'gx'), 'gy', 'gz'), parts along dimension 1, may hold values from -13 to 13
- reduced_state: float32 [256, 32], P('grp'), parts along dimension 0, may hold values from -0.6 to 0.6
- fine_state: bfloat16 [32, 64, 16, 256], P(None, ('grp', 'gx'), 'gy', 'gz'), parts along dimension 1, may hold values from -27 to 27
- bound_state: float32 [32, 64, 16, 256], P(None, ('grp', 'gx'), 'gy', 'gz'), parts along dimension 1, may hold values from 0 to 0.5
- velocity: float32 [64, 16, 256], P(('grp', 'gx'), 'gy', 'gz'), parts along dimension 0, may hold values from 0.1 to 0.5
- zone_labels: int32 [64, 16, 256], P(('grp', 'gx'), 'gy', 'gz'), parts along dimension 0, may hold values from 0 to 3
- capacity: float32 [3], replicated, may hold values from 0.5 to 2
- on_rate: float32 [32], replicated, may hold values from 0.02 to 0.1
- off_rate: float32 [32], replicated, may hold values from 0.02 to 0.3
- inlet_level: float32 [64], P('grp'), parts along dimension 0, may hold values from 0.5 to 5
Outputs:
- new_modes: float32 [32, 64, 16, 256], P(None, ('grp', 'gx'), 'gy', 'gz'), parts along dimension 1
- factor: float32 [64, 32], P('grp'), parts along dimension 0
- coefficients: float32 [256, 32], P('grp'), parts along dimension 0
- bound_next: float32 [32, 64, 16, 256], P(None, ('grp', 'gx'), 'gy', 'gz'), parts along dimension 1
There are 2 independent parts, one for each index of `grp`. A program takes and returns all parts, laid end to end along the dimension named above; an argument that names none is the same for every part. Nothing has to cross between parts.
All inputs are finite; a program needn't handle non-finite values.
Results may differ from a plain program's by a relative error of at most 0.0003.
Values sent between devices are 32-bit elements; how exact they have to be, the bound alone decides.
No kernel may reach another device: no remote copies, remote signals or barrier semaphores. Data moves between devices by JAX's collectives and lax.ppermute only.
A program may use at most 64 MiB of HBM per device.

v0:
```python
import functools

import jax
import jax.numpy as jnp
from jax import lax
from jax.experimental import pallas as pl
from jax.experimental.pallas import tpu as pltpu
from jax.sharding import PartitionSpec as P

highest = lax.Precision.HIGHEST
diffusion_number = 0.03
f32 = jnp.float32
bf16 = jnp.bfloat16


def split(value):
    high = value.astype(bf16)
    return high, (value - high.astype(f32)).astype(bf16)


def mm(a, b):
    return jnp.dot(a, b, preferred_element_type=f32)


def mm_nt(a, b):
    return lax.dot_general(a, b, (((1,), (1,)), ((), ())), preferred_element_type=f32)


def mm_exact(a, b):
    return jnp.dot(a, b, precision=highest, preferred_element_type=f32)


def face_count(axis):
    size = lax.axis_size(axis)
    return 0 if size == 1 else 1 if size == 2 else 2


def store_pair(refs, axis, low, high, put):
    if len(refs) == 1:
        put(refs[0], jnp.where(lax.axis_index(axis) == 0, high, low))
    elif len(refs) == 2:
        put(refs[0], low)
        put(refs[1], high)


def put_lanes(start, size):
    def put(ref, value):
        ref[:, pl.ds(start, size)] = value

    return put


def pack_column(refs, axis, tile, cell):
    lanes = tile.shape[1]
    here = lax.broadcasted_iota(jnp.int32, tile.shape, 1) == cell

    def put(ref, shift):
        ref[...] = jnp.where(here, pltpu.roll(tile, shift, 1), ref[...])

    if len(refs) == 1:
        high = lax.axis_index(axis) == 0
        put(refs[0], jnp.where(high, lax.rem(cell + 1, lanes), cell))
    elif len(refs) == 2:
        put(refs[0], cell)
        put(refs[1], lax.rem(cell + 1, lanes))


def emit_faces(faces, slab, x, shape):
    _, nx, ny, nz = shape
    xf, yf, zf = faces

    @pl.when(x == 0)
    def _():
        if len(xf) == 2:
            xf[0][...] = slab
        elif len(xf) == 1:
            xf[0][...] = slab

    @pl.when(x == nx - 1)
    def _():
        if len(xf) == 2:
            xf[1][...] = slab
        elif len(xf) == 1:

            @pl.when(lax.axis_index("gx") == 0)
            def _():
                xf[0][...] = slab

    store_pair(yf, "gy", slab[:, :nz], slab[:, -nz:], put_lanes(pl.multiple_of(x * nz, nz), nz))
    for y in range(ny):
        pack_column(zf, "gz", slab[:, y * nz : (y + 1) * nz], x * ny + y)


def face_shapes(shape):
    ns, nx, ny, nz = shape
    return (
        [(ns, ny * nz)] * face_count("gx"),
        [(ns, nx * nz)] * face_count("gy"),
        [(ns, nz)] * face_count("gz"),
    )


def unflatten(flat, shape):
    out = []
    for axis in ("gx", "gy", "gz"):
        n = face_count(axis)
        out.append(list(flat[:n]))
        flat = flat[n:]
    return out, flat


def exchange(faces):
    got = []
    for axis, sent in zip(("gx", "gy", "gz"), faces, strict=True):
        size = lax.axis_size(axis)
        if len(sent) == 1:
            got.append([lax.ppermute(sent[0], axis, [(0, 1), (1, 0)])])
        elif len(sent) == 2:
            up = [(i, i + 1) for i in range(size - 1)]
            down = [(j, i) for i, j in up]
            got.append([lax.ppermute(sent[1], axis, up), lax.ppermute(sent[0], axis, down)])
        else:
            got.append([])
    return got


def start_kernel(shape, nk, reduced, basis, fine, out_a, out_b, *rest):
    ns, nx, ny, nz = shape
    faces, (rows,) = unflatten(rest, shape)
    x = pl.program_id(0)

    @pl.when(x == 0)
    def _():
        for ref in faces[2]:
            ref[...] = jnp.zeros(ref.shape, f32)

    r_high, r_low = split(reduced[...].T)
    flat = basis.reshape(nk * ny, nz)
    rows[...] = fine[...].reshape(ns * ny, nz).astype(f32)
    tiles = []
    for y in range(ny):
        high, low = split(flat[pl.ds(y, nk, stride=ny), :])
        out_b[:nk, y * nz : (y + 1) * nz] = high
        out_b[nk:, y * nz : (y + 1) * nz] = low
    both = out_b[...]
    slab = mm(jnp.concatenate([r_high, r_high], axis=1), both) + mm(r_low, both[:nk])
    for y in range(ny):
        tiles.append(slab[:, y * nz : (y + 1) * nz] + rows[pl.ds(y, ns, stride=ny), :])
    slab = jnp.concatenate(tiles, axis=1)
    out_a[...] = slab
    emit_faces(faces, slab, x, shape)


def start(reduced, basis, fine):
    nk = basis.shape[0]
    ns, nx, ny, nz = shape = fine.shape
    whole = lambda s: pl.BlockSpec(s, lambda x: (0,) * len(s))
    groups = [s for g in face_shapes(shape) for s in g]
    outs = pl.pallas_call(
        functools.partial(start_kernel, shape, nk),
        grid=(nx,),
        in_specs=[
            whole((nk, ns)),
            pl.BlockSpec((nk, 1, ny, nz), lambda x: (0, x, 0, 0)),
            pl.BlockSpec((ns, 1, ny, nz), lambda x: (0, x, 0, 0)),
        ],
        out_specs=[
            pl.BlockSpec((ns, ny * nz), lambda x: (0, x)),
            pl.BlockSpec((2 * nk, ny * nz), lambda x: (0, x)),
        ]
        + [whole(s) for s in groups],
        out_shape=[
            jax.ShapeDtypeStruct((ns, nx * ny * nz), f32),
            jax.ShapeDtypeStruct((2 * nk, nx * ny * nz), bf16),
        ]
        + [jax.ShapeDtypeStruct(s, f32) for s in groups],
        scratch_shapes=[pltpu.VMEM((ns * ny, nz), f32)],
        name="start",
    )(reduced, basis, fine)
    faces, _ = unflatten(outs[2:], shape)
    return outs[0], outs[1], faces


def bb_kernel(nk, both, out):
    i = pl.program_id(0)
    product = mm_nt(both[:nk, :], both[...])
    mixed = product[:, nk:]
    product = product[:, :nk] + mixed + mixed.T

    @pl.when(i == 0)
    def _():
        out[...] = product

    @pl.when(i > 0)
    def _():
        out[...] = out[...] + product


def basis_products(both, steps):
    nk = both.shape[0] // 2
    return pl.pallas_call(
        functools.partial(bb_kernel, nk),
        grid=(steps,),
        in_specs=[pl.BlockSpec((2 * nk, both.shape[1] // steps), lambda i: (0, i))],
        out_specs=pl.BlockSpec((nk, nk), lambda i: (0, 0)),
        out_shape=jax.ShapeDtypeStruct((nk, nk), f32),
        name="basis_products",
    )(both)


def beside_of(got, at_start):
    return got[0] if len(got) == 1 else got[0 if at_start else 1]


def stencil(shape, x, pad, y_got, z_got, bound_tile, store, args):
    velocity, zone_labels, capacity, rates = args
    ns, nx, ny, nz = shape
    first = {a: lax.axis_index(a) == 0 for a in ("gy", "gz")}
    last = {a: lax.axis_index(a) == lax.axis_size(a) - 1 for a in ("gy", "gz")}
    labels = zone_labels[x]
    cap_slab = jnp.zeros(labels.shape, f32)
    for zone in range(capacity.shape[0]):
        cap_slab = cap_slab + jnp.where(labels == zone + 1, capacity[zone], 0.0)
    surface_slab = jnp.where(cap_slab > 0.0, 1.0, 0.0)
    velocity_slab = velocity[x]
    on = jnp.broadcast_to(rates[:, 0:1], (ns, nz))
    off = jnp.broadcast_to(rates[:, 1:2], (ns, nz))
    lane = lax.broadcasted_iota(jnp.int32, (ns, nz), 1)
    x_at = pl.multiple_of(x * nz, nz)
    left, right = lane == 0, lane == nz - 1
    slabs = []
    for y in range(ny):
        at = pl.multiple_of(x * ny * nz, nz) + y * nz
        tile = lambda slabs_on, rows_on: pad[
            :, pl.ds(pl.multiple_of(at + (slabs_on * ny + rows_on) * nz, nz), nz)
        ]
        centre, behind, ahead = tile(1, 0), tile(0, 0), tile(2, 0)
        if y > 0:
            y_low = tile(1, -1)
        elif y_got:
            y_low = jnp.where(first["gy"], centre, beside_of(y_got, True)[:, pl.ds(x_at, nz)])
        else:
            y_low = centre
        if y < ny - 1:
            y_high = tile(1, 1)
        elif y_got:
            y_high = jnp.where(last["gy"], centre, beside_of(y_got, False)[:, pl.ds(x_at, nz)])
        else:
            y_high = centre
        z_low, z_high = pltpu.roll(centre, 1, 1), pltpu.roll(centre, nz - 1, 1)
        cell = x * ny + y
        edge_low = edge_high = centre
        if len(z_got) == 1:
            shift = jnp.where(first["gz"], nz - 1 - cell, lax.rem(nz - cell, nz))
            beside = pltpu.roll(z_got[0][...], shift, 1)
            edge_low = jnp.where(first["gz"], centre, beside)
            edge_high = jnp.where(first["gz"], beside, centre)
        elif len(z_got) == 2:
            beside = pltpu.roll(z_got[0][...], lax.rem(nz - cell, nz), 1)
            edge_low = jnp.where(first["gz"], centre, beside)
            beside = pltpu.roll(z_got[1][...], nz - 1 - cell, 1)
            edge_high = jnp.where(last["gz"], centre, beside)
        z_low = jnp.where(left, edge_low, z_low)
        z_high = jnp.where(right, edge_high, z_high)
        near = behind + ahead + y_low + y_high + z_low + z_high
        row = lambda slab: jnp.broadcast_to(slab[y : y + 1], (ns, nz))
        bound_now = bound_tile(cell, y)
        reaction = row(surface_slab) * (
            on * centre * (row(cap_slab) - bound_now) - off * bound_now
        )
        moved = (
            centre
            + diffusion_number * (near - 6.0 * centre)
            - row(velocity_slab) * (centre - behind)
            - reaction
        )
        store(cell, y, bound_now + reaction)
        slabs.append(moved)
    return jnp.concatenate(slabs, axis=1)


def fill_pad(shape, pad, analyte, x_got, rates):
    ns, nx, ny, nz = shape
    slab = ny * nz
    pad[:, slab : (nx + 1) * slab] = analyte[...]
    at_inlet = lax.axis_index("gx") == 0
    at_outlet = lax.axis_index("gx") == lax.axis_size("gx") - 1
    inlet = jnp.broadcast_to(rates[:, 2:3], (ns, slab))
    outlet = analyte[:, (nx - 1) * slab :]
    if x_got:
        pad[:, :slab] = jnp.where(at_inlet, inlet, beside_of(x_got, True)[...])
        pad[:, (nx + 1) * slab :] = jnp.where(at_outlet, outlet, beside_of(x_got, False)[...])
    else:
        pad[:, :slab] = inlet
        pad[:, (nx + 1) * slab :] = outlet


def first_kernel(shape, analyte, bound, velocity, zone_labels, capacity, rates, *rest):
    ns, nx, ny, nz = shape
    got, rest = unflatten(rest, shape)
    out_a, out_bound = rest[:2]
    faces, (pad,) = unflatten(rest[2:], shape)
    fill_pad(shape, pad, analyte, got[0], rates)
    for ref in faces[2]:
        ref[...] = jnp.zeros(ref.shape, f32)

    def body(x, carry):
        def bound_tile(cell, y):
            return bound[pl.ds(cell, ns, stride=nx * ny), :]

        def store(cell, y, value):
            out_bound[:, pl.ds(pl.multiple_of(cell * nz, nz), nz)] = value

        slab = stencil(
            shape, x, pad, got[1], got[2], bound_tile, store, (velocity, zone_labels, capacity, rates)
        )
        out_a[:, pl.ds(pl.multiple_of(x * ny * nz, ny * nz), ny * nz)] = slab
        emit_faces(faces, slab, x, shape)
        return carry

    lax.fori_loop(0, nx, body, 0)


def second_kernel(shape, nk, analyte, bound, velocity, zone_labels, capacity, rates, both, bb, *rest):
    ns, nx, ny, nz = shape
    got, rest = unflatten(rest, shape)
    out_s, out_bound, out_totals, pad = rest
    fill_pad(shape, pad, analyte, got[0], rates)

    def body(x, carry):
        def bound_tile(cell, y):
            return bound[:, pl.ds(pl.multiple_of(cell * nz, nz), nz)]

        def store(cell, y, value):
            out_bound[pl.ds(cell, ns, stride=nx * ny), :] = value

        slab = stencil(
            shape, x, pad, got[1], got[2], bound_tile, store, (velocity, zone_labels, capacity, rates)
        )
        high, low = split(slab)
        at = pl.ds(pl.multiple_of(x * ny * nz, ny * nz), ny * nz)
        out_s[:ns, at] = high
        out_s[ns:, at] = low
        return carry

    lax.fori_loop(0, nx, body, 0)
    snap = out_s[...]
    product = mm_nt(snap, both[...])
    out_totals[:ns, :] = product[:ns, :nk] + product[:ns, nk:] + product[ns:, :nk]
    square = mm_nt(snap, snap)
    square = square[:ns, :ns] + square[:ns, ns:] + square[ns:, :ns]
    out_totals[ns : 2 * ns, :] = jnp.concatenate(
        [square, jnp.zeros((ns, nk - ns), f32)], axis=1
    )
    out_totals[2 * ns :, :] = bb[...]


def step_call(kernel, shape, operands, got, out_shape, name):
    ns, nx, ny, nz = shape
    smem = {4}
    flat = [g for group in got for g in group]
    in_specs = [
        pl.BlockSpec(memory_space=pltpu.SMEM if i in smem else pltpu.VMEM)
        for i in range(len(operands) + len(flat))
    ]
    return pl.pallas_call(
        kernel,
        in_specs=in_specs,
        out_specs=[pl.BlockSpec(memory_space=pltpu.VMEM) for _ in out_shape],
        out_shape=out_shape,
        scratch_shapes=[pltpu.VMEM((ns, (nx + 2) * ny * nz), f32)],
        name=name,
    )(*operands, *flat)


def finish_kernel(shape, nk, inverse_rows, totals, snap, both, out_modes, out_factor, out_coeffs, left_b, left_s):
    ns, nx, ny, nz = shape

    @pl.when(pl.program_id(0) == 0)
    def _():
        coeffs = totals[:ns, :] * inverse_rows
        out_coeffs[...] = coeffs.T
        weighted = mm_exact(coeffs, totals[2 * ns :, :] * inverse_rows)
        mixed = lax.dot_general(
            coeffs, coeffs, (((1,), (1,)), ((), ())), precision=highest, preferred_element_type=f32
        )
        double = lax.dot_general(
            weighted, coeffs, (((1,), (1,)), ((), ())), precision=highest, preferred_element_type=f32
        )
        gram = totals[ns : 2 * ns, :ns] * inverse_rows - mixed - mixed + double
        sub = lax.broadcasted_iota(jnp.int32, (ns, 2 * ns), 0)
        lane = lax.broadcasted_iota(jnp.int32, (ns, 2 * ns), 1)
        unit = jnp.where(sub[:, :ns] == lane[:, :ns], 1.0, 0.0)
        work = jnp.concatenate([gram, unit], axis=1)
        for j in range(ns):
            row = work[j : j + 1, :]
            scale = work[:, j : j + 1] / row[:, j : j + 1]
            work = work - jnp.where(sub > j, scale * row, 0.0)
        pivots = jnp.sum(jnp.where(lane == sub, work, 0.0), axis=1, keepdims=True)
        work = work / jnp.sqrt(pivots)
        out_factor[...] = jnp.where(lane[:, :ns] >= sub[:, :ns], work[:, :ns], 0.0)
        inverse = work[:, ns:]
        s_high, s_low = split(inverse)
        b_high, b_low = split(-mm_exact(inverse, coeffs))
        left_b[:, :nk] = b_high
        left_b[:, nk : 2 * nk] = b_high
        left_b[:, 2 * nk :] = b_low
        left_s[:, :] = jnp.concatenate([s_high, s_high, s_low], axis=1)

    modes = mm(left_b[:, : 2 * nk], both[...]) + mm(left_b[:, 2 * nk :], both[:nk, :])
    modes = modes + mm(left_s[:, : 2 * ns], snap[...]) + mm(left_s[:, 2 * ns :], snap[:ns, :])
    flat = out_modes.reshape(ns * ny, nz)
    for y in range(ny):
        flat[pl.ds(y, ns, stride=ny), :] = modes[:, y * nz : (y + 1) * nz]


def finish(shape, inverse_rows, totals, snap, both):
    ns, nx, ny, nz = shape
    nk = both.shape[0] // 2
    whole = lambda s: pl.BlockSpec(s, lambda x: (0,) * len(s))
    return pl.pallas_call(
        functools.partial(finish_kernel, shape, nk, inverse_rows),
        grid=(nx,),
        in_specs=[
            whole(totals.shape),
            pl.BlockSpec((2 * ns, ny * nz), lambda x: (0, x)),
            pl.BlockSpec((2 * nk, ny * nz), lambda x: (0, x)),
        ],
        out_specs=[
            pl.BlockSpec((ns, 1, ny, nz), lambda x: (0, x, 0, 0)),
            whole((ns, ns)),
            whole((nk, ns)),
        ],
        out_shape=[
            jax.ShapeDtypeStruct(shape, f32),
            jax.ShapeDtypeStruct((ns, ns), f32),
            jax.ShapeDtypeStruct((nk, ns), f32),
        ],
        scratch_shapes=[pltpu.VMEM((ns, 3 * nk), bf16), pltpu.VMEM((ns, 3 * ns), bf16)],
        name="finish",
    )(totals, snap, both)


def sum_over(value, axes):
    for axis in axes:
        size = lax.axis_size(axis)
        if size & (size - 1):
            value = lax.psum(value, axis)
            continue
        stride = 1
        while stride < size:
            value = value + lax.ppermute(value, axis, [(i, i ^ stride) for i in range(size)])
            stride *= 2
    return value


def on_device(
    basis_modes,
    reduced_state,
    fine_state,
    bound_state,
    velocity,
    zone_labels,
    capacity,
    on_rate,
    off_rate,
    inlet_level,
):
    ns, nx, ny, nz = shape = fine_state.shape
    nk = basis_modes.shape[0]
    cells = nx * ny * nz
    rates = jnp.stack([on_rate, off_rate, inlet_level], axis=1)
    analyte, both, faces = start(reduced_state, basis_modes, fine_state)
    got = exchange(faces)
    bb = basis_products(both, 4)
    fields = [velocity, zone_labels, capacity, rates]
    struct = jax.ShapeDtypeStruct
    outs = step_call(
        functools.partial(first_kernel, shape),
        shape,
        [analyte, bound_state.reshape(ns * nx * ny, nz)] + fields,
        got,
        [struct((ns, cells), f32), struct((ns, cells), f32)]
        + [struct(s, f32) for g in face_shapes(shape) for s in g],
        "first_step",
    )
    faces, _ = unflatten(outs[2:], shape)
    got = exchange(faces)
    snap, bound_next, totals = step_call(
        functools.partial(second_kernel, shape, nk),
        shape,
        [outs[0], outs[1]] + fields + [both, bb],
        got,
        [
            struct((2 * ns, cells), bf16),
            struct((ns * nx * ny, nz), f32),
            struct((2 * ns + nk, nk), f32),
        ],
        "second_step",
    )
    totals = sum_over(totals, ("gz", "gy", "gx"))
    inverse_rows = 1.0 / (
        cells * lax.axis_size("gx") * lax.axis_size("gy") * lax.axis_size("gz")
    )
    modes, factor, coeffs = finish(shape, inverse_rows, totals, snap, both)
    return (modes, factor, coeffs, bound_next.reshape(shape))


def solution(mesh):
    return jax.shard_map(
        on_device,
        mesh=mesh,
        in_specs=(
            P(None, ("grp", "gx"), "gy", "gz"),
            P("grp", None),
            P(None, ("grp", "gx"), "gy", "gz"),
            P(None, ("grp", "gx"), "gy", "gz"),
            P(("grp", "gx"), "gy", "gz"),
            P(("grp", "gx"), "gy", "gz"),
            P(),
            P(),
            P(),
            P("grp"),
        ),
        out_specs=(
            P(None, ("grp", "gx"), "gy", "gz"),
            P("grp", None),
            P("grp", None),
            P(None, ("grp", "gx"), "gy", "gz"),
        ),
        check_vma=False,
    )
```

profile of v0, /device:TPU:0, one launch (start us, length us, event | category | flops | bytes accessed | tf_op | source)
XLA Modules:
  0.0 81.1 jit_solution(13143532977265575935)
XLA Ops:
  0.7 1.5 %copy.19.reduced = f32[128,32]{1,0:T(8,128)} copy(f32[128,32]{0,1:T(8,128)} %param.11) | data formatting | bytes 32768 | tf_op args[1]
  2.1 8.2 %start.1 = (f32[32,8192]{1,0:T(8,128)}, bf16[256,8192]{1,0:T(8,128)(2,1)}, f32[32,1024]{1,0:T(8,128)}, f32[32,1024]{1,0:T(8,128)}, f32[32,1024]{1,0:T(8,128)}, /*index=5*/f32[32,128]{1,0:T(8,128)}) custom-call(f32[128,32]{1,0:T(8,128)} %copy.19.reduced, f32[128,8,8,128]{3,2,1,0:T(8,128)} %basis.1, bf16[32,8,8,128]{3,2,1,0:T(8,128)(2,1)} %fine.1), custom_call_target="tpu_custom_call" | custom-call | tf_op jit(solution)/shard_map/start/pallas_call | solution.py:159
  10.4 5.0 %collective-permute-start = (f32[32,1024]{1,0:T(8,128)}, f32[32,1024]{1,0:T(8,128)S(1)}, u32[]{:S(2)}, u32[]{:S(2)}) collective-permute-start(f32[32,1024]{1,0:T(8,128)} %get-tuple-element.23), channel_id=1, source_target_pairs={{0,4},{4,8},{8,12},{1,5},{5,9},{9,13},{2,6},{6,10},{10,14},{3,7},{... | collective-permute-start | bytes 393224 | tf_op jit(solution)/shard_map/ppermute | solution.py:121
  15.3 1.3 %collective-permute-start.1 = (f32[32,1024]{1,0:T(8,128)}, f32[32,1024]{1,0:T(8,128)S(1)}, u32[]{:S(2)}, u32[]{:S(2)}) collective-permute-start(f32[32,1024]{1,0:T(8,128)} %get-tuple-element.24), channel_id=1, source_target_pairs={{4,0},{8,4},{12,8},{5,1},{9,5},{13,9},{6,2},{10,6},{14,10},{7,3},{... | collective-permute-start | bytes 393224 | tf_op jit(solution)/shard_map/ppermute | solution.py:121
  16.6 1.6 %collective-permute-start.2 = (f32[32,1024]{1,0:T(8,128)}, f32[32,1024]{1,0:T(8,128)S(1)}, u32[]{:S(2)}, u32[]{:S(2)}) collective-permute-start(f32[32,1024]{1,0:T(8,128)} %get-tuple-element.25), channel_id=1, source_target_pairs={{0,2},{2,0},{1,3},{3,1},{4,6},{6,4},{5,7},{7,5},{8,10},{10,8},{9,1... | collective-permute-start | bytes 393224 | tf_op jit(solution)/shard_map/ppermute | solution.py:117
  18.2 0.7 copy.20.rates
  18.9 0.7 collective-permute-done.3.rest_3_
  19.6 2.8 %collective-permute-done.1.rest_1_ = f32[32,1024]{1,0:T(8,128)S(1)} collective-permute-done((f32[32,1024]{1,0:T(8,128)}, f32[32,1024]{1,0:T(8,128)S(1)}, u32[]{:S(2)}, u32[]{:S(2)}) %collective-permute-start.1) | collective-permute-done | bytes 131104 | tf_op jit(solution)/shard_map/ppermute | solution.py:121
  23.1 6.3 %first_step.1 = (f32[32,8192]{1,0:T(8,128)}, f32[32,8192]{1,0:T(8,128)}, f32[32,1024]{1,0:T(8,128)}, f32[32,1024]{1,0:T(8,128)}, f32[32,1024]{1,0:T(8,128)}, /*index=5*/f32[32,128]{1,0:T(8,128)}) custom-call(f32[32,8192]{1,0:T(8,128)} %get-tuple-element.22.analyte, f32[2048,128]{1,0:T(8,128)} %bitcast.5, f32[8,8,128]{2,1,0:T(8,128)} %velocity.3, ...), custom_call_target="tpu_custom_call" | custom-call | tf_op jit(solution)/shard_map/first_step/pallas_call | solution.py:366
  29.4 4.0 %collective-permute-start.4 = (f32[32,1024]{1,0:T(8,128)}, f32[32,1024]{1,0:T(8,128)S(1)}, u32[]{:S(2)}, u32[]{:S(2)}) collective-permute-start(f32[32,1024]{1,0:T(8,128)} %get-tuple-element.30), channel_id=1, source_target_pairs={{0,4},{4,8},{8,12},{1,5},{5,9},{9,13},{2,6},{6,10},{10,14},{3,7},{... | collective-permute-start | bytes 393224 | tf_op jit(solution)/shard_map/ppermute | solution.py:121
  33.4 1.3 %collective-permute-start.5 = (f32[32,1024]{1,0:T(8,128)}, f32[32,1024]{1,0:T(8,128)S(1)}, u32[]{:S(2)}, u32[]{:S(2)}) collective-permute-start(f32[32,1024]{1,0:T(8,128)} %get-tuple-element.31), channel_id=1, source_target_pairs={{4,0},{8,4},{12,8},{5,1},{9,5},{13,9},{6,2},{10,6},{14,10},{7,3},{... | collective-permute-start | bytes 393224 | tf_op jit(solution)/shard_map/ppermute | solution.py:121
  34.7 1.6 %collective-permute-start.6 = (f32[32,1024]{1,0:T(8,128)}, f32[32,1024]{1,0:T(8,128)S(1)}, u32[]{:S(2)}, u32[]{:S(2)}) collective-permute-start(f32[32,1024]{1,0:T(8,128)} %get-tuple-element.32), channel_id=1, source_target_pairs={{0,2},{2,0},{1,3},{3,1},{4,6},{6,4},{5,7},{7,5},{8,10},{10,8},{9,1... | collective-permute-start | bytes 393224 | tf_op jit(solution)/shard_map/ppermute | solution.py:117
  36.2 4.8 %basis_products.1.bb = f32[128,128]{1,0:T(8,128)} custom-call(bf16[256,8192]{1,0:T(8,128)(2,1)} %get-tuple-element.29.both), custom_call_target="tpu_custom_call" | custom-call | tf_op jit(solution)/shard_map/basis_products/pallas_call | solution.py:201
  41.8 7.9 %second_step.1 = (bf16[64,8192]{1,0:T(8,128)(2,1)}, f32[2048,128]{1,0:T(8,128)}, f32[192,128]{1,0:T(8,128)}) custom-call(f32[32,8192]{1,0:T(8,128)} %get-tuple-element.27.analyte, f32[32,8192]{1,0:T(8,128)} %get-tuple-element.28.bound, f32[8,8,128]{2,1,0:T(8,128)} %velocity.3, s32[8,8,128]{2,1,0:T(8,128)} %zone_labels.3, f32[3]{0:T(128)} %capacity.3, ...), custom_call_target="tpu_custom_call" | custom-call | tf_op jit(solution)/shard_map/second_step/pallas_call | solution.py:366
  50.3 1.2 %collective-permute-done.8 = f32[192,128]{1,0:T(8,128)S(1)} collective-permute-done((f32[192,128]{1,0:T(8,128)}, f32[192,128]{1,0:T(8,128)S(1)}, u32[]{:S(2)}, u32[]{:S(2)}) %collective-permute-start.8) | collective-permute-done | bytes 98336 | tf_op jit(solution)/shard_map/ppermute | solution.py:452
  51.4 0.9 %add.12 = f32[192,128]{1,0:T(8,128)S(1)} add(f32[192,128]{1,0:T(8,128)} %get-tuple-element.34, f32[192,128]{1,0:T(8,128)S(1)} %collective-permute-done.8) | non-fusion elementwise | flops 24576 | bytes 294912 | tf_op jit(solution)/shard_map/add | solution.py:452
  52.3 0.8 collective-permute-start.9
  53.1 4.4 %collective-permute-done.9 = f32[192,128]{1,0:T(8,128)S(1)} collective-permute-done((f32[192,128]{1,0:T(8,128)S(1)}, f32[192,128]{1,0:T(8,128)S(1)}, u32[]{:S(2)}, u32[]{:S(2)}) %collective-permute-start.9) | collective-permute-done | bytes 98336 | tf_op jit(solution)/shard_map/ppermute | solution.py:452
  57.5 2.7 %collective-permute-start.10 = (f32[192,128]{1,0:T(8,128)S(1)}, f32[192,128]{1,0:T(8,128)S(1)}, u32[]{:S(2)}, u32[]{:S(2)}) collective-permute-start(f32[192,128]{1,0:T(8,128)S(1)} %add.13), channel_id=1, source_target_pairs={{0,4},{4,0},{8,12},{12,8},{1,5},{5,1},{9,13},{13,9},{2,6},{6,2},{1... | collective-permute-start | bytes 294920 | tf_op jit(solution)/shard_map/ppermute | solution.py:452
  60.2 2.6 %collective-permute-done.10 = f32[192,128]{1,0:T(8,128)S(1)} collective-permute-done((f32[192,128]{1,0:T(8,128)S(1)}, f32[192,128]{1,0:T(8,128)S(1)}, u32[]{:S(2)}, u32[]{:S(2)}) %collective-permute-start.10) | collective-permute-done | bytes 98336 | tf_op jit(solution)/shard_map/ppermute | solution.py:452
  62.8 3.1 %collective-permute-start.11 = (f32[192,128]{1,0:T(8,128)S(1)}, f32[192,128]{1,0:T(8,128)S(1)}, u32[]{:S(2)}, u32[]{:S(2)}) collective-permute-start(f32[192,128]{1,0:T(8,128)S(1)} %add.14), channel_id=1, source_target_pairs={{0,8},{4,12},{8,0},{12,4},{1,9},{5,13},{9,1},{13,5},{2,10},{6,14},... | collective-permute-start | bytes 294920 | tf_op jit(solution)/shard_map/ppermute | solution.py:452
  65.9 2.6 %collective-permute-done.11 = f32[192,128]{1,0:T(8,128)S(1)} collective-permute-done((f32[192,128]{1,0:T(8,128)S(1)}, f32[192,128]{1,0:T(8,128)S(1)}, u32[]{:S(2)}, u32[]{:S(2)}) %collective-permute-start.11) | collective-permute-done | bytes 98336 | tf_op jit(solution)/shard_map/ppermute | solution.py:452
  69.1 10.4 %finish.1 = (f32[32,8,8,128]{3,2,1,0:T(8,128)}, f32[32,32]{1,0:T(8,128)}, f32[128,32]{1,0:T(8,128)}) custom-call(f32[192,128]{1,0:T(8,128)} %add.15.totals, bf16[64,8192]{1,0:T(8,128)(2,1)} %get-tuple-element.35.snap, bf16[256,8192]{1,0:T(8,128)(2,1)} %get-tuple-element.29.both), custom_call_target="tpu_custom_call" | custom-call | tf_op jit(solution)/shard_map/finish/pallas_call | solution.py:421
  79.6 1.5 %copy.22 = f32[128,32]{0,1:T(8,128)} copy(f32[128,32]{1,0:T(8,128)} %get-tuple-element.46) | data formatting | bytes 32768
  (35 shorter events, 2.6 us)
Async XLA Ops:
  0.6 17.6 %copy-start.8 = (f32[32]{0:T(128)S(1)}, f32[32]{0:T(128)}, u32[]{:S(2)}) copy-start(f32[32]{0:T(128)} %param.19) | copy-start | bytes 388
  0.6 17.6 %copy-start.9 = (f32[32]{0:T(128)S(1)}, f32[32]{0:T(128)}, u32[]{:S(2)}) copy-start(f32[32]{0:T(128)} %param.18) | copy-start | bytes 388
  0.7 17.5 %copy-start.10 = (f32[32]{0:T(128)S(1)}, f32[32]{0:T(128)}, u32[]{:S(2)}) copy-start(f32[32]{0:T(128)} %param.17) | copy-start | bytes 388
  10.4 9.2 %collective-permute-start = (f32[32,1024]{1,0:T(8,128)}, f32[32,1024]{1,0:T(8,128)S(1)}, u32[]{:S(2)}, u32[]{:S(2)}) collective-permute-start(f32[32,1024]{1,0:T(8,128)} %get-tuple-element.23), channel_id=1, source_target_pairs={{0,4},{4,8},{8,12},{1,5},{5,9},{9,13},{2,6},{6,10},{10,14},{3,7},{... | collective-permute-start | bytes 393224 | tf_op jit(solution)/shard_map/ppermute | solution.py:121
  15.3 7.1 %collective-permute-start.1 = (f32[32,1024]{1,0:T(8,128)}, f32[32,1024]{1,0:T(8,128)S(1)}, u32[]{:S(2)}, u32[]{:S(2)}) collective-permute-start(f32[32,1024]{1,0:T(8,128)} %get-tuple-element.24), channel_id=1, source_target_pairs={{4,0},{8,4},{12,8},{5,1},{9,5},{13,9},{6,2},{10,6},{14,10},{7,3},{... | collective-permute-start | bytes 393224 | tf_op jit(solution)/shard_map/ppermute | solution.py:121
  16.6 5.8 %collective-permute-start.2 = (f32[32,1024]{1,0:T(8,128)}, f32[32,1024]{1,0:T(8,128)S(1)}, u32[]{:S(2)}, u32[]{:S(2)}) collective-permute-start(f32[32,1024]{1,0:T(8,128)} %get-tuple-element.25), channel_id=1, source_target_pairs={{0,2},{2,0},{1,3},{3,1},{4,6},{6,4},{5,7},{7,5},{8,10},{10,8},{9,1... | collective-permute-start | bytes 393224 | tf_op jit(solution)/shard_map/ppermute | solution.py:117
  18.2 1.4 %collective-permute-start.3 = (f32[32,128]{1,0:T(8,128)}, f32[32,128]{1,0:T(8,128)S(1)}, u32[]{:S(2)}, u32[]{:S(2)}) collective-permute-start(f32[32,128]{1,0:T(8,128)} %get-tuple-element.26), channel_id=1, source_target_pairs={{0,1},{1,0},{2,3},{3,2},{4,5},{5,4},{6,7},{7,6},{8,9},{9,8},{10,11... | collective-permute-start | bytes 49160 | tf_op jit(solution)/shard_map/ppermute | solution.py:117
  19.6 2.8 %copy-start.6 = (f32[32,128]{1,0:T(8,128)}, f32[32,128]{1,0:T(8,128)S(1)}, u32[]{:S(2)}) copy-start(f32[32,128]{1,0:T(8,128)S(1)} %collective-permute-done.3.rest_3_) | copy-start | bytes 49156
  19.6 2.8 %copy-start = (f32[32,1024]{1,0:T(8,128)}, f32[32,1024]{1,0:T(8,128)S(1)}, u32[]{:S(2)}) copy-start(f32[32,1024]{1,0:T(8,128)S(1)} %collective-permute-done.rest_0_) | copy-start | bytes 393220
  22.4 0.7 copy-start.2
  22.4 0.7 copy-start.4
  29.4 11.7 %collective-permute-start.4 = (f32[32,1024]{1,0:T(8,128)}, f32[32,1024]{1,0:T(8,128)S(1)}, u32[]{:S(2)}, u32[]{:S(2)}) collective-permute-start(f32[32,1024]{1,0:T(8,128)} %get-tuple-element.30), channel_id=1, source_target_pairs={{0,4},{4,8},{8,12},{1,5},{5,9},{9,13},{2,6},{6,10},{10,14},{3,7},{... | collective-permute-start | bytes 393224 | tf_op jit(solution)/shard_map/ppermute | solution.py:121
  33.4 7.7 %collective-permute-start.5 = (f32[32,1024]{1,0:T(8,128)}, f32[32,1024]{1,0:T(8,128)S(1)}, u32[]{:S(2)}, u32[]{:S(2)}) collective-permute-start(f32[32,1024]{1,0:T(8,128)} %get-tuple-element.31), channel_id=1, source_target_pairs={{4,0},{8,4},{12,8},{5,1},{9,5},{13,9},{6,2},{10,6},{14,10},{7,3},{... | collective-permute-start | bytes 393224 | tf_op jit(solution)/shard_map/ppermute | solution.py:121
  34.7 6.4 %collective-permute-start.6 = (f32[32,1024]{1,0:T(8,128)}, f32[32,1024]{1,0:T(8,128)S(1)}, u32[]{:S(2)}, u32[]{:S(2)}) collective-permute-start(f32[32,1024]{1,0:T(8,128)} %get-tuple-element.32), channel_id=1, source_target_pairs={{0,2},{2,0},{1,3},{3,1},{4,6},{6,4},{5,7},{7,5},{8,10},{10,8},{9,1... | collective-permute-start | bytes 393224 | tf_op jit(solution)/shard_map/ppermute | solution.py:117
  36.2 4.8 %collective-permute-start.7 = (f32[32,128]{1,0:T(8,128)}, f32[32,128]{1,0:T(8,128)S(1)}, u32[]{:S(2)}, u32[]{:S(2)}) collective-permute-start(f32[32,128]{1,0:T(8,128)} %get-tuple-element.33), channel_id=1, source_target_pairs={{0,1},{1,0},{2,3},{3,2},{4,5},{5,4},{6,7},{7,6},{8,9},{9,8},{10,11... | collective-permute-start | bytes 49160 | tf_op jit(solution)/shard_map/ppermute | solution.py:117
  41.0 0.6 copy-start.7
  41.1 0.7 copy-start.1
  41.1 0.7 copy-start.3
  41.1 0.7 copy-start.5
  49.7 1.7 %collective-permute-start.8 = (f32[192,128]{1,0:T(8,128)}, f32[192,128]{1,0:T(8,128)S(1)}, u32[]{:S(2)}, u32[]{:S(2)}) collective-permute-start(f32[192,128]{1,0:T(8,128)} %get-tuple-element.34), channel_id=1, source_target_pairs={{0,1},{1,0},{2,3},{3,2},{4,5},{5,4},{6,7},{7,6},{8,9},{9,8},{10,11... | collective-permute-start | bytes 294920 | tf_op jit(solution)/shard_map/ppermute | solution.py:452
  52.3 5.1 %collective-permute-start.9 = (f32[192,128]{1,0:T(8,128)S(1)}, f32[192,128]{1,0:T(8,128)S(1)}, u32[]{:S(2)}, u32[]{:S(2)}) collective-permute-start(f32[192,128]{1,0:T(8,128)S(1)} %add.12), channel_id=1, source_target_pairs={{0,2},{2,0},{1,3},{3,1},{4,6},{6,4},{5,7},{7,5},{8,10},{10,8},{9,1... | collective-permute-start | bytes 294920 | tf_op jit(solution)/shard_map/ppermute | solution.py:452
  57.5 5.3 %collective-permute-start.10 = (f32[192,128]{1,0:T(8,128)S(1)}, f32[192,128]{1,0:T(8,128)S(1)}, u32[]{:S(2)}, u32[]{:S(2)}) collective-permute-start(f32[192,128]{1,0:T(8,128)S(1)} %add.13), channel_id=1, source_target_pairs={{0,4},{4,0},{8,12},{12,8},{1,5},{5,1},{9,13},{13,9},{2,6},{6,2},{1... | collective-permute-start | bytes 294920 | tf_op jit(solution)/shard_map/ppermute | solution.py:452
  62.8 5.7 %collective-permute-start.11 = (f32[192,128]{1,0:T(8,128)S(1)}, f32[192,128]{1,0:T(8,128)S(1)}, u32[]{:S(2)}, u32[]{:S(2)}) collective-permute-start(f32[192,128]{1,0:T(8,128)S(1)} %add.14), channel_id=1, source_target_pairs={{0,8},{4,12},{8,0},{12,4},{1,9},{5,13},{9,1},{13,5},{2,10},{6,14},... | collective-permute-start | bytes 294920 | tf_op jit(solution)/shard_map/ppermute | solution.py:452
where the time goes:
time: 81.8 us; the launch traced here: 81.1 us
  Pallas kernels  37.7 us (46%)
  starting transfers between devices  21.7 us (27%)
  waiting for transfers between devices  14.2 us (17%)
  local copies, waits for them, and re-layouts  5.07 us (6%)
  other arithmetic  1.6 us (2%)
    pallas_call x2, Pallas kernels, step_call(): pl.pallas_call(kernel, in_specs=in_specs, out_specs=[pl.BlockSpec(memory_...  14.2 us
    ppermute x4, waiting for transfers between devices, sum_over(): lax.ppermute(value, axis, [(i, i ^ stride) for i in range(size)])  10.7 us
    pallas_call x1, Pallas kernels, finish(): pl.pallas_call(functools.partial(finish_kernel, shape, nk, inverse_rows),...  10.4 us
    ppermute x2, starting transfers between devices, exchange(): lax.ppermute(sent[1], axis, up)  8.93 us
    pallas_call x1, Pallas kernels, start(): pl.pallas_call(functools.partial(start_kernel, shape, nk), grid=(nx,), in...  8.24 us
    ppermute x4, starting transfers between devices, sum_over(): lax.ppermute(value, axis, [(i, i ^ stride) for i in range(size)])  7.06 us
    pallas_call x1, Pallas kernels, basis_products(): pl.pallas_call(functools.partial(bb_kernel, nk), grid=(steps,), in_specs=...  4.81 us
    unnamed x24, local copies, waits for them, and re-layouts  4.38 us
  transfers between devices with their start and end apart: 12, of which 6 were waited for; matrix products, arithmetic and copies ran while one was open for 1% of the time, Pallas kernels for 6%

commit v1 on v0

v1 whole, which is shorter than its diff:
```python
import functools

import jax
import jax.numpy as jnp
from jax import lax
from jax.experimental import pallas as pl
from jax.experimental.pallas import tpu as pltpu
from jax.sharding import PartitionSpec as P

highest = lax.Precision.HIGHEST
diffusion_number = 0.03
f32 = jnp.float32
bf16 = jnp.bfloat16
vmem_limit = 16 << 20


def split(value):
    high = value.astype(bf16)
    return high, (value - high.astype(f32)).astype(bf16)


def mm(a, b):
    return jnp.dot(a, b, preferred_element_type=f32)


def mm_nt(a, b):
    return lax.dot_general(a, b, (((1,), (1,)), ((), ())), preferred_element_type=f32)


def mm_exact(a, b):
    return jnp.dot(a, b, precision=highest, preferred_element_type=f32)


def face_count(axis):
    size = lax.axis_size(axis)
    return 0 if size == 1 else 1 if size == 2 else 2


def pack_column(packed, axis, tile, cell):
    lanes = tile.shape[1]
    here = lax.broadcasted_iota(jnp.int32, tile.shape, 1) == cell
    after = lax.rem(cell + 1, lanes)
    if len(packed) == 1:
        shifts = [jnp.where(lax.axis_index(axis) == 0, after, cell)]
    else:
        shifts = [cell, after]
    return [jnp.where(here, pltpu.roll(tile, s, 1), p) for p, s in zip(packed, shifts)]


def copy_faces(faces, field, shape):
    _, nx, ny, nz = shape
    slab = ny * nz
    for refs, axis, width, count, last in (
        (faces[0], "gx", slab, 1, (nx - 1) * slab),
        (faces[1], "gy", nz, nx, slab - nz),
    ):
        for i, ref in enumerate(refs):
            if len(refs) == 1:
                at = pl.multiple_of(jnp.where(lax.axis_index(axis) == 0, last, 0), nz)
            else:
                at = last * i
            for j in range(count):
                ref[:, j * width : (j + 1) * width] = field[:, pl.ds(at + j * slab, width)]


def face_shapes(shape):
    ns, nx, ny, nz = shape
    return (
        [(ns, ny * nz)] * face_count("gx"),
        [(ns, nx * nz)] * face_count("gy"),
        [(ns, nz)] * face_count("gz"),
    )


def unflatten(flat, shape):
    out = []
    for axis in ("gx", "gy", "gz"):
        n = face_count(axis)
        out.append(list(flat[:n]))
        flat = flat[n:]
    return out, flat


def exchange(faces):
    got = []
    for axis, sent in zip(("gx", "gy", "gz"), faces, strict=True):
        size = lax.axis_size(axis)
        if len(sent) == 1:
            got.append([lax.ppermute(sent[0], axis, [(0, 1), (1, 0)])])
        elif len(sent) == 2:
            up = [(i, i + 1) for i in range(size - 1)]
            down = [(j, i) for i, j in up]
            got.append([lax.ppermute(sent[1], axis, up), lax.ppermute(sent[0], axis, down)])
        else:
            got.append([])
    return got


def start_kernel(shape, nk, reduced, basis, fine, out_a, out_b, out_bb, *rest):
    ns, nx, ny, nz = shape
    faces, scratch = unflatten(rest, shape)
    r_buf, b_buf, f_buf, rows, both, r_sem, b_sem, f_sem, o_sem = scratch
    slab_at = lambda x: pl.ds(pl.multiple_of(x * ny * nz, ny * nz), ny * nz)
    o_copy = lambda x: pltpu.make_async_copy(both.at[:, slab_at(x)], out_b.at[:, slab_at(x)], o_sem.at[x])
    r_copy = pltpu.make_async_copy(reduced, r_buf, r_sem)
    f_copy = pltpu.make_async_copy(fine, f_buf, f_sem)
    b_copy = lambda x: pltpu.make_async_copy(basis.at[:, x], b_buf.at[x], b_sem.at[x])
    r_copy.start()
    b_copy(0).start()
    f_copy.start()
    for x in range(1, nx):
        b_copy(x).start()
    r_copy.wait()
    r_high, r_low = split(r_buf[...])
    r_twice = jnp.concatenate([r_high, r_high], axis=1)
    group = max(1, min(ny, 256 // nz))

    def body(x, packed):
        b_copy(x).wait()

        @pl.when(x == 0)
        def _():
            f_copy.wait()

        flat = b_buf.at[x].reshape(nk * ny, nz)
        rows[...] = f_buf[:, pl.ds(x, 1)].reshape(ns * ny, nz).astype(f32)
        for y in range(0, ny, group):
            at = pl.multiple_of(x * ny * nz, ny * nz) + y * nz
            parts = [split(flat[pl.ds(y + i, nk, stride=ny), :]) for i in range(group)]
            high = jnp.concatenate([p[0] for p in parts], axis=1)
            low = jnp.concatenate([p[1] for p in parts], axis=1)
            both[:nk, pl.ds(at, group * nz)] = high
            both[nk:, pl.ds(at, group * nz)] = low
            slab = mm(r_twice, jnp.concatenate([high, low], axis=0)) + mm(r_low, high)
            for i in range(group):
                tile = slab[:, i * nz : (i + 1) * nz] + rows[pl.ds(y + i, ns, stride=ny), :]
                out_a[:, pl.ds(at + i * nz, nz)] = tile
                packed = pack_column(packed, "gz", tile, x * ny + y + i)
        o_copy(x).start()
        return packed

    packed = lax.fori_loop(0, nx, body, [jnp.zeros((ns, nz), f32) for _ in faces[2]])
    for ref, value in zip(faces[2], packed):
        ref[...] = value
    copy_faces(faces, out_a, shape)
    product = mm_nt(both[:nk, :], both[...])
    mixed = product[:, nk:]
    out_bb[...] = product[:, :nk] + mixed + mixed.T
    for x in range(nx):
        o_copy(x).wait()


def start(reduced, basis, fine):
    nk = basis.shape[0]
    ns, nx, ny, nz = shape = fine.shape
    groups = [s for g in face_shapes(shape) for s in g]
    outs = pl.pallas_call(
        functools.partial(start_kernel, shape, nk),
        in_specs=[pl.BlockSpec(memory_space=pltpu.HBM)] * 3,
        out_specs=[
            pl.BlockSpec(memory_space=pltpu.HBM if i == 1 else pltpu.VMEM)
            for i in range(3 + len(groups))
        ],
        out_shape=[
            jax.ShapeDtypeStruct((ns, nx * ny * nz), f32),
            pltpu.HBM((2 * nk, nx * ny * nz), bf16),
            jax.ShapeDtypeStruct((nk, nk), f32),
        ]
        + [jax.ShapeDtypeStruct(s, f32) for s in groups],
        scratch_shapes=[
            pltpu.VMEM((ns, nk), f32),
            pltpu.VMEM((nx, nk, ny, nz), f32),
            pltpu.VMEM((ns, nx, ny, nz), bf16),
            pltpu.VMEM((ns * ny, nz), f32),
            pltpu.VMEM((2 * nk, nx * ny * nz), bf16),
            pltpu.SemaphoreType.DMA,
            pltpu.SemaphoreType.DMA((nx,)),
            pltpu.SemaphoreType.DMA,
            pltpu.SemaphoreType.DMA((nx,)),
        ],
        compiler_params=pltpu.CompilerParams(vmem_limit_bytes=vmem_limit),
        name="start",
    )(*[pltpu.with_memory_space_constraint(a, pltpu.HBM) for a in (reduced, basis, fine)])
    faces, _ = unflatten(outs[3:], shape)
    return outs[:3], faces


def beside_of(got, at_start):
    return got[0] if len(got) == 1 else got[0 if at_start else 1]


def stencil(shape, x, pad, y_got, z_got, bound_tile, store, args):
    velocity, zone_labels, capacity, rates = args
    ns, nx, ny, nz = shape
    first = {a: lax.axis_index(a) == 0 for a in ("gy", "gz")}
    last = {a: lax.axis_index(a) == lax.axis_size(a) - 1 for a in ("gy", "gz")}
    labels = zone_labels[x]
    cap_slab = jnp.zeros(labels.shape, f32)
    for zone in range(capacity.shape[0]):
        cap_slab = cap_slab + jnp.where(labels == zone + 1, capacity[zone], 0.0)
    surface_slab = jnp.where(cap_slab > 0.0, 1.0, 0.0)
    velocity_slab = velocity[x]
    on = jnp.broadcast_to(rates[:, 0:1], (ns, nz))
    off = jnp.broadcast_to(rates[:, 1:2], (ns, nz))
    lane = lax.broadcasted_iota(jnp.int32, (ns, nz), 1)
    x_at = pl.multiple_of(x * nz, nz)
    left, right = lane == 0, lane == nz - 1
    inner = lane == jnp.where(first["gz"], nz - 1, 0)
    inner_low = lane == jnp.where(first["gz"], -1, 0)
    inner_high = lane == jnp.where(last["gz"], -1, nz - 1)
    for y in range(ny):
        at = pl.multiple_of(x * ny * nz, nz) + y * nz
        tile = lambda slabs_on, rows_on: pad[
            :, pl.ds(pl.multiple_of(at + (slabs_on * ny + rows_on) * nz, nz), nz)
        ]
        centre, behind, ahead = tile(1, 0), tile(0, 0), tile(2, 0)
        if y > 0:
            y_low = tile(1, -1)
        elif y_got:
            y_low = jnp.where(first["gy"], centre, beside_of(y_got, True)[:, pl.ds(x_at, nz)])
        else:
            y_low = centre
        if y < ny - 1:
            y_high = tile(1, 1)
        elif y_got:
            y_high = jnp.where(last["gy"], centre, beside_of(y_got, False)[:, pl.ds(x_at, nz)])
        else:
            y_high = centre
        z_low, z_high = pltpu.roll(centre, 1, 1), pltpu.roll(centre, nz - 1, 1)
        cell = x * ny + y
        edge = centre
        if len(z_got) == 1:
            shift = jnp.where(first["gz"], nz - 1 - cell, lax.rem(nz - cell, nz))
            edge = jnp.where(inner, pltpu.roll(z_got[0][...], shift, 1), edge)
        elif len(z_got) == 2:
            beside = pltpu.roll(z_got[0][...], lax.rem(nz - cell, nz), 1)
            edge = jnp.where(inner_low, beside, edge)
            beside = pltpu.roll(z_got[1][...], nz - 1 - cell, 1)
            edge = jnp.where(inner_high, beside, edge)
        z_low = jnp.where(left, edge, z_low)
        z_high = jnp.where(right, edge, z_high)
        near = behind + ahead + y_low + y_high + z_low + z_high
        row = lambda slab: jnp.broadcast_to(slab[y : y + 1], (ns, nz))
        bound_now = bound_tile(cell, at)
        reaction = row(surface_slab) * (
            on * centre * (row(cap_slab) - bound_now) - off * bound_now
        )
        moved = (
            centre
            + diffusion_number * (near - 6.0 * centre)
            - row(velocity_slab) * (centre - behind)
            - reaction
        )
        store(cell, at, moved, bound_now + reaction)


def fill_pad(shape, pad, analyte, x_got, rates):
    ns, nx, ny, nz = shape
    slab = ny * nz
    pad[:, slab : (nx + 1) * slab] = analyte[...]
    at_inlet = lax.axis_index("gx") == 0
    at_outlet = lax.axis_index("gx") == lax.axis_size("gx") - 1
    inlet = jnp.broadcast_to(rates[:, 2:3], (ns, slab))
    outlet = analyte[:, (nx - 1) * slab :]
    if x_got:
        pad[:, :slab] = jnp.where(at_inlet, inlet, beside_of(x_got, True)[...])
        pad[:, (nx + 1) * slab :] = jnp.where(at_outlet, outlet, beside_of(x_got, False)[...])
    else:
        pad[:, :slab] = inlet
        pad[:, (nx + 1) * slab :] = outlet


def first_kernel(shape, analyte, bound, velocity, zone_labels, capacity, rates, *rest):
    ns, nx, ny, nz = shape
    got, rest = unflatten(rest, shape)
    out_a, out_bound = rest[:2]
    faces, (pad,) = unflatten(rest[2:], shape)
    fill_pad(shape, pad, analyte, got[0], rates)

    def body(x, packed):
        packs = [packed]

        def bound_tile(cell, at):
            return bound[pl.ds(cell, ns, stride=nx * ny), :]

        def store(cell, at, moved, bound_then):
            out_bound[:, pl.ds(at, nz)] = bound_then
            out_a[:, pl.ds(at, nz)] = moved
            packs[0] = pack_column(packs[0], "gz", moved, cell)

        stencil(
            shape, x, pad, got[1], got[2], bound_tile, store, (velocity, zone_labels, capacity, rates)
        )
        return packs[0]

    packed = lax.fori_loop(0, nx, body, [jnp.zeros((ns, nz), f32) for _ in faces[2]])
    for ref, value in zip(faces[2], packed):
        ref[...] = value
    copy_faces(faces, out_a, shape)


def second_kernel(shape, nk, analyte, bound, velocity, zone_labels, capacity, rates, both, bb, *rest):
    ns, nx, ny, nz = shape
    got, rest = unflatten(rest, shape)
    out_s, out_bound, out_totals, pad, bound_buf, both_buf, sem, both_sem = rest
    both_copy = pltpu.make_async_copy(both, both_buf, both_sem)
    both_copy.start()
    fill_pad(shape, pad, analyte, got[0], rates)

    def body(x, carry):
        def bound_tile(cell, at):
            return bound[:, pl.ds(at, nz)]

        def store(cell, at, moved, bound_then):
            bound_buf[pl.ds(cell, ns, stride=nx * ny), :] = bound_then
            high, low = split(moved)
            out_s[:ns, pl.ds(at, nz)] = high
            out_s[ns:, pl.ds(at, nz)] = low

        stencil(
            shape, x, pad, got[1], got[2], bound_tile, store, (velocity, zone_labels, capacity, rates)
        )
        return carry

    lax.fori_loop(0, nx, body, 0)
    copy = pltpu.make_async_copy(bound_buf, out_bound, sem)
    copy.start()
    snap = out_s[...]
    both_copy.wait()
    product = mm_nt(snap, both_buf[...])
    out_totals[:ns, :] = product[:ns, :nk] + product[:ns, nk:] + product[ns:, :nk]
    square = mm_nt(snap, snap)
    square = square[:ns, :ns] + square[:ns, ns:] + square[ns:, :ns]
    out_totals[ns : 2 * ns, :] = jnp.concatenate(
        [square, jnp.zeros((ns, nk - ns), f32)], axis=1
    )
    out_totals[2 * ns :, :] = bb[...]
    copy.wait()


def step_call(kernel, shape, operands, got, out_shape, name, hbm=(), scratch=()):
    ns, nx, ny, nz = shape
    space = {4: pltpu.SMEM, 6: pltpu.HBM if scratch else pltpu.VMEM}
    flat = [g for group in got for g in group]
    in_specs = [
        pl.BlockSpec(memory_space=space.get(i, pltpu.VMEM))
        for i in range(len(operands) + len(flat))
    ]
    return pl.pallas_call(
        kernel,
        in_specs=in_specs,
        out_specs=[
            pl.BlockSpec(memory_space=pltpu.HBM if i in hbm else pltpu.VMEM)
            for i in range(len(out_shape))
        ],
        out_shape=out_shape,
        scratch_shapes=[pltpu.VMEM((ns, (nx + 2) * ny * nz), f32), *scratch],
        compiler_params=pltpu.CompilerParams(vmem_limit_bytes=vmem_limit),
        name=name,
    )(*operands, *flat)


def eliminate(gram, width, between):
    n = gram.shape[0]
    sub = lax.broadcasted_iota(jnp.int32, (n, 2 * n), 0)
    lane = lax.broadcasted_iota(jnp.int32, (n, 2 * n), 1)
    unit = jnp.where(sub[:, :n] == lane[:, :n], 1.0, 0.0)
    work = jnp.concatenate([gram, unit], axis=1)
    for start_at in range(0, n, width):
        columns = [
            jnp.broadcast_to(work[:, start_at + i : start_at + i + 1], (n, 2 * n))
            for i in range(width)
        ]
        for i in range(width):
            j = start_at + i
            scale = jnp.where(sub > j, columns[i] / columns[i][j : j + 1, :], 0.0)
            for k in range(i + 1, width):
                columns[k] = columns[k] - scale * columns[k][j : j + 1, :]
            work = work - scale * work[j : j + 1, :]
            between(j)
    pivots = jnp.sum(jnp.where(lane == sub, work, 0.0), axis=1, keepdims=True)
    work = work / jnp.sqrt(pivots)
    return jnp.where(lane[:, :n] >= sub[:, :n], work[:, :n], 0.0), work[:, n:]


def finish_kernel(shape, nk, inverse_rows, totals, snap, both, out_modes, out_factor, out_coeffs, *scratch):
    ns, nx, ny, nz = shape
    slab = ny * nz
    rest, modes, both_buf, sem, both_sem = scratch
    part = lambda x: slice(x * slab, (x + 1) * slab)
    both_copy = lambda x: pltpu.make_async_copy(both.at[:, part(x)], both_buf.at[:, part(x)], both_sem.at[x])
    for x in range(nx):
        both_copy(x).start()
    coeffs = totals[:ns, :] * inverse_rows
    out_coeffs[...] = coeffs
    c_high, c_low = split(coeffs)
    c_twice = jnp.concatenate([c_high, c_high], axis=1)
    weighted = mm_exact(coeffs, totals[2 * ns :, :] * inverse_rows)
    exact_nt = functools.partial(
        lax.dot_general,
        dimension_numbers=(((1,), (1,)), ((), ())),
        precision=highest,
        preferred_element_type=f32,
    )
    mixed = exact_nt(coeffs, coeffs)
    gram = totals[ns : 2 * ns, :ns] * inverse_rows - mixed - mixed + exact_nt(weighted, coeffs)

    pieces = 2 * nx if ny % 2 == 0 and 2 * nx <= ns else nx
    width = nx * slab // pieces

    def residual(j):
        if j >= pieces:
            return
        if j % (pieces // nx) == 0:
            both_copy(j // (pieces // nx)).wait()
        at = slice(j * width, (j + 1) * width)
        value = snap[:ns, at].astype(f32) + snap[ns:, at].astype(f32)
        value = value - (mm(c_twice, both_buf[:, at]) + mm(c_low, both_buf[:nk, at]))
        high, low = split(value)
        rest[:ns, at] = high
        rest[ns:, at] = low

    factor, inverse = eliminate(gram, 8 if ns % 8 == 0 else 1, residual)
    out_factor[...] = factor
    i_high, i_low = split(inverse)
    i_twice = jnp.concatenate([i_high, i_high], axis=1)
    copy = lambda x: pltpu.make_async_copy(modes.at[:, x], out_modes.at[:, x], sem.at[x])
    flat = modes.reshape(ns * nx * ny, nz)
    for x in range(nx):
        at = slice(x * slab, (x + 1) * slab)
        value = mm(i_twice, rest[:, at]) + mm(i_low, rest[:ns, at])
        for y in range(ny):
            flat[pl.ds(x * ny + y, ns, stride=nx * ny), :] = value[:, y * nz : (y + 1) * nz]
        copy(x).start()
    for x in range(nx):
        copy(x).wait()


def finish(shape, inverse_rows, totals, snap, both):
    ns, nx, ny, nz = shape
    nk = both.shape[0] // 2
    vmem = pl.BlockSpec(memory_space=pltpu.VMEM)
    return pl.pallas_call(
        functools.partial(finish_kernel, shape, nk, inverse_rows),
        in_specs=[vmem, vmem, pl.BlockSpec(memory_space=pltpu.HBM)],
        out_specs=[pl.BlockSpec(memory_space=pltpu.HBM), vmem, vmem],
        out_shape=[
            jax.ShapeDtypeStruct(shape, f32),
            jax.ShapeDtypeStruct((ns, ns), f32),
            jax.ShapeDtypeStruct((ns, nk), f32),
        ],
        scratch_shapes=[
            pltpu.VMEM((2 * ns, nx * ny * nz), bf16),
            pltpu.VMEM(shape, f32),
            pltpu.VMEM(both.shape, bf16),
            pltpu.SemaphoreType.DMA((nx,)),
            pltpu.SemaphoreType.DMA((nx,)),
        ],
        compiler_params=pltpu.CompilerParams(vmem_limit_bytes=vmem_limit),
        name="finish",
    )(totals, snap, both)


def sum_over(value, axes):
    for axis in axes:
        size = lax.axis_size(axis)
        if size & (size - 1):
            value = lax.psum(value, axis)
            continue
        stride = 1
        while stride < size:
            value = value + lax.ppermute(value, axis, [(i, i ^ stride) for i in range(size)])
            stride *= 2
    return value


def on_device(
    basis_modes,
    reduced_state,
    fine_state,
    bound_state,
    velocity,
    zone_labels,
    capacity,
    on_rate,
    off_rate,
    inlet_level,
):
    ns, nx, ny, nz = shape = fine_state.shape
    nk = basis_modes.shape[0]
    cells = nx * ny * nz
    rates = jnp.stack([on_rate, off_rate, inlet_level], axis=1)
    (analyte, both, bb), faces = start(reduced_state.T, basis_modes, fine_state)
    got = exchange(faces)
    both = pltpu.with_memory_space_constraint(both, pltpu.HBM)
    fields = [velocity, zone_labels, capacity, rates]
    struct = jax.ShapeDtypeStruct
    outs = step_call(
        functools.partial(first_kernel, shape),
        shape,
        [analyte, bound_state.reshape(ns * nx * ny, nz)] + fields,
        got,
        [struct((ns, cells), f32), struct((ns, cells), f32)]
        + [struct(s, f32) for g in face_shapes(shape) for s in g],
        "first_step",
    )
    faces, _ = unflatten(outs[2:], shape)
    got = exchange(faces)
    snap, bound_next, totals = step_call(
        functools.partial(second_kernel, shape, nk),
        shape,
        [outs[0], outs[1]] + fields + [both, bb],
        got,
        [
            struct((2 * ns, cells), bf16),
            struct((ns * nx * ny, nz), f32),
            struct((2 * ns + nk, nk), f32),
        ],
        "second_step",
        hbm=(1,),
        scratch=[
            pltpu.VMEM((ns * nx * ny, nz), f32),
            pltpu.VMEM((2 * nk, cells), bf16),
            pltpu.SemaphoreType.DMA,
            pltpu.SemaphoreType.DMA,
        ],
    )
    totals = sum_over(totals, ("gz", "gy", "gx"))
    inverse_rows = 1.0 / (
        cells * lax.axis_size("gx") * lax.axis_size("gy") * lax.axis_size("gz")
    )
    modes, factor, coeffs = finish(shape, inverse_rows, totals, snap, both)
    return (modes, factor, coeffs.T, bound_next.reshape(shape))


def solution(mesh):
    return jax.shard_map(
        on_device,
        mesh=mesh,
        in_specs=(
            P(None, ("grp", "gx"), "gy", "gz"),
            P("grp", None),
            P(None, ("grp", "gx"), "gy", "gz"),
            P(None, ("grp", "gx"), "gy", "gz"),
            P(("grp", "gx"), "gy", "gz"),
            P(("grp", "gx"), "gy", "gz"),
            P(),
            P(),
            P(),
            P("grp"),
        ),
        out_specs=(
            P(None, ("grp", "gx"), "gy", "gz"),
            P("grp", None),
            P("grp", None),
            P(None, ("grp", "gx"), "gy", "gz"),
        ),
        check_vma=False,
    )
```

time: 81.8 us -> 61.6 us (0.75)
  Pallas kernels: 37.7 us -> 21.1 us
  local copies, waits for them, and re-layouts: 5.07 us -> 0.12 us
  waiting for transfers between devices: 14.2 us -> 17.7 us
  other arithmetic: 1.6 us -> 0.06 us
    pallas_call x2 -> x1, Pallas kernels: 13 us -> 7.15 us  [start(): pl.pallas_call(functools.partial(start_kernel, shape, nk), in_specs=[pl.B...]
    pallas_call x2, Pallas kernels: 14.2 us -> 8.34 us  [step_call(): pl.pallas_call(kernel, in_specs=in_specs, out_specs=[pl.BlockSpec(memory_...]
    pallas_call x1, Pallas kernels: 10.4 us -> 5.66 us  [finish(): pl.pallas_call(functools.partial(finish_kernel, shape, nk, inverse_rows),...]
    unnamed x24 -> x14, local copies, waits for them, and re-layouts: 4.38 us -> 0.03 us
    ppermute x2, waiting for transfers between devices: 2.81 us -> 5.64 us  [exchange(): lax.ppermute(sent[0], axis, down)]
    ppermute x4, waiting for transfers between devices: 0.67 us -> 2.24 us  [exchange(): got.append([lax.ppermute(sent[0], axis, [(0, 1), (1, 0)])])]
    add x4, other arithmetic: 1.58 us -> 0.05 us  [sum_over(): value + lax.ppermute(value, axis, [(i, i ^ stride) for i in range(size)])]
    ppermute x4, waiting for transfers between devices: 10.7 us -> 9.84 us  [sum_over(): lax.ppermute(value, axis, [(i, i ^ stride) for i in range(size)])]
  transfers between devices with their start and end apart: 12 -> 12, of which waited for: 6 -> 8; matrix products, arithmetic and copies ran while one was open for 1% -> 0% of each run, Pallas kernels for 6% -> 0%
where the time goes in v1:
time: 61.6 us; the launch traced here: 61.4 us
  starting transfers between devices  21.6 us (35%)
  Pallas kernels  21.1 us (34%)
  waiting for transfers between devices  17.7 us (29%)
  between operations  0.81 us (1%)
    ppermute x4, waiting for transfers between devices, sum_over(): lax.ppermute(value, axis, [(i, i ^ stride) for i in range(size)])  9.84 us
    ppermute x2, starting transfers between devices, exchange(): lax.ppermute(sent[1], axis, up)  8.98 us
    pallas_call x2, Pallas kernels, step_call(): pl.pallas_call(kernel, in_specs=in_specs, out_specs=[pl.BlockSpec(memory_...  8.34 us
    pallas_call x1, Pallas kernels, start(): pl.pallas_call(functools.partial(start_kernel, shape, nk), in_specs=[pl.B...  7.15 us
    ppermute x4, starting transfers between devices, sum_over(): lax.ppermute(value, axis, [(i, i ^ stride) for i in range(size)])  6.89 us
    pallas_call x1, Pallas kernels, finish(): pl.pallas_call(functools.partial(finish_kernel, shape, nk, inverse_rows),...  5.66 us
    ppermute x2, waiting for transfers between devices, exchange(): lax.ppermute(sent[0], axis, down)  5.64 us
    ppermute x4, starting transfers between devices, exchange(): got.append([lax.ppermute(sent[0], axis, [(0, 1), (1, 0)])])  3.11 us
  transfers between devices with their start and end apart: 12, of which 8 were waited for; matrix products, arithmetic and copies ran while one was open for 0% of the time, Pallas kernels for 0%

profile of v1, /device:TPU:0, one launch (start us, length us, event | category | flops | bytes accessed | tf_op | source)
XLA Modules:
  0.0 61.4 jit_solution(15039943673912413757)
XLA Ops:
  0.7 7.1 %start.1 = (f32[32,8192]{1,0:T(8,128)S(1)}, bf16[256,8192]{1,0:T(8,128)(2,1)}, f32[128,128]{1,0:T(8,128)S(1)}, f32[32,1024]{1,0:T(8,128)S(1)}, f32[32,1024]{1,0:...) custom-call(f32[32,128]{1,0:T(8,128)} %bitcast.8, f32[128,8,8,128]{3,2,1,0:T(8,128)} %basis.1, ...), custom_call_target="tpu_custom_call" | custom-call | tf_op jit(solution)/shard_map/start/pallas_call | solution.py:157
  7.9 5.0 %collective-permute-start = (f32[32,1024]{1,0:T(8,128)S(1)}, f32[32,1024]{1,0:T(8,128)S(1)}, u32[]{:S(2)}, u32[]{:S(2)}) collective-permute-start(f32[32,1024]{1,0:T(8,128)S(1)} %get-tuple-element.24), channel_id=1, source_target_pairs={{0,4},{4,8},{8,12},{1,5},{5,9},{9,13},{2,6},{6,10},{10,14},{3,7},{... | collective-permute-start | bytes 393224 | tf_op jit(solution)/shard_map/ppermute | solution.py:93
  12.8 1.3 %collective-permute-start.1 = (f32[32,1024]{1,0:T(8,128)S(1)}, f32[32,1024]{1,0:T(8,128)S(1)}, u32[]{:S(2)}, u32[]{:S(2)}) collective-permute-start(f32[32,1024]{1,0:T(8,128)S(1)} %get-tuple-element.25), channel_id=1, source_target_pairs={{4,0},{8,4},{12,8},{5,1},{9,5},{13,9},{6,2},{10,6},{14,10},{7,3},{... | collective-permute-start | bytes 393224 | tf_op jit(solution)/shard_map/ppermute | solution.py:93
  14.1 1.6 %collective-permute-start.2 = (f32[32,1024]{1,0:T(8,128)S(1)}, f32[32,1024]{1,0:T(8,128)S(1)}, u32[]{:S(2)}, u32[]{:S(2)}) collective-permute-start(f32[32,1024]{1,0:T(8,128)S(1)} %get-tuple-element.26), channel_id=1, source_target_pairs={{0,2},{2,0},{1,3},{3,1},{4,6},{6,4},{5,7},{7,5},{8,10},{10,8},{9,1... | collective-permute-start | bytes 393224 | tf_op jit(solution)/shard_map/ppermute | solution.py:89
  15.7 0.1 copy.17.rates
  15.8 1.1 %collective-permute-done.3.rest_3_ = f32[32,128]{1,0:T(8,128)S(1)} collective-permute-done((f32[32,128]{1,0:T(8,128)S(1)}, f32[32,128]{1,0:T(8,128)S(1)}, u32[]{:S(2)}, u32[]{:S(2)}) %collective-permute-start.3) | collective-permute-done | bytes 16416 | tf_op jit(solution)/shard_map/ppermute | solution.py:89
  16.9 0.0 collective-permute-done.rest_0_
  16.9 2.8 %collective-permute-done.1.rest_1_ = f32[32,1024]{1,0:T(8,128)S(1)} collective-permute-done((f32[32,1024]{1,0:T(8,128)S(1)}, f32[32,1024]{1,0:T(8,128)S(1)}, u32[]{:S(2)}, u32[]{:S(2)}) %collective-permute-start.1) | collective-permute-done | bytes 131104 | tf_op jit(solution)/shard_map/ppermute | solution.py:93
  19.7 3.5 %first_step.1 = (f32[32,8192]{1,0:T(8,128)S(1)}, f32[32,8192]{1,0:T(8,128)S(1)}, f32[32,1024]{1,0:T(8,128)S(1)}, f32[32,1024]{1,0:T(8,128)S(1)}, f32[32,1024]{1,0:T(8,128)S(1)}, /*index=5*/f32[32,128]{1,0:T(8,128)S(1)}) custom-call(f32[32,8192]{1,0:T(8,128)S(1)} %get-tuple-element.23.analyte, f32[2048,128]{1,0:T(8,128)S(1)} %bitcast.7, ...), custom_call_target="tpu_custom_call" | custom-call | tf_op jit(solution)/shard_map/first_step/pallas_call | solution.py:349
  23.3 4.0 %collective-permute-start.4 = (f32[32,1024]{1,0:T(8,128)S(1)}, f32[32,1024]{1,0:T(8,128)S(1)}, u32[]{:S(2)}, u32[]{:S(2)}) collective-permute-start(f32[32,1024]{1,0:T(8,128)S(1)} %get-tuple-element.32), channel_id=1, source_target_pairs={{0,4},{4,8},{8,12},{1,5},{5,9},{9,13},{2,6},{6,10},{10,14},{3,7},{... | collective-permute-start | bytes 393224 | tf_op jit(solution)/shard_map/ppermute | solution.py:93
  27.3 1.3 %collective-permute-start.5 = (f32[32,1024]{1,0:T(8,128)S(1)}, f32[32,1024]{1,0:T(8,128)S(1)}, u32[]{:S(2)}, u32[]{:S(2)}) collective-permute-start(f32[32,1024]{1,0:T(8,128)S(1)} %get-tuple-element.33), channel_id=1, source_target_pairs={{4,0},{8,4},{12,8},{5,1},{9,5},{13,9},{6,2},{10,6},{14,10},{7,3},{... | collective-permute-start | bytes 393224 | tf_op jit(solution)/shard_map/ppermute | solution.py:93
  28.6 1.6 %collective-permute-start.6 = (f32[32,1024]{1,0:T(8,128)S(1)}, f32[32,1024]{1,0:T(8,128)S(1)}, u32[]{:S(2)}, u32[]{:S(2)}) collective-permute-start(f32[32,1024]{1,0:T(8,128)S(1)} %get-tuple-element.34), channel_id=1, source_target_pairs={{0,2},{2,0},{1,3},{3,1},{4,6},{6,4},{5,7},{7,5},{8,10},{10,8},{9,1... | collective-permute-start | bytes 393224 | tf_op jit(solution)/shard_map/ppermute | solution.py:89
  30.1 1.2 %collective-permute-done.7.rest_3_ = f32[32,128]{1,0:T(8,128)S(1)} collective-permute-done((f32[32,128]{1,0:T(8,128)S(1)}, f32[32,128]{1,0:T(8,128)S(1)}, u32[]{:S(2)}, u32[]{:S(2)}) %collective-permute-start.7) | collective-permute-done | bytes 16416 | tf_op jit(solution)/shard_map/ppermute | solution.py:89
  31.3 2.8 %collective-permute-done.5.rest_1_ = f32[32,1024]{1,0:T(8,128)S(1)} collective-permute-done((f32[32,1024]{1,0:T(8,128)S(1)}, f32[32,1024]{1,0:T(8,128)S(1)}, u32[]{:S(2)}, u32[]{:S(2)}) %collective-permute-start.5) | collective-permute-done | bytes 131104 | tf_op jit(solution)/shard_map/ppermute | solution.py:93
  34.1 4.8 %second_step.1 = (bf16[64,8192]{1,0:T(8,128)(2,1)S(1)}, f32[2048,128]{1,0:T(8,128)}, f32[192,128]{1,0:T(8,128)S(1)}) custom-call(f32[32,8192]{1,0:T(8,128)S(1)} %get-tuple-element.28.analyte, f32[32,8192]{1,0:T(8,128)S(1)} %get-tuple-element.29.bound, f32[8,8,128]{2,1,0:T(8,128)S(1)} %copy-done.1, s32[8,8,128]{2,1,0:T(8,128)S(1)} %copy-done.2, ...), custom_call_target="tpu_custom_call" | custom-call | tf_op jit(solution)/shard_map/second_step/pallas_call | solution.py:349
  39.0 0.1 collective-permute-start.8
  39.0 1.3 %collective-permute-done.8 = f32[192,128]{1,0:T(8,128)S(1)} collective-permute-done((f32[192,128]{1,0:T(8,128)S(1)}, f32[192,128]{1,0:T(8,128)S(1)}, u32[]{:S(2)}, u32[]{:S(2)}) %collective-permute-start.8) | collective-permute-done | bytes 98336 | tf_op jit(solution)/shard_map/ppermute | solution.py:472
  40.4 1.6 %collective-permute-start.9 = (f32[192,128]{1,0:T(8,128)S(1)}, f32[192,128]{1,0:T(8,128)S(1)}, u32[]{:S(2)}, u32[]{:S(2)}) collective-permute-start(f32[192,128]{1,0:T(8,128)S(1)} %add.12), channel_id=1, source_target_pairs={{0,2},{2,0},{1,3},{3,1},{4,6},{6,4},{5,7},{7,5},{8,10},{10,8},{9,1... | collective-permute-start | bytes 294920 | tf_op jit(solution)/shard_map/ppermute | solution.py:472
  41.9 3.4 %collective-permute-done.9 = f32[192,128]{1,0:T(8,128)S(1)} collective-permute-done((f32[192,128]{1,0:T(8,128)S(1)}, f32[192,128]{1,0:T(8,128)S(1)}, u32[]{:S(2)}, u32[]{:S(2)}) %collective-permute-start.9) | collective-permute-done | bytes 98336 | tf_op jit(solution)/shard_map/ppermute | solution.py:472
  45.3 2.2 %collective-permute-start.10 = (f32[192,128]{1,0:T(8,128)S(1)}, f32[192,128]{1,0:T(8,128)S(1)}, u32[]{:S(2)}, u32[]{:S(2)}) collective-permute-start(f32[192,128]{1,0:T(8,128)S(1)} %add.13), channel_id=1, source_target_pairs={{0,4},{4,0},{8,12},{12,8},{1,5},{5,1},{9,13},{13,9},{2,6},{6,2},{1... | collective-permute-start | bytes 294920 | tf_op jit(solution)/shard_map/ppermute | solution.py:472
  47.5 2.6 %collective-permute-done.10 = f32[192,128]{1,0:T(8,128)S(1)} collective-permute-done((f32[192,128]{1,0:T(8,128)S(1)}, f32[192,128]{1,0:T(8,128)S(1)}, u32[]{:S(2)}, u32[]{:S(2)}) %collective-permute-start.10) | collective-permute-done | bytes 98336 | tf_op jit(solution)/shard_map/ppermute | solution.py:472
  50.1 3.1 %collective-permute-start.11 = (f32[192,128]{1,0:T(8,128)S(1)}, f32[192,128]{1,0:T(8,128)S(1)}, u32[]{:S(2)}, u32[]{:S(2)}) collective-permute-start(f32[192,128]{1,0:T(8,128)S(1)} %add.14), channel_id=1, source_target_pairs={{0,8},{4,12},{8,0},{12,4},{1,9},{5,13},{9,1},{13,5},{2,10},{6,14},... | collective-permute-start | bytes 294920 | tf_op jit(solution)/shard_map/ppermute | solution.py:472
  53.2 2.6 %collective-permute-done.11 = f32[192,128]{1,0:T(8,128)S(1)} collective-permute-done((f32[192,128]{1,0:T(8,128)S(1)}, f32[192,128]{1,0:T(8,128)S(1)}, u32[]{:S(2)}, u32[]{:S(2)}) %collective-permute-start.11) | collective-permute-done | bytes 98336 | tf_op jit(solution)/shard_map/ppermute | solution.py:472
  55.8 5.7 %finish.1 = (f32[32,8,8,128]{3,2,1,0:T(8,128)}, f32[32,32]{1,0:T(8,128)}, f32[32,128]{1,0:T(8,128)}) custom-call(f32[192,128]{1,0:T(8,128)S(1)} %add.15.totals, bf16[64,8192]{1,0:T(8,128)(2,1)S(1)} %get-tuple-element.37.snap, bf16[256,8192]{1,0:T(8,128)(2,1)} %get-tuple-element.30.both), custom_call_target="tpu_custom_call" | custom-call | tf_op jit(solution)/shard_map/finish/pallas_call | solution.py:443
  (24 shorter events, 0.1 us)
Async XLA Ops:
  0.6 15.1 %copy-start.4 = (f32[32]{0:T(128)S(1)}, f32[32]{0:T(128)}, u32[]{:S(2)}) copy-start(f32[32]{0:T(128)} %param.19) | copy-start | bytes 388
  0.6 15.1 %copy-start.5 = (f32[32]{0:T(128)S(1)}, f32[32]{0:T(128)}, u32[]{:S(2)}) copy-start(f32[32]{0:T(128)} %param.18) | copy-start | bytes 388
  0.7 15.0 %copy-start.6 = (f32[32]{0:T(128)S(1)}, f32[32]{0:T(128)}, u32[]{:S(2)}) copy-start(f32[32]{0:T(128)} %param.17) | copy-start | bytes 388
  0.7 19.0 %copy-start.3 = (f32[3]{0:T(128)S(1)}, f32[3]{0:T(128)}, u32[]{:S(2)}) copy-start(f32[3]{0:T(128)} %capacity.3) | copy-start | bytes 40
  0.7 19.0 %copy-start.2 = (s32[8,8,128]{2,1,0:T(8,128)S(1)}, s32[8,8,128]{2,1,0:T(8,128)}, u32[]{:S(2)}) copy-start(s32[8,8,128]{2,1,0:T(8,128)} %zone_labels.3) | copy-start | bytes 98308
  0.7 19.0 %copy-start.1 = (f32[8,8,128]{2,1,0:T(8,128)S(1)}, f32[8,8,128]{2,1,0:T(8,128)}, u32[]{:S(2)}) copy-start(f32[8,8,128]{2,1,0:T(8,128)} %velocity.3) | copy-start | bytes 98308
  0.7 19.0 %copy-start = (f32[32,8,8,128]{3,2,1,0:T(8,128)S(1)}, f32[32,8,8,128]{3,2,1,0:T(8,128)}, u32[]{:S(2)}) copy-start(f32[32,8,8,128]{3,2,1,0:T(8,128)} %param.13) | copy-start | bytes 3145732
  7.9 9.0 %collective-permute-start = (f32[32,1024]{1,0:T(8,128)S(1)}, f32[32,1024]{1,0:T(8,128)S(1)}, u32[]{:S(2)}, u32[]{:S(2)}) collective-permute-start(f32[32,1024]{1,0:T(8,128)S(1)} %get-tuple-element.24), channel_id=1, source_target_pairs={{0,4},{4,8},{8,12},{1,5},{5,9},{9,13},{2,6},{6,10},{10,14},{3,7},{... | collective-permute-start | bytes 393224 | tf_op jit(solution)/shard_map/ppermute | solution.py:93
  12.8 6.9 %collective-permute-start.1 = (f32[32,1024]{1,0:T(8,128)S(1)}, f32[32,1024]{1,0:T(8,128)S(1)}, u32[]{:S(2)}, u32[]{:S(2)}) collective-permute-start(f32[32,1024]{1,0:T(8,128)S(1)} %get-tuple-element.25), channel_id=1, source_target_pairs={{4,0},{8,4},{12,8},{5,1},{9,5},{13,9},{6,2},{10,6},{14,10},{7,3},{... | collective-permute-start | bytes 393224 | tf_op jit(solution)/shard_map/ppermute | solution.py:93
  14.1 5.6 %collective-permute-start.2 = (f32[32,1024]{1,0:T(8,128)S(1)}, f32[32,1024]{1,0:T(8,128)S(1)}, u32[]{:S(2)}, u32[]{:S(2)}) collective-permute-start(f32[32,1024]{1,0:T(8,128)S(1)} %get-tuple-element.26), channel_id=1, source_target_pairs={{0,2},{2,0},{1,3},{3,1},{4,6},{6,4},{5,7},{7,5},{8,10},{10,8},{9,1... | collective-permute-start | bytes 393224 | tf_op jit(solution)/shard_map/ppermute | solution.py:89
  15.7 1.2 %collective-permute-start.3 = (f32[32,128]{1,0:T(8,128)S(1)}, f32[32,128]{1,0:T(8,128)S(1)}, u32[]{:S(2)}, u32[]{:S(2)}) collective-permute-start(f32[32,128]{1,0:T(8,128)S(1)} %get-tuple-element.27), channel_id=1, source_target_pairs={{0,1},{1,0},{2,3},{3,2},{4,5},{5,4},{6,7},{7,6},{8,9},{9,8},{10,11... | collective-permute-start | bytes 49160 | tf_op jit(solution)/shard_map/ppermute | solution.py:89
  23.3 8.1 %collective-permute-start.4 = (f32[32,1024]{1,0:T(8,128)S(1)}, f32[32,1024]{1,0:T(8,128)S(1)}, u32[]{:S(2)}, u32[]{:S(2)}) collective-permute-start(f32[32,1024]{1,0:T(8,128)S(1)} %get-tuple-element.32), channel_id=1, source_target_pairs={{0,4},{4,8},{8,12},{1,5},{5,9},{9,13},{2,6},{6,10},{10,14},{3,7},{... | collective-permute-start | bytes 393224 | tf_op jit(solution)/shard_map/ppermute | solution.py:93
  27.3 6.9 %collective-permute-start.5 = (f32[32,1024]{1,0:T(8,128)S(1)}, f32[32,1024]{1,0:T(8,128)S(1)}, u32[]{:S(2)}, u32[]{:S(2)}) collective-permute-start(f32[32,1024]{1,0:T(8,128)S(1)} %get-tuple-element.33), channel_id=1, source_target_pairs={{4,0},{8,4},{12,8},{5,1},{9,5},{13,9},{6,2},{10,6},{14,10},{7,3},{... | collective-permute-start | bytes 393224 | tf_op jit(solution)/shard_map/ppermute | solution.py:93
  28.6 5.6 %collective-permute-start.6 = (f32[32,1024]{1,0:T(8,128)S(1)}, f32[32,1024]{1,0:T(8,128)S(1)}, u32[]{:S(2)}, u32[]{:S(2)}) collective-permute-start(f32[32,1024]{1,0:T(8,128)S(1)} %get-tuple-element.34), channel_id=1, source_target_pairs={{0,2},{2,0},{1,3},{3,1},{4,6},{6,4},{5,7},{7,5},{8,10},{10,8},{9,1... | collective-permute-start | bytes 393224 | tf_op jit(solution)/shard_map/ppermute | solution.py:89
  30.1 1.2 %collective-permute-start.7 = (f32[32,128]{1,0:T(8,128)S(1)}, f32[32,128]{1,0:T(8,128)S(1)}, u32[]{:S(2)}, u32[]{:S(2)}) collective-permute-start(f32[32,128]{1,0:T(8,128)S(1)} %get-tuple-element.35), channel_id=1, source_target_pairs={{0,1},{1,0},{2,3},{3,2},{4,5},{5,4},{6,7},{7,6},{8,9},{9,8},{10,11... | collective-permute-start | bytes 49160 | tf_op jit(solution)/shard_map/ppermute | solution.py:89
  39.0 1.4 %collective-permute-start.8 = (f32[192,128]{1,0:T(8,128)S(1)}, f32[192,128]{1,0:T(8,128)S(1)}, u32[]{:S(2)}, u32[]{:S(2)}) collective-permute-start(f32[192,128]{1,0:T(8,128)S(1)} %get-tuple-element.36), channel_id=1, source_target_pairs={{0,1},{1,0},{2,3},{3,2},{4,5},{5,4},{6,7},{7,6},{8,9},{9,8},{10,11... | collective-permute-start | bytes 294920 | tf_op jit(solution)/shard_map/ppermute | solution.py:472
  40.4 4.9 %collective-permute-start.9 = (f32[192,128]{1,0:T(8,128)S(1)}, f32[192,128]{1,0:T(8,128)S(1)}, u32[]{:S(2)}, u32[]{:S(2)}) collective-permute-start(f32[192,128]{1,0:T(8,128)S(1)} %add.12), channel_id=1, source_target_pairs={{0,2},{2,0},{1,3},{3,1},{4,6},{6,4},{5,7},{7,5},{8,10},{10,8},{9,1... | collective-permute-start | bytes 294920 | tf_op jit(solution)/shard_map/ppermute | solution.py:472
  45.3 4.8 %collective-permute-start.10 = (f32[192,128]{1,0:T(8,128)S(1)}, f32[192,128]{1,0:T(8,128)S(1)}, u32[]{:S(2)}, u32[]{:S(2)}) collective-permute-start(f32[192,128]{1,0:T(8,128)S(1)} %add.13), channel_id=1, source_target_pairs={{0,4},{4,0},{8,12},{12,8},{1,5},{5,1},{9,13},{13,9},{2,6},{6,2},{1... | collective-permute-start | bytes 294920 | tf_op jit(solution)/shard_map/ppermute | solution.py:472
  50.1 5.7 %collective-permute-start.11 = (f32[192,128]{1,0:T(8,128)S(1)}, f32[192,128]{1,0:T(8,128)S(1)}, u32[]{:S(2)}, u32[]{:S(2)}) collective-permute-start(f32[192,128]{1,0:T(8,128)S(1)} %add.14), channel_id=1, source_target_pairs={{0,8},{4,12},{8,0},{12,4},{1,9},{5,13},{9,1},{13,5},{2,10},{6,14},... | collective-permute-start | bytes 294920 | tf_op jit(solution)/shard_map/ppermute | solution.py:472

commit v2 on v1

--- a/solution.py
+++ b/solution.py
@@ -36,18 +36,23 @@
     return 0 if size == 1 else 1 if size == 2 else 2
 
 
+def faces_up(axis, swap):
+    return lax.rem(lax.axis_index(axis) + swap, 2) == 0
+
+
+def doubling(axis):
+    size = lax.axis_size(axis)
+    return size > 1 and size & (size - 1) == 0
+
+
 def pack_column(packed, axis, tile, cell):
-    lanes = tile.shape[1]
     here = lax.broadcasted_iota(jnp.int32, tile.shape, 1) == cell
-    after = lax.rem(cell + 1, lanes)
-    if len(packed) == 1:
-        shifts = [jnp.where(lax.axis_index(axis) == 0, after, cell)]
-    else:
-        shifts = [cell, after]
+    after = lax.rem(cell + 1, tile.shape[1])
+    shifts = [jnp.where(faces_up(axis, i), after, cell) for i in range(len(packed))]
     return [jnp.where(here, pltpu.roll(tile, s, 1), p) for p, s in zip(packed, shifts)]
 
 
-def copy_faces(faces, field, shape):
+def copy_faces(faces, field, shape, extra):
     _, nx, ny, nz = shape
     slab = ny * nz
     for refs, axis, width, count, last in (
@@ -55,24 +60,50 @@
         (faces[1], "gy", nz, nx, slab - nz),
     ):
         for i, ref in enumerate(refs):
-            if len(refs) == 1:
-                at = pl.multiple_of(jnp.where(lax.axis_index(axis) == 0, last, 0), nz)
-            else:
-                at = last * i
+            at = pl.multiple_of(jnp.where(faces_up(axis, i), last, 0), nz)
             for j in range(count):
                 ref[:, j * width : (j + 1) * width] = field[:, pl.ds(at + j * slab, width)]
-
-
-def face_shapes(shape):
-    ns, nx, ny, nz = shape
-    return (
-        [(ns, ny * nz)] * face_count("gx"),
-        [(ns, nx * nz)] * face_count("gy"),
-        [(ns, nz)] * face_count("gz"),
-    )
-
-
-def unflatten(flat, shape):
+        if refs and axis in extra:
+            refs[0][:, count * width :] = extra[axis]
+
+
+def pack_symmetric(square, rows):
+    n = square.shape[0]
+    half = n // 2
+    low = square[half:, half:]
+    low = jnp.concatenate([low[: half // 2], low[half // 2 :]], axis=1)
+    whole = jnp.concatenate([square[:half], low], axis=0)
+    return jnp.concatenate([whole[i : i + rows] for i in range(0, whole.shape[0], rows)], axis=1)
+
+
+def unpack_symmetric(rows):
+    n = rows.shape[1]
+    half = n // 2
+    low = rows[half:]
+    low = jnp.concatenate([low[:, :half], low[:, half:]], axis=0)
+    corner = rows[:half, half:]
+    return jnp.concatenate([rows[:half], jnp.concatenate([corner.T, low], axis=1)], axis=0)
+
+
+def pack_square(square, lanes):
+    rows = square.shape[0] ** 2 // lanes
+    return jnp.concatenate([square[i : i + rows] for i in range(0, square.shape[0], rows)], axis=1)
+
+
+def unpack_square(rows, n):
+    return jnp.concatenate([rows[:, i : i + n] for i in range(0, rows.shape[1], n)], axis=0)
+
+
+def face_shapes(shape, extra=(), width=0):
+    ns, nx, ny, nz = shape
+    out = []
+    for axis, lanes in (("gx", ny * nz), ("gy", nx * nz), ("gz", nz)):
+        n = face_count(axis)
+        out.append([(ns, lanes + (width if i == 0 and axis in extra else 0)) for i in range(n)])
+    return out
+
+
+def unflatten(flat):
     out = []
     for axis in ("gx", "gy", "gz"):
         n = face_count(axis)
@@ -82,23 +113,20 @@
 
 
 def exchange(faces):
-    got = []
-    for axis, sent in zip(("gx", "gy", "gz"), faces, strict=True):
+    got = {}
+    for axis, sent in reversed(list(zip(("gx", "gy", "gz"), faces, strict=True))):
         size = lax.axis_size(axis)
-        if len(sent) == 1:
-            got.append([lax.ppermute(sent[0], axis, [(0, 1), (1, 0)])])
-        elif len(sent) == 2:
-            up = [(i, i + 1) for i in range(size - 1)]
-            down = [(j, i) for i, j in up]
-            got.append([lax.ppermute(sent[1], axis, up), lax.ppermute(sent[0], axis, down)])
-        else:
-            got.append([])
-    return got
+        got[axis] = []
+        for i, face in enumerate(sent):
+            pairs = [(j, j + 1) for j in range(i, size - 1, 2)]
+            pairs = pairs + [(j, i) for i, j in pairs]
+            got[axis].append(lax.ppermute(face, axis, pairs))
+    return [got["gx"], got["gy"], got["gz"]]
 
 
 def start_kernel(shape, nk, reduced, basis, fine, out_a, out_b, out_bb, *rest):
     ns, nx, ny, nz = shape
-    faces, scratch = unflatten(rest, shape)
+    faces, scratch = unflatten(rest)
     r_buf, b_buf, f_buf, rows, both, r_sem, b_sem, f_sem, o_sem = scratch
     slab_at = lambda x: pl.ds(pl.multiple_of(x * ny * nz, ny * nz), ny * nz)
     o_copy = lambda x: pltpu.make_async_copy(both.at[:, slab_at(x)], out_b.at[:, slab_at(x)], o_sem.at[x])
@@ -142,10 +170,10 @@
     packed = lax.fori_loop(0, nx, body, [jnp.zeros((ns, nz), f32) for _ in faces[2]])
     for ref, value in zip(faces[2], packed):
         ref[...] = value
-    copy_faces(faces, out_a, shape)
     product = mm_nt(both[:nk, :], both[...])
     mixed = product[:, nk:]
-    out_bb[...] = product[:, :nk] + mixed + mixed.T
+    out_bb[...] = pack_symmetric(product[:, :nk] + mixed + mixed.T, ns)
+    copy_faces(faces, out_a, shape, {"gy": out_bb[...]} if doubling("gy") else {})
     for x in range(nx):
         o_copy(x).wait()
 
@@ -153,7 +181,8 @@
 def start(reduced, basis, fine):
     nk = basis.shape[0]
     ns, nx, ny, nz = shape = fine.shape
-    groups = [s for g in face_shapes(shape) for s in g]
+    width = nk * nk * 3 // 4 // ns
+    groups = [s for g in face_shapes(shape, ["gy"] if doubling("gy") else [], width) for s in g]
     outs = pl.pallas_call(
         functools.partial(start_kernel, shape, nk),
         in_specs=[pl.BlockSpec(memory_space=pltpu.HBM)] * 3,
@@ -164,7 +193,7 @@
         out_shape=[
             jax.ShapeDtypeStruct((ns, nx * ny * nz), f32),
             pltpu.HBM((2 * nk, nx * ny * nz), bf16),
-            jax.ShapeDtypeStruct((nk, nk), f32),
+            jax.ShapeDtypeStruct((ns, width), f32),
         ]
         + [jax.ShapeDtypeStruct(s, f32) for s in groups],
         scratch_shapes=[
@@ -181,12 +210,14 @@
         compiler_params=pltpu.CompilerParams(vmem_limit_bytes=vmem_limit),
         name="start",
     )(*[pltpu.with_memory_space_constraint(a, pltpu.HBM) for a in (reduced, basis, fine)])
-    faces, _ = unflatten(outs[3:], shape)
+    faces, _ = unflatten(outs[3:])
     return outs[:3], faces
 
 
-def beside_of(got, at_start):
-    return got[0] if len(got) == 1 else got[0 if at_start else 1]
+def beside_of(got, axis, before):
+    if len(got) == 1:
+        return got[0][...]
+    return jnp.where(faces_up(axis, 1 if before else 0), got[1][...], got[0][...])
 
 
 def stencil(shape, x, pad, y_got, z_got, bound_tile, store, args):
@@ -204,6 +235,7 @@
     off = jnp.broadcast_to(rates[:, 1:2], (ns, nz))
     lane = lax.broadcasted_iota(jnp.int32, (ns, nz), 1)
     x_at = pl.multiple_of(x * nz, nz)
+    y_at = [ref.at[:, pl.ds(x_at, nz)] for ref in y_got]
     left, right = lane == 0, lane == nz - 1
     inner = lane == jnp.where(first["gz"], nz - 1, 0)
     inner_low = lane == jnp.where(first["gz"], -1, 0)
@@ -217,13 +249,13 @@
         if y > 0:
             y_low = tile(1, -1)
         elif y_got:
-            y_low = jnp.where(first["gy"], centre, beside_of(y_got, True)[:, pl.ds(x_at, nz)])
+            y_low = jnp.where(first["gy"], centre, beside_of(y_at, "gy", True))
         else:
             y_low = centre
         if y < ny - 1:
             y_high = tile(1, 1)
         elif y_got:
-            y_high = jnp.where(last["gy"], centre, beside_of(y_got, False)[:, pl.ds(x_at, nz)])
+            y_high = jnp.where(last["gy"], centre, beside_of(y_at, "gy", False))
         else:
             y_high = centre
         z_low, z_high = pltpu.roll(centre, 1, 1), pltpu.roll(centre, nz - 1, 1)
@@ -233,9 +265,9 @@
             shift = jnp.where(first["gz"], nz - 1 - cell, lax.rem(nz - cell, nz))
             edge = jnp.where(inner, pltpu.roll(z_got[0][...], shift, 1), edge)
         elif len(z_got) == 2:
-            beside = pltpu.roll(z_got[0][...], lax.rem(nz - cell, nz), 1)
+            beside = pltpu.roll(beside_of(z_got, "gz", True), lax.rem(nz - cell, nz), 1)
             edge = jnp.where(inner_low, beside, edge)
-            beside = pltpu.roll(z_got[1][...], nz - 1 - cell, 1)
+            beside = pltpu.roll(beside_of(z_got, "gz", False), nz - 1 - cell, 1)
             edge = jnp.where(inner_high, beside, edge)
         z_low = jnp.where(left, edge, z_low)
         z_high = jnp.where(right, edge, z_high)
@@ -258,23 +290,25 @@
     ns, nx, ny, nz = shape
     slab = ny * nz
     pad[:, slab : (nx + 1) * slab] = analyte[...]
-    at_inlet = lax.axis_index("gx") == 0
-    at_outlet = lax.axis_index("gx") == lax.axis_size("gx") - 1
-    inlet = jnp.broadcast_to(rates[:, 2:3], (ns, slab))
-    outlet = analyte[:, (nx - 1) * slab :]
-    if x_got:
-        pad[:, :slab] = jnp.where(at_inlet, inlet, beside_of(x_got, True)[...])
-        pad[:, (nx + 1) * slab :] = jnp.where(at_outlet, outlet, beside_of(x_got, False)[...])
-    else:
-        pad[:, :slab] = inlet
-        pad[:, (nx + 1) * slab :] = outlet
-
-
-def first_kernel(shape, analyte, bound, velocity, zone_labels, capacity, rates, *rest):
-    ns, nx, ny, nz = shape
-    got, rest = unflatten(rest, shape)
-    out_a, out_bound = rest[:2]
-    faces, (pad,) = unflatten(rest[2:], shape)
+    end = (nx + 1) * slab
+    for i, ref in enumerate(x_got):
+        at = pl.multiple_of(jnp.where(faces_up("gx", i), end, 0), slab)
+        pad[:, pl.ds(at, slab)] = ref[:, :slab]
+
+    @pl.when(lax.axis_index("gx") == 0)
+    def _():
+        pad[:, :slab] = jnp.broadcast_to(rates[:, 2:3], (ns, slab))
+
+    @pl.when(lax.axis_index("gx") == lax.axis_size("gx") - 1)
+    def _():
+        pad[:, end:] = analyte[:, (nx - 1) * slab :]
+
+
+def first_kernel(shape, analyte, bound, velocity, zone_labels, capacity, rates, bb, *rest):
+    ns, nx, ny, nz = shape
+    got, rest = unflatten(rest)
+    out_a, out_bound, out_bb = rest[:3]
+    faces, (pad,) = unflatten(rest[3:])
     fill_pad(shape, pad, analyte, got[0], rates)
 
     def body(x, packed):
@@ -296,13 +330,14 @@
     packed = lax.fori_loop(0, nx, body, [jnp.zeros((ns, nz), f32) for _ in faces[2]])
     for ref, value in zip(faces[2], packed):
         ref[...] = value
-    copy_faces(faces, out_a, shape)
-
-
-def second_kernel(shape, nk, analyte, bound, velocity, zone_labels, capacity, rates, both, bb, *rest):
-    ns, nx, ny, nz = shape
-    got, rest = unflatten(rest, shape)
-    out_s, out_bound, out_totals, pad, bound_buf, both_buf, sem, both_sem = rest
+    out_bb[...] = bb[...] + got[1][0][:, nx * nz :] if doubling("gy") else bb[...]
+    copy_faces(faces, out_a, shape, {"gx": out_bb[...]} if doubling("gx") else {})
+
+
+def second_kernel(shape, nk, analyte, bound, velocity, zone_labels, capacity, rates, bb, both, *rest):
+    ns, nx, ny, nz = shape
+    got, rest = unflatten(rest)
+    out_s, out_bound, out_totals, out_bb, pad, bound_buf, both_buf, sem, both_sem = rest
     both_copy = pltpu.make_async_copy(both, both_buf, both_sem)
     both_copy.start()
     fill_pad(shape, pad, analyte, got[0], rates)
@@ -331,16 +366,16 @@
     out_totals[:ns, :] = product[:ns, :nk] + product[:ns, nk:] + product[ns:, :nk]
     square = mm_nt(snap, snap)
     square = square[:ns, :ns] + square[:ns, ns:] + square[ns:, :ns]
-    out_totals[ns : 2 * ns, :] = jnp.concatenate(
-        [square, jnp.zeros((ns, nk - ns), f32)], axis=1
-    )
-    out_totals[2 * ns :, :] = bb[...]
+    out_totals[ns:, :] = pack_square(square, nk)
+    total = bb[...] + got[0][0][:, ny * nz :] if doubling("gx") else bb[...]
+    for i in range(total.shape[1] // nk):
+        out_bb[i * ns : (i + 1) * ns, :] = total[:, i * nk : (i + 1) * nk]
     copy.wait()
 
 
 def step_call(kernel, shape, operands, got, out_shape, name, hbm=(), scratch=()):
     ns, nx, ny, nz = shape
-    space = {4: pltpu.SMEM, 6: pltpu.HBM if scratch else pltpu.VMEM}
+    space = {4: pltpu.SMEM, 7: pltpu.HBM if scratch else pltpu.VMEM}
     flat = [g for group in got for g in group]
     in_specs = [
         pl.BlockSpec(memory_space=space.get(i, pltpu.VMEM))
@@ -395,7 +430,8 @@
     out_coeffs[...] = coeffs
     c_high, c_low = split(coeffs)
     c_twice = jnp.concatenate([c_high, c_high], axis=1)
-    weighted = mm_exact(coeffs, totals[2 * ns :, :] * inverse_rows)
+    squares = ns + ns * ns // nk
+    weighted = mm_exact(coeffs, unpack_symmetric(totals[squares:, :] * inverse_rows))
     exact_nt = functools.partial(
         lax.dot_general,
         dimension_numbers=(((1,), (1,)), ((), ())),
@@ -403,7 +439,7 @@
         preferred_element_type=f32,
     )
     mixed = exact_nt(coeffs, coeffs)
-    gram = totals[ns : 2 * ns, :ns] * inverse_rows - mixed - mixed + exact_nt(weighted, coeffs)
+    gram = unpack_square(totals[ns:squares, :] * inverse_rows, ns) - mixed - mixed + exact_nt(weighted, coeffs)
 
     pieces = 2 * nx if ny % 2 == 0 and 2 * nx <= ns else nx
     width = nx * slab // pieces
@@ -461,15 +497,23 @@
     )(totals, snap, both)
 
 
-def sum_over(value, axes):
-    for axis in axes:
+def sum_over(small, large):
+    def swapped(value, axis, stride):
         size = lax.axis_size(axis)
-        if size & (size - 1):
-            value = lax.psum(value, axis)
+        return value + lax.ppermute(value, axis, [(i, i ^ stride) for i in range(size)])
+
+    for axis in ("gy", "gx"):
+        if doubling(axis):
+            small = swapped(small, axis, 1)
+    value = jnp.concatenate([small, large], axis=0)
+    for axis in ("gz", "gy", "gx"):
+        size = lax.axis_size(axis)
+        if not doubling(axis):
+            value = lax.psum(value, axis) if size > 1 else value
             continue
-        stride = 1
+        stride = 1 if axis == "gz" else 2
         while stride < size:
-            value = value + lax.ppermute(value, axis, [(i, i ^ stride) for i in range(size)])
+            value = swapped(value, axis, stride)
             stride *= 2
     return value
 
@@ -498,23 +542,28 @@
     outs = step_call(
         functools.partial(first_kernel, shape),
         shape,
-        [analyte, bound_state.reshape(ns * nx * ny, nz)] + fields,
+        [analyte, bound_state.reshape(ns * nx * ny, nz)] + fields + [bb],
         got,
-        [struct((ns, cells), f32), struct((ns, cells), f32)]
-        + [struct(s, f32) for g in face_shapes(shape) for s in g],
+        [struct((ns, cells), f32), struct((ns, cells), f32), struct(bb.shape, f32)]
+        + [
+            struct(s, f32)
+            for g in face_shapes(shape, ["gx"] if doubling("gx") else [], bb.shape[1])
+            for s in g
+        ],
         "first_step",
     )
-    faces, _ = unflatten(outs[2:], shape)
+    faces, _ = unflatten(outs[3:])
     got = exchange(faces)
-    snap, bound_next, totals = step_call(
+    snap, bound_next, small, large = step_call(
         functools.partial(second_kernel, shape, nk),
         shape,
-        [outs[0], outs[1]] + fields + [both, bb],
+        [outs[0], outs[1]] + fields + [outs[2], both],
         got,
         [
             struct((2 * ns, cells), bf16),
             struct((ns * nx * ny, nz), f32),
-            struct((2 * ns + nk, nk), f32),
+            struct((ns + ns * ns // nk, nk), f32),
+            struct((bb.size // nk, nk), f32),
         ],
         "second_step",
         hbm=(1,),
@@ -525,7 +574,7 @@
             pltpu.SemaphoreType.DMA,
         ],
     )
-    totals = sum_over(totals, ("gz", "gy", "gx"))
+    totals = sum_over(small, large)
     inverse_rows = 1.0 / (
         cells * lax.axis_size("gx") * lax.axis_size("gy") * lax.axis_size("gz")
     )

time: 61.6 us -> 56.1 us (0.911)
  starting transfers between devices: 21.6 us -> 16.6 us
  waiting for transfers between devices: 17.7 us -> 17 us
    ppermute x12, starting transfers between devices: 21.6 us -> 16.6 us  [the longest x8 11.2 us: exchange(): got[axis].append(lax.ppermute(face, axis, pairs))]
    ppermute x12, waiting for transfers between devices: 17.7 us -> 17 us  [the longest x4 10 us: swapped(): lax.ppermute(value, axis, [(i, i ^ stride) for i in range(size)])]
where the time goes in v2:
time: 56.1 us; the launch traced here: 55.9 us
  Pallas kernels  21.4 us (38%)
  waiting for transfers between devices  17 us (30%)
  starting transfers between devices  16.6 us (30%)
  between operations  0.82 us (1%)
    ppermute x8, starting transfers between devices, exchange(): got[axis].append(lax.ppermute(face, axis, pairs))  11.2 us
    ppermute x4, waiting for transfers between devices, swapped(): lax.ppermute(value, axis, [(i, i ^ stride) for i in range(size)])  10 us
    pallas_call x2, Pallas kernels, step_call(): pl.pallas_call(kernel, in_specs=in_specs, out_specs=[pl.BlockSpec(memory_...  8.54 us
    pallas_call x1, Pallas kernels, start(): pl.pallas_call(functools.partial(start_kernel, shape, nk), in_specs=[pl.B...  7.17 us
    ppermute x8, waiting for transfers between devices, exchange(): got[axis].append(lax.ppermute(face, axis, pairs))  6.95 us
    pallas_call x1, Pallas kernels, finish(): pl.pallas_call(functools.partial(finish_kernel, shape, nk, inverse_rows),...  5.67 us
    ppermute x4, starting transfers between devices, swapped(): lax.ppermute(value, axis, [(i, i ^ stride) for i in range(size)])  5.42 us
  transfers between devices with their start and end apart: 12, of which 8 were waited for; matrix products, arithmetic and copies ran while one was open for 0% of the time, Pallas kernels for 0%

profile of v2, /device:TPU:0, one launch (start us, length us, event | category | flops | bytes accessed | tf_op | source)
XLA Modules:
  0.0 55.9 jit_solution(16146599099042588142)
XLA Ops:
  0.7 7.2 %start.1 = (f32[32,8192]{1,0:T(8,128)S(1)}, bf16[256,8192]{1,0:T(8,128)(2,1)}, f32[32,384]{1,0:T(8,128)S(1)}, f32[32,1024]{1,0:T(8,128)S(1)}, f32[32,1024]{1,0:T...) custom-call(f32[32,128]{1,0:T(8,128)} %bitcast.8, f32[128,8,8,128]{3,2,1,0:T(8,128)} %basis.1, ...), custom_call_target="tpu_custom_call" | custom-call | tf_op jit(solution)/shard_map/start/pallas_call | solution.py:186
  7.9 3.0 %collective-permute-start.2 = (f32[32,1408]{1,0:T(8,128)S(1)}, f32[32,1408]{1,0:T(8,128)S(1)}, u32[]{:S(2)}, u32[]{:S(2)}) collective-permute-start(f32[32,1408]{1,0:T(8,128)S(1)} %get-tuple-element.29), channel_id=1, source_target_pairs={{0,2},{2,0},{1,3},{3,1},{4,6},{6,4},{5,7},{7,5},{8,10},{10,8},{9,1... | collective-permute-start | bytes 540680 | tf_op jit(solution)/shard_map/ppermute | solution.py:123
  10.9 1.6 %collective-permute-start = (f32[32,1024]{1,0:T(8,128)S(1)}, f32[32,1024]{1,0:T(8,128)S(1)}, u32[]{:S(2)}, u32[]{:S(2)}) collective-permute-start(f32[32,1024]{1,0:T(8,128)S(1)} %get-tuple-element.27), channel_id=1, source_target_pairs={{0,4},{8,12},{4,0},{12,8},{1,5},{9,13},{5,1},{13,9},{2,6},{10,14},... | collective-permute-start | bytes 393224 | tf_op jit(solution)/shard_map/ppermute | solution.py:123
  12.5 0.7 %collective-permute-start.1 = (f32[32,1024]{1,0:T(8,128)S(1)}, f32[32,1024]{1,0:T(8,128)S(1)}, u32[]{:S(2)}, u32[]{:S(2)}) collective-permute-start(f32[32,1024]{1,0:T(8,128)S(1)} %get-tuple-element.28), channel_id=1, source_target_pairs={{4,8},{8,4},{5,9},{9,5},{6,10},{10,6},{7,11},{11,7},{20,24},{24,20... | collective-permute-start | bytes 393224 | tf_op jit(solution)/shard_map/ppermute | solution.py:123
  13.2 0.1 collective-permute-start.3
  13.3 0.1 copy.17.rates
  13.4 1.0 %collective-permute-done.3.rest_3_ = f32[32,128]{1,0:T(8,128)S(1)} collective-permute-done((f32[32,128]{1,0:T(8,128)S(1)}, f32[32,128]{1,0:T(8,128)S(1)}, u32[]{:S(2)}, u32[]{:S(2)}) %collective-permute-start.3) | collective-permute-done | bytes 16416 | tf_op jit(solution)/shard_map/ppermute | solution.py:123
  14.4 1.5 %collective-permute-done.rest_0_ = f32[32,1024]{1,0:T(8,128)S(1)} collective-permute-done((f32[32,1024]{1,0:T(8,128)S(1)}, f32[32,1024]{1,0:T(8,128)S(1)}, u32[]{:S(2)}, u32[]{:S(2)}) %collective-permute-start) | collective-permute-done | bytes 131104 | tf_op jit(solution)/shard_map/ppermute | solution.py:123
  15.9 3.6 %first_step.1 = (f32[32,8192]{1,0:T(8,128)S(1)}, f32[32,8192]{1,0:T(8,128)S(1)}, f32[32,384]{1,0:T(8,128)S(1)}, f32[32,1408]{1,0:T(8,128)S(1)}, f32[32,1024]{1,0...) custom-call(f32[32,8192]{1,0:T(8,128)S(1)} %get-tuple-element.25.analyte, f32[2048,128]{1,0:T(8,128)S(1)} %bitcast.7, ...), custom_call_target="tpu_custom_call" | custom-call | tf_op jit(solution)/shard_map/first_step/pallas_call | solution.py:384
  19.5 4.6 %collective-permute-start.4 = (f32[32,1408]{1,0:T(8,128)S(1)}, f32[32,1408]{1,0:T(8,128)S(1)}, u32[]{:S(2)}, u32[]{:S(2)}) collective-permute-start(f32[32,1408]{1,0:T(8,128)S(1)} %get-tuple-element.35), channel_id=1, source_target_pairs={{0,4},{8,12},{4,0},{12,8},{1,5},{9,13},{5,1},{13,9},{2,6},{10,14},... | collective-permute-start | bytes 540680 | tf_op jit(solution)/shard_map/ppermute | solution.py:123
  24.1 0.7 %collective-permute-start.5 = (f32[32,1024]{1,0:T(8,128)S(1)}, f32[32,1024]{1,0:T(8,128)S(1)}, u32[]{:S(2)}, u32[]{:S(2)}) collective-permute-start(f32[32,1024]{1,0:T(8,128)S(1)} %get-tuple-element.36), channel_id=1, source_target_pairs={{4,8},{8,4},{5,9},{9,5},{6,10},{10,6},{7,11},{11,7},{20,24},{24,20... | collective-permute-start | bytes 393224 | tf_op jit(solution)/shard_map/ppermute | solution.py:123
  24.8 0.6 %collective-permute-start.6 = (f32[32,1024]{1,0:T(8,128)S(1)}, f32[32,1024]{1,0:T(8,128)S(1)}, u32[]{:S(2)}, u32[]{:S(2)}) collective-permute-start(f32[32,1024]{1,0:T(8,128)S(1)} %get-tuple-element.37), channel_id=1, source_target_pairs={{0,2},{2,0},{1,3},{3,1},{4,6},{6,4},{5,7},{7,5},{8,10},{10,8},{9,1... | collective-permute-start | bytes 393224 | tf_op jit(solution)/shard_map/ppermute | solution.py:123
  25.4 1.2 %collective-permute-done.7.rest_3_ = f32[32,128]{1,0:T(8,128)S(1)} collective-permute-done((f32[32,128]{1,0:T(8,128)S(1)}, f32[32,128]{1,0:T(8,128)S(1)}, u32[]{:S(2)}, u32[]{:S(2)}) %collective-permute-start.7) | collective-permute-done | bytes 16416 | tf_op jit(solution)/shard_map/ppermute | solution.py:123
  26.6 3.2 %collective-permute-done.6.rest_2_ = f32[32,1024]{1,0:T(8,128)S(1)} collective-permute-done((f32[32,1024]{1,0:T(8,128)S(1)}, f32[32,1024]{1,0:T(8,128)S(1)}, u32[]{:S(2)}, u32[]{:S(2)}) %collective-permute-start.6) | collective-permute-done | bytes 131104 | tf_op jit(solution)/shard_map/ppermute | solution.py:123
  29.8 4.9 %second_step.1 = (bf16[64,8192]{1,0:T(8,128)(2,1)S(1)}, f32[2048,128]{1,0:T(8,128)}, f32[40,128]{1,0:T(8,128)S(1)}, f32[96,128]{1,0:T(8,128)S(1)}) custom-call(f32[32,8192]{1,0:T(8,128)S(1)} %get-tuple-element.31.analyte, f32[32,8192]{1,0:T(8,128)S(1)} %get-tuple-element.32.bound, f32[8,8,128]{2,1,0:T(8,128)S(1)} %copy-done.1, s32[8,8,128]{2,1,0:T(8,128)S(1)} %copy-done.2, ...), custom_call_target="tpu_custom_call" | custom-call | tf_op jit(solution)/shard_map/second_step/pallas_call | solution.py:384
  34.8 0.6 %collective-permute-start.8 = (f32[40,128]{1,0:T(8,128)S(1)}, f32[40,128]{1,0:T(8,128)S(1)}, u32[]{:S(2)}, u32[]{:S(2)}) collective-permute-start(f32[40,128]{1,0:T(8,128)S(1)} %get-tuple-element.39), channel_id=1, source_target_pairs={{0,2},{2,0},{1,3},{3,1},{4,6},{6,4},{5,7},{7,5},{8,10},{10,8},{9,1... | collective-permute-start | bytes 61448 | tf_op jit(solution)/shard_map/ppermute | solution.py:503
  35.4 3.2 %collective-permute-done.8 = f32[40,128]{1,0:T(8,128)S(1)} collective-permute-done((f32[40,128]{1,0:T(8,128)S(1)}, f32[40,128]{1,0:T(8,128)S(1)}, u32[]{:S(2)}, u32[]{:S(2)}) %collective-permute-start.8) | collective-permute-done | bytes 20512 | tf_op jit(solution)/shard_map/ppermute | solution.py:503
  38.6 3.2 %collective-permute-start.9 = (f32[40,128]{1,0:T(8,128)S(1)}, f32[40,128]{1,0:T(8,128)S(1)}, u32[]{:S(2)}, u32[]{:S(2)}) collective-permute-start(f32[40,128]{1,0:T(8,128)S(1)} %add.12), channel_id=1, source_target_pairs={{0,4},{4,0},{8,12},{12,8},{1,5},{5,1},{9,13},{13,9},{2,6},{6,2},{1... | collective-permute-start | bytes 61448 | tf_op jit(solution)/shard_map/ppermute | solution.py:503
  41.9 1.8 %collective-permute-done.9 = f32[40,128]{1,0:T(8,128)S(1)} collective-permute-done((f32[40,128]{1,0:T(8,128)S(1)}, f32[40,128]{1,0:T(8,128)S(1)}, u32[]{:S(2)}, u32[]{:S(2)}) %collective-permute-start.9) | collective-permute-done | bytes 20512 | tf_op jit(solution)/shard_map/ppermute | solution.py:503
  43.6 0.1 collective-permute-start.10
  43.7 1.2 %collective-permute-done.10 = f32[136,128]{1,0:T(8,128)S(1)} collective-permute-done((f32[136,128]{1,0:T(8,128)S(1)}, f32[136,128]{1,0:T(8,128)S(1)}, u32[]{:S(2)}, u32[]{:S(2)}) %collective-permute-start.10) | collective-permute-done | bytes 69664 | tf_op jit(solution)/shard_map/ppermute | solution.py:503
  45.0 1.5 %collective-permute-start.11 = (f32[136,128]{1,0:T(8,128)S(1)}, f32[136,128]{1,0:T(8,128)S(1)}, u32[]{:S(2)}, u32[]{:S(2)}) collective-permute-start(f32[136,128]{1,0:T(8,128)S(1)} %fusion), channel_id=1, source_target_pairs={{0,8},{4,12},{8,0},{12,4},{1,9},{5,13},{9,1},{13,5},{2,10},{6,14},... | collective-permute-start | bytes 208904 | tf_op jit(solution)/shard_map/ppermute | solution.py:503
  46.5 3.7 %collective-permute-done.11 = f32[136,128]{1,0:T(8,128)S(1)} collective-permute-done((f32[136,128]{1,0:T(8,128)S(1)}, f32[136,128]{1,0:T(8,128)S(1)}, u32[]{:S(2)}, u32[]{:S(2)}) %collective-permute-start.11) | collective-permute-done | bytes 69664 | tf_op jit(solution)/shard_map/ppermute | solution.py:503
  50.3 5.7 %finish.1 = (f32[32,8,8,128]{3,2,1,0:T(8,128)}, f32[32,32]{1,0:T(8,128)}, f32[32,128]{1,0:T(8,128)}) custom-call(f32[136,128]{1,0:T(8,128)S(1)} %add.15.totals, bf16[64,8192]{1,0:T(8,128)(2,1)S(1)} %get-tuple-element.41.snap, bf16[256,8192]{1,0:T(8,128)(2,1)} %get-tuple-element.34.both), custom_call_target="tpu_custom_call" | custom-call | tf_op jit(solution)/shard_map/finish/pallas_call | solution.py:479
  (25 shorter events, 0.1 us)
Async XLA Ops:
  0.6 12.6 %copy-start.4 = (f32[32]{0:T(128)S(1)}, f32[32]{0:T(128)}, u32[]{:S(2)}) copy-start(f32[32]{0:T(128)} %param.19) | copy-start | bytes 388
  0.6 12.6 %copy-start.5 = (f32[32]{0:T(128)S(1)}, f32[32]{0:T(128)}, u32[]{:S(2)}) copy-start(f32[32]{0:T(128)} %param.18) | copy-start | bytes 388
  0.7 12.6 %copy-start.6 = (f32[32]{0:T(128)S(1)}, f32[32]{0:T(128)}, u32[]{:S(2)}) copy-start(f32[32]{0:T(128)} %param.17) | copy-start | bytes 388
  0.7 15.2 %copy-start.3 = (f32[3]{0:T(128)S(1)}, f32[3]{0:T(128)}, u32[]{:S(2)}) copy-start(f32[3]{0:T(128)} %capacity.3) | copy-start | bytes 40
  0.7 15.2 %copy-start.2 = (s32[8,8,128]{2,1,0:T(8,128)S(1)}, s32[8,8,128]{2,1,0:T(8,128)}, u32[]{:S(2)}) copy-start(s32[8,8,128]{2,1,0:T(8,128)} %zone_labels.3) | copy-start | bytes 98308
  0.7 15.2 %copy-start.1 = (f32[8,8,128]{2,1,0:T(8,128)S(1)}, f32[8,8,128]{2,1,0:T(8,128)}, u32[]{:S(2)}) copy-start(f32[8,8,128]{2,1,0:T(8,128)} %velocity.3) | copy-start | bytes 98308
  0.7 15.2 %copy-start = (f32[32,8,8,128]{3,2,1,0:T(8,128)S(1)}, f32[32,8,8,128]{3,2,1,0:T(8,128)}, u32[]{:S(2)}) copy-start(f32[32,8,8,128]{3,2,1,0:T(8,128)} %param.13) | copy-start | bytes 3145732
  7.9 8.0 %collective-permute-start.2 = (f32[32,1408]{1,0:T(8,128)S(1)}, f32[32,1408]{1,0:T(8,128)S(1)}, u32[]{:S(2)}, u32[]{:S(2)}) collective-permute-start(f32[32,1408]{1,0:T(8,128)S(1)} %get-tuple-element.29), channel_id=1, source_target_pairs={{0,2},{2,0},{1,3},{3,1},{4,6},{6,4},{5,7},{7,5},{8,10},{10,8},{9,1... | collective-permute-start | bytes 540680 | tf_op jit(solution)/shard_map/ppermute | solution.py:123
  10.9 5.0 %collective-permute-start = (f32[32,1024]{1,0:T(8,128)S(1)}, f32[32,1024]{1,0:T(8,128)S(1)}, u32[]{:S(2)}, u32[]{:S(2)}) collective-permute-start(f32[32,1024]{1,0:T(8,128)S(1)} %get-tuple-element.27), channel_id=1, source_target_pairs={{0,4},{8,12},{4,0},{12,8},{1,5},{9,13},{5,1},{13,9},{2,6},{10,14},... | collective-permute-start | bytes 393224 | tf_op jit(solution)/shard_map/ppermute | solution.py:123
  12.5 3.4 %collective-permute-start.1 = (f32[32,1024]{1,0:T(8,128)S(1)}, f32[32,1024]{1,0:T(8,128)S(1)}, u32[]{:S(2)}, u32[]{:S(2)}) collective-permute-start(f32[32,1024]{1,0:T(8,128)S(1)} %get-tuple-element.28), channel_id=1, source_target_pairs={{4,8},{8,4},{5,9},{9,5},{6,10},{10,6},{7,11},{11,7},{20,24},{24,20... | collective-permute-start | bytes 393224 | tf_op jit(solution)/shard_map/ppermute | solution.py:123
  13.2 1.2 %collective-permute-start.3 = (f32[32,128]{1,0:T(8,128)S(1)}, f32[32,128]{1,0:T(8,128)S(1)}, u32[]{:S(2)}, u32[]{:S(2)}) collective-permute-start(f32[32,128]{1,0:T(8,128)S(1)} %get-tuple-element.30), channel_id=1, source_target_pairs={{0,1},{1,0},{2,3},{3,2},{4,5},{5,4},{6,7},{7,6},{8,9},{9,8},{10,11... | collective-permute-start | bytes 49160 | tf_op jit(solution)/shard_map/ppermute | solution.py:123
  19.5 10.3 %collective-permute-start.4 = (f32[32,1408]{1,0:T(8,128)S(1)}, f32[32,1408]{1,0:T(8,128)S(1)}, u32[]{:S(2)}, u32[]{:S(2)}) collective-permute-start(f32[32,1408]{1,0:T(8,128)S(1)} %get-tuple-element.35), channel_id=1, source_target_pairs={{0,4},{8,12},{4,0},{12,8},{1,5},{9,13},{5,1},{13,9},{2,6},{10,14},... | collective-permute-start | bytes 540680 | tf_op jit(solution)/shard_map/ppermute | solution.py:123
  24.1 2.5 %collective-permute-start.5 = (f32[32,1024]{1,0:T(8,128)S(1)}, f32[32,1024]{1,0:T(8,128)S(1)}, u32[]{:S(2)}, u32[]{:S(2)}) collective-permute-start(f32[32,1024]{1,0:T(8,128)S(1)} %get-tuple-element.36), channel_id=1, source_target_pairs={{4,8},{8,4},{5,9},{9,5},{6,10},{10,6},{7,11},{11,7},{20,24},{24,20... | collective-permute-start | bytes 393224 | tf_op jit(solution)/shard_map/ppermute | solution.py:123
  24.8 5.0 %collective-permute-start.6 = (f32[32,1024]{1,0:T(8,128)S(1)}, f32[32,1024]{1,0:T(8,128)S(1)}, u32[]{:S(2)}, u32[]{:S(2)}) collective-permute-start(f32[32,1024]{1,0:T(8,128)S(1)} %get-tuple-element.37), channel_id=1, source_target_pairs={{0,2},{2,0},{1,3},{3,1},{4,6},{6,4},{5,7},{7,5},{8,10},{10,8},{9,1... | collective-permute-start | bytes 393224 | tf_op jit(solution)/shard_map/ppermute | solution.py:123
  25.4 1.2 %collective-permute-start.7 = (f32[32,128]{1,0:T(8,128)S(1)}, f32[32,128]{1,0:T(8,128)S(1)}, u32[]{:S(2)}, u32[]{:S(2)}) collective-permute-start(f32[32,128]{1,0:T(8,128)S(1)} %get-tuple-element.38), channel_id=1, source_target_pairs={{0,1},{1,0},{2,3},{3,2},{4,5},{5,4},{6,7},{7,6},{8,9},{9,8},{10,11... | collective-permute-start | bytes 49160 | tf_op jit(solution)/shard_map/ppermute | solution.py:123
  34.8 3.8 %collective-permute-start.8 = (f32[40,128]{1,0:T(8,128)S(1)}, f32[40,128]{1,0:T(8,128)S(1)}, u32[]{:S(2)}, u32[]{:S(2)}) collective-permute-start(f32[40,128]{1,0:T(8,128)S(1)} %get-tuple-element.39), channel_id=1, source_target_pairs={{0,2},{2,0},{1,3},{3,1},{4,6},{6,4},{5,7},{7,5},{8,10},{10,8},{9,1... | collective-permute-start | bytes 61448 | tf_op jit(solution)/shard_map/ppermute | solution.py:503
  38.6 5.0 %collective-permute-start.9 = (f32[40,128]{1,0:T(8,128)S(1)}, f32[40,128]{1,0:T(8,128)S(1)}, u32[]{:S(2)}, u32[]{:S(2)}) collective-permute-start(f32[40,128]{1,0:T(8,128)S(1)} %add.12), channel_id=1, source_target_pairs={{0,4},{4,0},{8,12},{12,8},{1,5},{5,1},{9,13},{13,9},{2,6},{6,2},{1... | collective-permute-start | bytes 61448 | tf_op jit(solution)/shard_map/ppermute | solution.py:503
  43.6 1.3 %collective-permute-start.10 = (f32[136,128]{1,0:T(8,128)S(1)}, f32[136,128]{1,0:T(8,128)S(1)}, u32[]{:S(2)}, u32[]{:S(2)}) collective-permute-start(f32[136,128]{1,0:T(8,128)S(1)} %pad_maximum_fusion), channel_id=1, source_target_pairs={{0,1},{1,0},{2,3},{3,2},{4,5},{5,4},{6,7},{7,6},{8,9},{9,8},{10,11... | collective-permute-start | bytes 208904 | tf_op jit(solution)/shard_map/ppermute | solution.py:503
  45.0 5.3 %collective-permute-start.11 = (f32[136,128]{1,0:T(8,128)S(1)}, f32[136,128]{1,0:T(8,128)S(1)}, u32[]{:S(2)}, u32[]{:S(2)}) collective-permute-start(f32[136,128]{1,0:T(8,128)S(1)} %fusion), channel_id=1, source_target_pairs={{0,8},{4,12},{8,0},{12,4},{1,9},{5,13},{9,1},{13,5},{2,10},{6,14},... | collective-permute-start | bytes 208904 | tf_op jit(solution)/shard_map/ppermute | solution.py:503

commit v3 on v2

--- a/solution.py
+++ b/solution.py
@@ -124,12 +124,17 @@
     return [got["gx"], got["gy"], got["gz"]]
 
 
-def start_kernel(shape, nk, reduced, basis, fine, out_a, out_b, out_bb, *rest):
-    ns, nx, ny, nz = shape
+def start_kernel(shape, nk, reduced, basis, fine, bound, on, off, inlet, out_a, out_bb, out_bound, out_rates, *rest):
+    ns, nx, ny, nz = shape
+    both, rest = rest[:nx], rest[nx:]
     faces, scratch = unflatten(rest)
-    r_buf, b_buf, f_buf, rows, both, r_sem, b_sem, f_sem, o_sem = scratch
-    slab_at = lambda x: pl.ds(pl.multiple_of(x * ny * nz, ny * nz), ny * nz)
-    o_copy = lambda x: pltpu.make_async_copy(both.at[:, slab_at(x)], out_b.at[:, slab_at(x)], o_sem.at[x])
+    r_buf, b_buf, f_buf, rows, on_buf, off_buf, inlet_buf, r_sem, b_sem, f_sem, bound_sem, rate_sem = scratch
+    rate_bufs = (on_buf, off_buf, inlet_buf)
+    rate_copies = [
+        pltpu.make_async_copy(a, b, rate_sem.at[i])
+        for i, (a, b) in enumerate(zip((on, off, inlet), rate_bufs))
+    ]
+    bound_copy = lambda x: pltpu.make_async_copy(bound.at[:, x], out_bound.at[x], bound_sem.at[x])
     r_copy = pltpu.make_async_copy(reduced, r_buf, r_sem)
     f_copy = pltpu.make_async_copy(fine, f_buf, f_sem)
     b_copy = lambda x: pltpu.make_async_copy(basis.at[:, x], b_buf.at[x], b_sem.at[x])
@@ -138,80 +143,98 @@
     f_copy.start()
     for x in range(1, nx):
         b_copy(x).start()
+    for copy in rate_copies:
+        copy.start()
+    for x in range(nx):
+        bound_copy(x).start()
     r_copy.wait()
     r_high, r_low = split(r_buf[...])
     r_twice = jnp.concatenate([r_high, r_high], axis=1)
+    for copy in rate_copies:
+        copy.wait()
+    lane = lax.broadcasted_iota(jnp.int32, (ns, ns), 1)
+    own = lax.broadcasted_iota(jnp.int32, (ns, ns), 0) == lane
+    column = lambda ref: jnp.sum(
+        jnp.where(own, jnp.broadcast_to(ref[...], (ns, ns)), 0.0), axis=1, keepdims=True
+    )
+    lane = lax.broadcasted_iota(jnp.int32, out_rates.shape, 1)
+    out_rates[...] = jnp.where(
+        lane == 0, column(on_buf), jnp.where(lane == 1, column(off_buf), column(inlet_buf))
+    )
     group = max(1, min(ny, 256 // nz))
 
     def body(x, packed):
         b_copy(x).wait()
 
-        @pl.when(x == 0)
-        def _():
+        if x == 0:
             f_copy.wait()
-
         flat = b_buf.at[x].reshape(nk * ny, nz)
         rows[...] = f_buf[:, pl.ds(x, 1)].reshape(ns * ny, nz).astype(f32)
         for y in range(0, ny, group):
-            at = pl.multiple_of(x * ny * nz, ny * nz) + y * nz
+            at = (x * ny + y) * nz
             parts = [split(flat[pl.ds(y + i, nk, stride=ny), :]) for i in range(group)]
             high = jnp.concatenate([p[0] for p in parts], axis=1)
             low = jnp.concatenate([p[1] for p in parts], axis=1)
-            both[:nk, pl.ds(at, group * nz)] = high
-            both[nk:, pl.ds(at, group * nz)] = low
+            both[x][:nk, pl.ds(y * nz, group * nz)] = high
+            both[x][nk:, pl.ds(y * nz, group * nz)] = low
             slab = mm(r_twice, jnp.concatenate([high, low], axis=0)) + mm(r_low, high)
             for i in range(group):
                 tile = slab[:, i * nz : (i + 1) * nz] + rows[pl.ds(y + i, ns, stride=ny), :]
                 out_a[:, pl.ds(at + i * nz, nz)] = tile
                 packed = pack_column(packed, "gz", tile, x * ny + y + i)
-        o_copy(x).start()
         return packed
 
-    packed = lax.fori_loop(0, nx, body, [jnp.zeros((ns, nz), f32) for _ in faces[2]])
+    packed = [jnp.zeros((ns, nz), f32) for _ in faces[2]]
+    for x in range(nx):
+        packed = body(x, packed)
     for ref, value in zip(faces[2], packed):
         ref[...] = value
-    product = mm_nt(both[:nk, :], both[...])
+    product = sum(mm_nt(piece[:nk, :], piece[...]) for piece in both)
     mixed = product[:, nk:]
     out_bb[...] = pack_symmetric(product[:, :nk] + mixed + mixed.T, ns)
     copy_faces(faces, out_a, shape, {"gy": out_bb[...]} if doubling("gy") else {})
     for x in range(nx):
-        o_copy(x).wait()
-
-
-def start(reduced, basis, fine):
+        bound_copy(x).wait()
+
+
+def start(reduced, basis, fine, bound, rates):
     nk = basis.shape[0]
     ns, nx, ny, nz = shape = fine.shape
     width = nk * nk * 3 // 4 // ns
     groups = [s for g in face_shapes(shape, ["gy"] if doubling("gy") else [], width) for s in g]
     outs = pl.pallas_call(
         functools.partial(start_kernel, shape, nk),
-        in_specs=[pl.BlockSpec(memory_space=pltpu.HBM)] * 3,
+        in_specs=[pl.BlockSpec(memory_space=pltpu.HBM)] * 7,
         out_specs=[
-            pl.BlockSpec(memory_space=pltpu.HBM if i == 1 else pltpu.VMEM)
-            for i in range(3 + len(groups))
+            pl.BlockSpec(memory_space=pltpu.VMEM) for _ in range(4 + nx + len(groups))
         ],
         out_shape=[
             jax.ShapeDtypeStruct((ns, nx * ny * nz), f32),
-            pltpu.HBM((2 * nk, nx * ny * nz), bf16),
             jax.ShapeDtypeStruct((ns, width), f32),
+            jax.ShapeDtypeStruct((nx, ns, ny, nz), f32),
+            jax.ShapeDtypeStruct((ns, nz), f32),
         ]
+        + [jax.ShapeDtypeStruct((2 * nk, ny * nz), bf16)] * nx
         + [jax.ShapeDtypeStruct(s, f32) for s in groups],
         scratch_shapes=[
             pltpu.VMEM((ns, nk), f32),
             pltpu.VMEM((nx, nk, ny, nz), f32),
             pltpu.VMEM((ns, nx, ny, nz), bf16),
             pltpu.VMEM((ns * ny, nz), f32),
-            pltpu.VMEM((2 * nk, nx * ny * nz), bf16),
+            pltpu.VMEM((1, ns), f32),
+            pltpu.VMEM((1, ns), f32),
+            pltpu.VMEM((1, ns), f32),
             pltpu.SemaphoreType.DMA,
             pltpu.SemaphoreType.DMA((nx,)),
             pltpu.SemaphoreType.DMA,
             pltpu.SemaphoreType.DMA((nx,)),
+            pltpu.SemaphoreType.DMA((3,)),
         ],
         compiler_params=pltpu.CompilerParams(vmem_limit_bytes=vmem_limit),
         name="start",
-    )(*[pltpu.with_memory_space_constraint(a, pltpu.HBM) for a in (reduced, basis, fine)])
-    faces, _ = unflatten(outs[3:])
-    return outs[:3], faces
+    )(*[pltpu.with_memory_space_constraint(a, pltpu.HBM) for a in (reduced, basis, fine, bound, *rates)])
+    faces, _ = unflatten(outs[4 + nx :])
+    return outs[:4], outs[4 : 4 + nx], faces
 
 
 def beside_of(got, axis, before):
@@ -273,7 +296,7 @@
         z_high = jnp.where(right, edge, z_high)
         near = behind + ahead + y_low + y_high + z_low + z_high
         row = lambda slab: jnp.broadcast_to(slab[y : y + 1], (ns, nz))
-        bound_now = bound_tile(cell, at)
+        bound_now = bound_tile(y, at)
         reaction = row(surface_slab) * (
             on * centre * (row(cap_slab) - bound_now) - off * bound_now
         )
@@ -283,7 +306,7 @@
             - row(velocity_slab) * (centre - behind)
             - reaction
         )
-        store(cell, at, moved, bound_now + reaction)
+        store(cell, y, at, moved, bound_now + reaction)
 
 
 def fill_pad(shape, pad, analyte, x_got, rates):
@@ -314,10 +337,12 @@
     def body(x, packed):
         packs = [packed]
 
-        def bound_tile(cell, at):
-            return bound[pl.ds(cell, ns, stride=nx * ny), :]
-
-        def store(cell, at, moved, bound_then):
+        rows = bound.at[x].reshape(ns * ny, nz)
+
+        def bound_tile(y, at):
+            return rows[pl.ds(y, ns, stride=ny), :]
+
+        def store(cell, y, at, moved, bound_then):
             out_bound[:, pl.ds(at, nz)] = bound_then
             out_a[:, pl.ds(at, nz)] = moved
             packs[0] = pack_column(packs[0], "gz", moved, cell)
@@ -334,20 +359,21 @@
     copy_faces(faces, out_a, shape, {"gx": out_bb[...]} if doubling("gx") else {})
 
 
-def second_kernel(shape, nk, analyte, bound, velocity, zone_labels, capacity, rates, bb, both, *rest):
-    ns, nx, ny, nz = shape
+def second_kernel(shape, nk, analyte, bound, velocity, zone_labels, capacity, rates, bb, *rest):
+    ns, nx, ny, nz = shape
+    both, rest = rest[:nx], rest[nx:]
     got, rest = unflatten(rest)
-    out_s, out_bound, out_totals, out_bb, pad, bound_buf, both_buf, sem, both_sem = rest
-    both_copy = pltpu.make_async_copy(both, both_buf, both_sem)
-    both_copy.start()
+    out_s, out_bound, out_totals, out_bb, pad, bound_buf, sem = rest
     fill_pad(shape, pad, analyte, got[0], rates)
 
     def body(x, carry):
-        def bound_tile(cell, at):
+        rows = bound_buf.at[x].reshape(ns * ny, nz)
+
+        def bound_tile(y, at):
             return bound[:, pl.ds(at, nz)]
 
-        def store(cell, at, moved, bound_then):
-            bound_buf[pl.ds(cell, ns, stride=nx * ny), :] = bound_then
+        def store(cell, y, at, moved, bound_then):
+            rows[pl.ds(y, ns, stride=ny), :] = bound_then
             high, low = split(moved)
             out_s[:ns, pl.ds(at, nz)] = high
             out_s[ns:, pl.ds(at, nz)] = low
@@ -355,14 +381,14 @@
         stencil(
             shape, x, pad, got[1], got[2], bound_tile, store, (velocity, zone_labels, capacity, rates)
         )
+        copy(x).start()
         return carry
 
+    copy = lambda x: pltpu.make_async_copy(bound_buf.at[x], out_bound.at[:, x], sem.at[x])
     lax.fori_loop(0, nx, body, 0)
-    copy = pltpu.make_async_copy(bound_buf, out_bound, sem)
-    copy.start()
     snap = out_s[...]
-    both_copy.wait()
-    product = mm_nt(snap, both_buf[...])
+    slab = ny * nz
+    product = sum(mm_nt(out_s[:, x * slab : (x + 1) * slab], both[x][...]) for x in range(nx))
     out_totals[:ns, :] = product[:ns, :nk] + product[:ns, nk:] + product[ns:, :nk]
     square = mm_nt(snap, snap)
     square = square[:ns, :ns] + square[:ns, ns:] + square[ns:, :ns]
@@ -370,12 +396,13 @@
     total = bb[...] + got[0][0][:, ny * nz :] if doubling("gx") else bb[...]
     for i in range(total.shape[1] // nk):
         out_bb[i * ns : (i + 1) * ns, :] = total[:, i * nk : (i + 1) * nk]
-    copy.wait()
-
-
-def step_call(kernel, shape, operands, got, out_shape, name, hbm=(), scratch=()):
-    ns, nx, ny, nz = shape
-    space = {4: pltpu.SMEM, 7: pltpu.HBM if scratch else pltpu.VMEM}
+    for x in range(nx):
+        copy(x).wait()
+
+
+def step_call(kernel, shape, operands, got, out_shape, name, hbm=(), scratch=(), aliases=None):
+    ns, nx, ny, nz = shape
+    space = {4: pltpu.SMEM}
     flat = [g for group in got for g in group]
     in_specs = [
         pl.BlockSpec(memory_space=space.get(i, pltpu.VMEM))
@@ -390,6 +417,7 @@
         ],
         out_shape=out_shape,
         scratch_shapes=[pltpu.VMEM((ns, (nx + 2) * ny * nz), f32), *scratch],
+        input_output_aliases=aliases or {},
         compiler_params=pltpu.CompilerParams(vmem_limit_bytes=vmem_limit),
         name=name,
     )(*operands, *flat)
@@ -418,14 +446,11 @@
     return jnp.where(lane[:, :n] >= sub[:, :n], work[:, :n], 0.0), work[:, n:]
 
 
-def finish_kernel(shape, nk, inverse_rows, totals, snap, both, out_modes, out_factor, out_coeffs, *scratch):
-    ns, nx, ny, nz = shape
+def finish_kernel(shape, nk, inverse_rows, totals, snap, *refs):
+    ns, nx, ny, nz = shape
+    both, (out_modes, out_factor, out_coeffs, *scratch) = refs[:nx], refs[nx:]
     slab = ny * nz
-    rest, modes, both_buf, sem, both_sem = scratch
-    part = lambda x: slice(x * slab, (x + 1) * slab)
-    both_copy = lambda x: pltpu.make_async_copy(both.at[:, part(x)], both_buf.at[:, part(x)], both_sem.at[x])
-    for x in range(nx):
-        both_copy(x).start()
+    rest, modes, sem = scratch
     coeffs = totals[:ns, :] * inverse_rows
     out_coeffs[...] = coeffs
     c_high, c_low = split(coeffs)
@@ -447,11 +472,11 @@
     def residual(j):
         if j >= pieces:
             return
-        if j % (pieces // nx) == 0:
-            both_copy(j // (pieces // nx)).wait()
         at = slice(j * width, (j + 1) * width)
         value = snap[:ns, at].astype(f32) + snap[ns:, at].astype(f32)
-        value = value - (mm(c_twice, both_buf[:, at]) + mm(c_low, both_buf[:nk, at]))
+        piece = both[at.start // slab]
+        on = slice(at.start % slab, at.start % slab + width)
+        value = value - (mm(c_twice, piece[:, on]) + mm(c_low, piece[:nk, on]))
         high, low = split(value)
         rest[:ns, at] = high
         rest[ns:, at] = low
@@ -460,13 +485,13 @@
     out_factor[...] = factor
     i_high, i_low = split(inverse)
     i_twice = jnp.concatenate([i_high, i_high], axis=1)
-    copy = lambda x: pltpu.make_async_copy(modes.at[:, x], out_modes.at[:, x], sem.at[x])
-    flat = modes.reshape(ns * nx * ny, nz)
+    copy = lambda x: pltpu.make_async_copy(modes.at[x], out_modes.at[:, x], sem.at[x])
     for x in range(nx):
         at = slice(x * slab, (x + 1) * slab)
         value = mm(i_twice, rest[:, at]) + mm(i_low, rest[:ns, at])
+        flat = modes.at[x].reshape(ns * ny, nz)
         for y in range(ny):
-            flat[pl.ds(x * ny + y, ns, stride=nx * ny), :] = value[:, y * nz : (y + 1) * nz]
+            flat[pl.ds(y, ns, stride=ny), :] = value[:, y * nz : (y + 1) * nz]
         copy(x).start()
     for x in range(nx):
         copy(x).wait()
@@ -474,11 +499,11 @@
 
 def finish(shape, inverse_rows, totals, snap, both):
     ns, nx, ny, nz = shape
-    nk = both.shape[0] // 2
+    nk = both[0].shape[0] // 2
     vmem = pl.BlockSpec(memory_space=pltpu.VMEM)
     return pl.pallas_call(
         functools.partial(finish_kernel, shape, nk, inverse_rows),
-        in_specs=[vmem, vmem, pl.BlockSpec(memory_space=pltpu.HBM)],
+        in_specs=[vmem] * (2 + nx),
         out_specs=[pl.BlockSpec(memory_space=pltpu.HBM), vmem, vmem],
         out_shape=[
             jax.ShapeDtypeStruct(shape, f32),
@@ -487,14 +512,12 @@
         ],
         scratch_shapes=[
             pltpu.VMEM((2 * ns, nx * ny * nz), bf16),
-            pltpu.VMEM(shape, f32),
-            pltpu.VMEM(both.shape, bf16),
-            pltpu.SemaphoreType.DMA((nx,)),
+            pltpu.VMEM((nx, ns, ny, nz), f32),
             pltpu.SemaphoreType.DMA((nx,)),
         ],
         compiler_params=pltpu.CompilerParams(vmem_limit_bytes=vmem_limit),
         name="finish",
-    )(totals, snap, both)
+    )(totals, snap, *both)
 
 
 def sum_over(small, large):
@@ -533,16 +556,17 @@
     ns, nx, ny, nz = shape = fine_state.shape
     nk = basis_modes.shape[0]
     cells = nx * ny * nz
-    rates = jnp.stack([on_rate, off_rate, inlet_level], axis=1)
-    (analyte, both, bb), faces = start(reduced_state.T, basis_modes, fine_state)
+    rates = [value[None] for value in (on_rate, off_rate, inlet_level)]
+    (analyte, bb, bound, rates), both, faces = start(
+        reduced_state.T, basis_modes, fine_state, bound_state, rates
+    )
     got = exchange(faces)
-    both = pltpu.with_memory_space_constraint(both, pltpu.HBM)
     fields = [velocity, zone_labels, capacity, rates]
     struct = jax.ShapeDtypeStruct
     outs = step_call(
         functools.partial(first_kernel, shape),
         shape,
-        [analyte, bound_state.reshape(ns * nx * ny, nz)] + fields + [bb],
+        [analyte, bound] + fields + [bb],
         got,
         [struct((ns, cells), f32), struct((ns, cells), f32), struct(bb.shape, f32)]
         + [
@@ -557,21 +581,19 @@
     snap, bound_next, small, large = step_call(
         functools.partial(second_kernel, shape, nk),
         shape,
-        [outs[0], outs[1]] + fields + [outs[2], both],
+        [outs[0], outs[1]] + fields + [outs[2], *both],
         got,
         [
             struct((2 * ns, cells), bf16),
-            struct((ns * nx * ny, nz), f32),
+            struct(shape, f32),
             struct((ns + ns * ns // nk, nk), f32),
             struct((bb.size // nk, nk), f32),
         ],
         "second_step",
         hbm=(1,),
         scratch=[
-            pltpu.VMEM((ns * nx * ny, nz), f32),
-            pltpu.VMEM((2 * nk, cells), bf16),
-            pltpu.SemaphoreType.DMA,
-            pltpu.SemaphoreType.DMA,
+            pltpu.VMEM((nx, ns, ny, nz), f32),
+            pltpu.SemaphoreType.DMA((nx,)),
         ],
     )
     totals = sum_over(small, large)
@@ -579,7 +601,7 @@
         cells * lax.axis_size("gx") * lax.axis_size("gy") * lax.axis_size("gz")
     )
     modes, factor, coeffs = finish(shape, inverse_rows, totals, snap, both)
-    return (modes, factor, coeffs.T, bound_next.reshape(shape))
+    return (modes, factor, coeffs.T, bound_next)
 
 
 def solution(mesh):

time: 56.1 us -> 53.1 us (0.947)
  Pallas kernels: 21.4 us -> 18.5 us
    pallas_call x1, Pallas kernels: 5.67 us -> 3.42 us  [finish(): pl.pallas_call(functools.partial(finish_kernel, shape, nk, inverse_rows),...]
    pallas_call x2, Pallas kernels: 8.54 us -> 7.7 us  [step_call(): pl.pallas_call(kernel, in_specs=in_specs, out_specs=[pl.BlockSpec(memory_...]
where the time goes in v3:
time: 53.1 us; the launch traced here: 53 us
  Pallas kernels  18.5 us (35%)
  waiting for transfers between devices  17.1 us (32%)
  starting transfers between devices  16.6 us (31%)
  between operations  0.75 us (1%)
    ppermute x8, starting transfers between devices, exchange(): got[axis].append(lax.ppermute(face, axis, pairs))  11.2 us
    ppermute x4, waiting for transfers between devices, swapped(): lax.ppermute(value, axis, [(i, i ^ stride) for i in range(size)])  10 us
    pallas_call x2, Pallas kernels, step_call(): pl.pallas_call(kernel, in_specs=in_specs, out_specs=[pl.BlockSpec(memory_...  7.7 us
    pallas_call x1, Pallas kernels, start(): pl.pallas_call(functools.partial(start_kernel, shape, nk), in_specs=[pl.B...  7.35 us
    ppermute x8, waiting for transfers between devices, exchange(): got[axis].append(lax.ppermute(face, axis, pairs))  7.08 us
    ppermute x4, starting transfers between devices, swapped(): lax.ppermute(value, axis, [(i, i ^ stride) for i in range(size)])  5.43 us
    pallas_call x1, Pallas kernels, finish(): pl.pallas_call(functools.partial(finish_kernel, shape, nk, inverse_rows),...  3.42 us
  transfers between devices with their start and end apart: 12, of which 8 were waited for; matrix products, arithmetic and copies ran while one was open for 0% of the time, Pallas kernels for 0%

profile of v3, /device:TPU:0, one launch (start us, length us, event | category | flops | bytes accessed | tf_op | source)
XLA Modules:
  0.0 53.0 jit_solution(13307119843207523362)
XLA Ops:
  0.7 7.4 %start.1 = (f32[32,8192]{1,0:T(8,128)S(1)}, f32[32,384]{1,0:T(8,128)S(1)}, f32[8,32,8,128]{3,2,1,0:T(8,128)S(1)}, f32[32,128]{1,0:T(8,128)S(1)}, bf16[256,1024]{...) custom-call(f32[32,128]{1,0:T(8,128)} %bitcast.5, ...), custom_call_target="tpu_custom_call" | custom-call | tf_op jit(solution)/shard_map/start/pallas_call | solution.py:205
  8.0 3.0 %collective-permute-start.2 = (f32[32,1408]{1,0:T(8,128)S(1)}, f32[32,1408]{1,0:T(8,128)S(1)}, u32[]{:S(2)}, u32[]{:S(2)}) collective-permute-start(f32[32,1408]{1,0:T(8,128)S(1)} %get-tuple-element.40), channel_id=1, source_target_pairs={{0,2},{2,0},{1,3},{3,1},{4,6},{6,4},{5,7},{7,5},{8,10},{10,8},{9,1... | collective-permute-start | bytes 540680 | tf_op jit(solution)/shard_map/ppermute | solution.py:123
  11.1 1.6 %collective-permute-start = (f32[32,1024]{1,0:T(8,128)S(1)}, f32[32,1024]{1,0:T(8,128)S(1)}, u32[]{:S(2)}, u32[]{:S(2)}) collective-permute-start(f32[32,1024]{1,0:T(8,128)S(1)} %get-tuple-element.38), channel_id=1, source_target_pairs={{0,4},{8,12},{4,0},{12,8},{1,5},{9,13},{5,1},{13,9},{2,6},{10,14},... | collective-permute-start | bytes 393224 | tf_op jit(solution)/shard_map/ppermute | solution.py:123
  12.6 0.7 %collective-permute-start.1 = (f32[32,1024]{1,0:T(8,128)S(1)}, f32[32,1024]{1,0:T(8,128)S(1)}, u32[]{:S(2)}, u32[]{:S(2)}) collective-permute-start(f32[32,1024]{1,0:T(8,128)S(1)} %get-tuple-element.39), channel_id=1, source_target_pairs={{4,8},{8,4},{5,9},{9,5},{6,10},{10,6},{7,11},{11,7},{20,24},{24,20... | collective-permute-start | bytes 393224 | tf_op jit(solution)/shard_map/ppermute | solution.py:123
  13.3 0.1 collective-permute-start.3
  13.4 1.2 %collective-permute-done.3.rest_3_ = f32[32,128]{1,0:T(8,128)S(1)} collective-permute-done((f32[32,128]{1,0:T(8,128)S(1)}, f32[32,128]{1,0:T(8,128)S(1)}, u32[]{:S(2)}, u32[]{:S(2)}) %collective-permute-start.3) | collective-permute-done | bytes 16416 | tf_op jit(solution)/shard_map/ppermute | solution.py:123
  14.6 1.5 %collective-permute-done.rest_0_ = f32[32,1024]{1,0:T(8,128)S(1)} collective-permute-done((f32[32,1024]{1,0:T(8,128)S(1)}, f32[32,1024]{1,0:T(8,128)S(1)}, u32[]{:S(2)}, u32[]{:S(2)}) %collective-permute-start) | collective-permute-done | bytes 131104 | tf_op jit(solution)/shard_map/ppermute | solution.py:123
  16.0 0.0 collective-permute-done.1.rest_1_
  16.1 3.3 %first_step.1 = (f32[32,8192]{1,0:T(8,128)S(1)}, f32[32,8192]{1,0:T(8,128)S(1)}, f32[32,384]{1,0:T(8,128)S(1)}, f32[32,1408]{1,0:T(8,128)S(1)}, f32[32,1024]{1,0...) custom-call(f32[32,8192]{1,0:T(8,128)S(1)} %get-tuple-element.34.analyte, ...), custom_call_target="tpu_custom_call" | custom-call | tf_op jit(solution)/shard_map/first_step/pallas_call | solution.py:411
  19.4 4.6 %collective-permute-start.4 = (f32[32,1408]{1,0:T(8,128)S(1)}, f32[32,1408]{1,0:T(8,128)S(1)}, u32[]{:S(2)}, u32[]{:S(2)}) collective-permute-start(f32[32,1408]{1,0:T(8,128)S(1)} %get-tuple-element.53), channel_id=1, source_target_pairs={{0,4},{8,12},{4,0},{12,8},{1,5},{9,13},{5,1},{13,9},{2,6},{10,14},... | collective-permute-start | bytes 540680 | tf_op jit(solution)/shard_map/ppermute | solution.py:123
  24.0 0.7 %collective-permute-start.5 = (f32[32,1024]{1,0:T(8,128)S(1)}, f32[32,1024]{1,0:T(8,128)S(1)}, u32[]{:S(2)}, u32[]{:S(2)}) collective-permute-start(f32[32,1024]{1,0:T(8,128)S(1)} %get-tuple-element.54), channel_id=1, source_target_pairs={{4,8},{8,4},{5,9},{9,5},{6,10},{10,6},{7,11},{11,7},{20,24},{24,20... | collective-permute-start | bytes 393224 | tf_op jit(solution)/shard_map/ppermute | solution.py:123
  24.6 0.6 %collective-permute-start.6 = (f32[32,1024]{1,0:T(8,128)S(1)}, f32[32,1024]{1,0:T(8,128)S(1)}, u32[]{:S(2)}, u32[]{:S(2)}) collective-permute-start(f32[32,1024]{1,0:T(8,128)S(1)} %get-tuple-element.55), channel_id=1, source_target_pairs={{0,2},{2,0},{1,3},{3,1},{4,6},{6,4},{5,7},{7,5},{8,10},{10,8},{9,1... | collective-permute-start | bytes 393224 | tf_op jit(solution)/shard_map/ppermute | solution.py:123
  25.2 1.2 %collective-permute-done.7.rest_11_ = f32[32,128]{1,0:T(8,128)S(1)} collective-permute-done((f32[32,128]{1,0:T(8,128)S(1)}, f32[32,128]{1,0:T(8,128)S(1)}, u32[]{:S(2)}, u32[]{:S(2)}) %collective-permute-start.7) | collective-permute-done | bytes 16416 | tf_op jit(solution)/shard_map/ppermute | solution.py:123
  26.4 3.2 %collective-permute-done.6.rest_10_ = f32[32,1024]{1,0:T(8,128)S(1)} collective-permute-done((f32[32,1024]{1,0:T(8,128)S(1)}, f32[32,1024]{1,0:T(8,128)S(1)}, u32[]{:S(2)}, u32[]{:S(2)}) %collective-permute-start.6) | collective-permute-done | bytes 131104 | tf_op jit(solution)/shard_map/ppermute | solution.py:123
  29.7 4.4 %second_step.1 = (bf16[64,8192]{1,0:T(8,128)(2,1)S(1)}, f32[32,8,8,128]{3,2,1,0:T(8,128)}, f32[40,128]{1,0:T(8,128)S(1)}, f32[96,128]{1,0:T(8,128)S(1)}) custom-call(f32[32,8192]{1,0:T(8,128)S(1)} %get-tuple-element.42.analyte, f32[32,8192]{1,0:T(8,128)S(1)} %get-tuple-element.43.bound, f32[8,8,128]{2,1,0:T(8,128)S(1)} %copy-done, ...), custom_call_target="tpu_custom_call" | custom-call | tf_op jit(solution)/shard_map/second_step/pallas_call | solution.py:411
  34.1 0.6 %collective-permute-start.8 = (f32[40,128]{1,0:T(8,128)S(1)}, f32[40,128]{1,0:T(8,128)S(1)}, u32[]{:S(2)}, u32[]{:S(2)}) collective-permute-start(f32[40,128]{1,0:T(8,128)S(1)} %get-tuple-element.57), channel_id=1, source_target_pairs={{0,2},{2,0},{1,3},{3,1},{4,6},{6,4},{5,7},{7,5},{8,10},{10,8},{9,1... | collective-permute-start | bytes 61448 | tf_op jit(solution)/shard_map/ppermute | solution.py:526
  34.7 3.2 %collective-permute-done.8 = f32[40,128]{1,0:T(8,128)S(1)} collective-permute-done((f32[40,128]{1,0:T(8,128)S(1)}, f32[40,128]{1,0:T(8,128)S(1)}, u32[]{:S(2)}, u32[]{:S(2)}) %collective-permute-start.8) | collective-permute-done | bytes 20512 | tf_op jit(solution)/shard_map/ppermute | solution.py:526
  37.9 3.2 %collective-permute-start.9 = (f32[40,128]{1,0:T(8,128)S(1)}, f32[40,128]{1,0:T(8,128)S(1)}, u32[]{:S(2)}, u32[]{:S(2)}) collective-permute-start(f32[40,128]{1,0:T(8,128)S(1)} %add.12), channel_id=1, source_target_pairs={{0,4},{4,0},{8,12},{12,8},{1,5},{5,1},{9,13},{13,9},{2,6},{6,2},{1... | collective-permute-start | bytes 61448 | tf_op jit(solution)/shard_map/ppermute | solution.py:526
  41.1 1.8 %collective-permute-done.9 = f32[40,128]{1,0:T(8,128)S(1)} collective-permute-done((f32[40,128]{1,0:T(8,128)S(1)}, f32[40,128]{1,0:T(8,128)S(1)}, u32[]{:S(2)}, u32[]{:S(2)}) %collective-permute-start.9) | collective-permute-done | bytes 20512 | tf_op jit(solution)/shard_map/ppermute | solution.py:526
  42.9 0.1 collective-permute-start.10
  43.0 1.2 %collective-permute-done.10 = f32[136,128]{1,0:T(8,128)S(1)} collective-permute-done((f32[136,128]{1,0:T(8,128)S(1)}, f32[136,128]{1,0:T(8,128)S(1)}, u32[]{:S(2)}, u32[]{:S(2)}) %collective-permute-start.10) | collective-permute-done | bytes 69664 | tf_op jit(solution)/shard_map/ppermute | solution.py:526
  44.3 1.5 %collective-permute-start.11 = (f32[136,128]{1,0:T(8,128)S(1)}, f32[136,128]{1,0:T(8,128)S(1)}, u32[]{:S(2)}, u32[]{:S(2)}) collective-permute-start(f32[136,128]{1,0:T(8,128)S(1)} %fusion), channel_id=1, source_target_pairs={{0,8},{4,12},{8,0},{12,4},{1,9},{5,13},{9,1},{13,5},{2,10},{6,14},... | collective-permute-start | bytes 208904 | tf_op jit(solution)/shard_map/ppermute | solution.py:526
  45.8 3.7 %collective-permute-done.11 = f32[136,128]{1,0:T(8,128)S(1)} collective-permute-done((f32[136,128]{1,0:T(8,128)S(1)}, f32[136,128]{1,0:T(8,128)S(1)}, u32[]{:S(2)}, u32[]{:S(2)}) %collective-permute-start.11) | collective-permute-done | bytes 69664 | tf_op jit(solution)/shard_map/ppermute | solution.py:526
  49.6 3.4 %finish.1 = (f32[32,8,8,128]{3,2,1,0:T(8,128)}, f32[32,32]{1,0:T(8,128)}, f32[32,128]{1,0:T(8,128)}) custom-call(f32[136,128]{1,0:T(8,128)S(1)} %add.15.totals, bf16[64,8192]{1,0:T(8,128)(2,1)S(1)} %get-tuple-element.59.snap, bf16[256,1024]{1,0:T(8,128)(2,1)S(1)} %get-tuple-element.45.rest_0_.refs_0_, ...), custom_call_target="tpu_custom_call" | custom-call | tf_op jit(solution)/shard_map/finish/pallas_call | solution.py:504
  (15 shorter events, 0.1 us)
Async XLA Ops:
  0.6 15.4 %copy-start.2 = (f32[3]{0:T(128)S(1)}, f32[3]{0:T(128)}, u32[]{:S(2)}) copy-start(f32[3]{0:T(128)} %capacity.3) | copy-start | bytes 40
  0.6 15.4 %copy-start.1 = (s32[8,8,128]{2,1,0:T(8,128)S(1)}, s32[8,8,128]{2,1,0:T(8,128)}, u32[]{:S(2)}) copy-start(s32[8,8,128]{2,1,0:T(8,128)} %zone_labels.3) | copy-start | bytes 98308
  0.7 15.4 %copy-start = (f32[8,8,128]{2,1,0:T(8,128)S(1)}, f32[8,8,128]{2,1,0:T(8,128)}, u32[]{:S(2)}) copy-start(f32[8,8,128]{2,1,0:T(8,128)} %velocity.3) | copy-start | bytes 98308
  8.0 8.0 %collective-permute-start.2 = (f32[32,1408]{1,0:T(8,128)S(1)}, f32[32,1408]{1,0:T(8,128)S(1)}, u32[]{:S(2)}, u32[]{:S(2)}) collective-permute-start(f32[32,1408]{1,0:T(8,128)S(1)} %get-tuple-element.40), channel_id=1, source_target_pairs={{0,2},{2,0},{1,3},{3,1},{4,6},{6,4},{5,7},{7,5},{8,10},{10,8},{9,1... | collective-permute-start | bytes 540680 | tf_op jit(solution)/shard_map/ppermute | solution.py:123
  11.1 5.0 %collective-permute-start = (f32[32,1024]{1,0:T(8,128)S(1)}, f32[32,1024]{1,0:T(8,128)S(1)}, u32[]{:S(2)}, u32[]{:S(2)}) collective-permute-start(f32[32,1024]{1,0:T(8,128)S(1)} %get-tuple-element.38), channel_id=1, source_target_pairs={{0,4},{8,12},{4,0},{12,8},{1,5},{9,13},{5,1},{13,9},{2,6},{10,14},... | collective-permute-start | bytes 393224 | tf_op jit(solution)/shard_map/ppermute | solution.py:123
  12.6 3.4 %collective-permute-start.1 = (f32[32,1024]{1,0:T(8,128)S(1)}, f32[32,1024]{1,0:T(8,128)S(1)}, u32[]{:S(2)}, u32[]{:S(2)}) collective-permute-start(f32[32,1024]{1,0:T(8,128)S(1)} %get-tuple-element.39), channel_id=1, source_target_pairs={{4,8},{8,4},{5,9},{9,5},{6,10},{10,6},{7,11},{11,7},{20,24},{24,20... | collective-permute-start | bytes 393224 | tf_op jit(solution)/shard_map/ppermute | solution.py:123
  13.3 1.2 %collective-permute-start.3 = (f32[32,128]{1,0:T(8,128)S(1)}, f32[32,128]{1,0:T(8,128)S(1)}, u32[]{:S(2)}, u32[]{:S(2)}) collective-permute-start(f32[32,128]{1,0:T(8,128)S(1)} %get-tuple-element.41), channel_id=1, source_target_pairs={{0,1},{1,0},{2,3},{3,2},{4,5},{5,4},{6,7},{7,6},{8,9},{9,8},{10,11... | collective-permute-start | bytes 49160 | tf_op jit(solution)/shard_map/ppermute | solution.py:123
  19.4 10.3 %collective-permute-start.4 = (f32[32,1408]{1,0:T(8,128)S(1)}, f32[32,1408]{1,0:T(8,128)S(1)}, u32[]{:S(2)}, u32[]{:S(2)}) collective-permute-start(f32[32,1408]{1,0:T(8,128)S(1)} %get-tuple-element.53), channel_id=1, source_target_pairs={{0,4},{8,12},{4,0},{12,8},{1,5},{9,13},{5,1},{13,9},{2,6},{10,14},... | collective-permute-start | bytes 540680 | tf_op jit(solution)/shard_map/ppermute | solution.py:123
  24.0 2.5 %collective-permute-start.5 = (f32[32,1024]{1,0:T(8,128)S(1)}, f32[32,1024]{1,0:T(8,128)S(1)}, u32[]{:S(2)}, u32[]{:S(2)}) collective-permute-start(f32[32,1024]{1,0:T(8,128)S(1)} %get-tuple-element.54), channel_id=1, source_target_pairs={{4,8},{8,4},{5,9},{9,5},{6,10},{10,6},{7,11},{11,7},{20,24},{24,20... | collective-permute-start | bytes 393224 | tf_op jit(solution)/shard_map/ppermute | solution.py:123
  24.6 5.0 %collective-permute-start.6 = (f32[32,1024]{1,0:T(8,128)S(1)}, f32[32,1024]{1,0:T(8,128)S(1)}, u32[]{:S(2)}, u32[]{:S(2)}) collective-permute-start(f32[32,1024]{1,0:T(8,128)S(1)} %get-tuple-element.55), channel_id=1, source_target_pairs={{0,2},{2,0},{1,3},{3,1},{4,6},{6,4},{5,7},{7,5},{8,10},{10,8},{9,1... | collective-permute-start | bytes 393224 | tf_op jit(solution)/shard_map/ppermute | solution.py:123
  25.2 1.2 %collective-permute-start.7 = (f32[32,128]{1,0:T(8,128)S(1)}, f32[32,128]{1,0:T(8,128)S(1)}, u32[]{:S(2)}, u32[]{:S(2)}) collective-permute-start(f32[32,128]{1,0:T(8,128)S(1)} %get-tuple-element.56), channel_id=1, source_target_pairs={{0,1},{1,0},{2,3},{3,2},{4,5},{5,4},{6,7},{7,6},{8,9},{9,8},{10,11... | collective-permute-start | bytes 49160 | tf_op jit(solution)/shard_map/ppermute | solution.py:123
  34.1 3.8 %collective-permute-start.8 = (f32[40,128]{1,0:T(8,128)S(1)}, f32[40,128]{1,0:T(8,128)S(1)}, u32[]{:S(2)}, u32[]{:S(2)}) collective-permute-start(f32[40,128]{1,0:T(8,128)S(1)} %get-tuple-element.57), channel_id=1, source_target_pairs={{0,2},{2,0},{1,3},{3,1},{4,6},{6,4},{5,7},{7,5},{8,10},{10,8},{9,1... | collective-permute-start | bytes 61448 | tf_op jit(solution)/shard_map/ppermute | solution.py:526
  37.9 5.0 %collective-permute-start.9 = (f32[40,128]{1,0:T(8,128)S(1)}, f32[40,128]{1,0:T(8,128)S(1)}, u32[]{:S(2)}, u32[]{:S(2)}) collective-permute-start(f32[40,128]{1,0:T(8,128)S(1)} %add.12), channel_id=1, source_target_pairs={{0,4},{4,0},{8,12},{12,8},{1,5},{5,1},{9,13},{13,9},{2,6},{6,2},{1... | collective-permute-start | bytes 61448 | tf_op jit(solution)/shard_map/ppermute | solution.py:526
  42.9 1.3 %collective-permute-start.10 = (f32[136,128]{1,0:T(8,128)S(1)}, f32[136,128]{1,0:T(8,128)S(1)}, u32[]{:S(2)}, u32[]{:S(2)}) collective-permute-start(f32[136,128]{1,0:T(8,128)S(1)} %pad_maximum_fusion), channel_id=1, source_target_pairs={{0,1},{1,0},{2,3},{3,2},{4,5},{5,4},{6,7},{7,6},{8,9},{9,8},{10,11... | collective-permute-start | bytes 208904 | tf_op jit(solution)/shard_map/ppermute | solution.py:526
  44.3 5.3 %collective-permute-start.11 = (f32[136,128]{1,0:T(8,128)S(1)}, f32[136,128]{1,0:T(8,128)S(1)}, u32[]{:S(2)}, u32[]{:S(2)}) collective-permute-start(f32[136,128]{1,0:T(8,128)S(1)} %fusion), channel_id=1, source_target_pairs={{0,8},{4,12},{8,0},{12,4},{1,9},{5,13},{9,1},{13,5},{2,10},{6,14},... | collective-permute-start | bytes 208904 | tf_op jit(solution)/shard_map/ppermute | solution.py:526

commit v4 on v3

--- a/solution.py
+++ b/solution.py
@@ -23,6 +23,15 @@
     return jnp.dot(a, b, preferred_element_type=f32)
 
 
+def aligned(offset, size):
+    return offset if isinstance(offset, int) else pl.multiple_of(offset, size)
+
+
+def stacked(high, low):
+    low = jnp.concatenate([low, jnp.zeros_like(low)], axis=1)
+    return jnp.concatenate([jnp.concatenate([high, high], axis=1), low], axis=0)
+
+
 def mm_nt(a, b):
     return lax.dot_general(a, b, (((1,), (1,)), ((), ())), preferred_element_type=f32)
 
@@ -50,6 +59,20 @@
     after = lax.rem(cell + 1, tile.shape[1])
     shifts = [jnp.where(faces_up(axis, i), after, cell) for i in range(len(packed))]
     return [jnp.where(here, pltpu.roll(tile, s, 1), p) for p, s in zip(packed, shifts)]
+
+
+def pack_columns(refs, field, shape):
+    ns, nx, ny, nz = shape
+
+    def body(x, packed):
+        for y in range(ny):
+            tile = field[:, pl.ds(pl.multiple_of(x * ny * nz, ny * nz) + y * nz, nz)]
+            packed = pack_column(packed, "gz", tile, x * ny + y)
+        return packed
+
+    packed = lax.fori_loop(0, nx, body, [jnp.zeros((ns, nz), f32) for _ in refs])
+    for ref, value in zip(refs, packed):
+        ref[...] = value
 
 
 def copy_faces(faces, field, shape, extra):
@@ -149,7 +172,7 @@
         bound_copy(x).start()
     r_copy.wait()
     r_high, r_low = split(r_buf[...])
-    r_twice = jnp.concatenate([r_high, r_high], axis=1)
+    r_all = stacked(r_high, r_low)
     for copy in rate_copies:
         copy.wait()
     lane = lax.broadcasted_iota(jnp.int32, (ns, ns), 1)
@@ -164,8 +187,9 @@
     group = max(1, min(ny, 256 // nz))
 
     def body(x, packed):
-        b_copy(x).wait()
-
+        if x % 4 == 0:
+            for i in range(x, min(x + 4, nx)):
+                b_copy(i).wait()
         if x == 0:
             f_copy.wait()
         flat = b_buf.at[x].reshape(nk * ny, nz)
@@ -177,7 +201,8 @@
             low = jnp.concatenate([p[1] for p in parts], axis=1)
             both[x][:nk, pl.ds(y * nz, group * nz)] = high
             both[x][nk:, pl.ds(y * nz, group * nz)] = low
-            slab = mm(r_twice, jnp.concatenate([high, low], axis=0)) + mm(r_low, high)
+            slab = mm(r_all, jnp.concatenate([high, low], axis=0))
+            slab = slab[:ns] + slab[ns:]
             for i in range(group):
                 tile = slab[:, i * nz : (i + 1) * nz] + rows[pl.ds(y + i, ns, stride=ny), :]
                 out_a[:, pl.ds(at + i * nz, nz)] = tile
@@ -257,16 +282,16 @@
     on = jnp.broadcast_to(rates[:, 0:1], (ns, nz))
     off = jnp.broadcast_to(rates[:, 1:2], (ns, nz))
     lane = lax.broadcasted_iota(jnp.int32, (ns, nz), 1)
-    x_at = pl.multiple_of(x * nz, nz)
+    x_at = aligned(x * nz, nz)
     y_at = [ref.at[:, pl.ds(x_at, nz)] for ref in y_got]
     left, right = lane == 0, lane == nz - 1
     inner = lane == jnp.where(first["gz"], nz - 1, 0)
     inner_low = lane == jnp.where(first["gz"], -1, 0)
     inner_high = lane == jnp.where(last["gz"], -1, nz - 1)
     for y in range(ny):
-        at = pl.multiple_of(x * ny * nz, nz) + y * nz
+        at = aligned(x * ny * nz, nz) + y * nz
         tile = lambda slabs_on, rows_on: pad[
-            :, pl.ds(pl.multiple_of(at + (slabs_on * ny + rows_on) * nz, nz), nz)
+            :, pl.ds(aligned(at + (slabs_on * ny + rows_on) * nz, nz), nz)
         ]
         centre, behind, ahead = tile(1, 0), tile(0, 0), tile(2, 0)
         if y > 0:
@@ -334,8 +359,7 @@
     faces, (pad,) = unflatten(rest[3:])
     fill_pad(shape, pad, analyte, got[0], rates)
 
-    def body(x, packed):
-        packs = [packed]
+    def body(x):
 
         rows = bound.at[x].reshape(ns * ny, nz)
 
@@ -345,16 +369,13 @@
         def store(cell, y, at, moved, bound_then):
             out_bound[:, pl.ds(at, nz)] = bound_then
             out_a[:, pl.ds(at, nz)] = moved
-            packs[0] = pack_column(packs[0], "gz", moved, cell)
 
         stencil(
             shape, x, pad, got[1], got[2], bound_tile, store, (velocity, zone_labels, capacity, rates)
         )
-        return packs[0]
-
-    packed = lax.fori_loop(0, nx, body, [jnp.zeros((ns, nz), f32) for _ in faces[2]])
-    for ref, value in zip(faces[2], packed):
-        ref[...] = value
+    for x in range(nx):
+        body(x)
+    pack_columns(faces[2], out_a, shape)
     out_bb[...] = bb[...] + got[1][0][:, nx * nz :] if doubling("gy") else bb[...]
     copy_faces(faces, out_a, shape, {"gx": out_bb[...]} if doubling("gx") else {})
 
@@ -385,7 +406,8 @@
         return carry
 
     copy = lambda x: pltpu.make_async_copy(bound_buf.at[x], out_bound.at[:, x], sem.at[x])
-    lax.fori_loop(0, nx, body, 0)
+    for x in range(nx):
+        body(x, 0)
     snap = out_s[...]
     slab = ny * nz
     product = sum(mm_nt(out_s[:, x * slab : (x + 1) * slab], both[x][...]) for x in range(nx))
@@ -454,7 +476,7 @@
     coeffs = totals[:ns, :] * inverse_rows
     out_coeffs[...] = coeffs
     c_high, c_low = split(coeffs)
-    c_twice = jnp.concatenate([c_high, c_high], axis=1)
+    c_all = stacked(c_high, c_low)
     squares = ns + ns * ns // nk
     weighted = mm_exact(coeffs, unpack_symmetric(totals[squares:, :] * inverse_rows))
     exact_nt = functools.partial(
@@ -476,7 +498,8 @@
         value = snap[:ns, at].astype(f32) + snap[ns:, at].astype(f32)
         piece = both[at.start // slab]
         on = slice(at.start % slab, at.start % slab + width)
-        value = value - (mm(c_twice, piece[:, on]) + mm(c_low, piece[:nk, on]))
+        product = mm(c_all, piece[:, on])
+        value = value - (product[:ns] + product[ns:])
         high, low = split(value)
         rest[:ns, at] = high
         rest[ns:, at] = low
@@ -484,11 +507,12 @@
     factor, inverse = eliminate(gram, 8 if ns % 8 == 0 else 1, residual)
     out_factor[...] = factor
     i_high, i_low = split(inverse)
-    i_twice = jnp.concatenate([i_high, i_high], axis=1)
+    i_all = stacked(i_high, i_low)
     copy = lambda x: pltpu.make_async_copy(modes.at[x], out_modes.at[:, x], sem.at[x])
     for x in range(nx):
         at = slice(x * slab, (x + 1) * slab)
-        value = mm(i_twice, rest[:, at]) + mm(i_low, rest[:ns, at])
+        value = mm(i_all, rest[:, at])
+        value = value[:ns] + value[ns:]
         flat = modes.at[x].reshape(ns * ny, nz)
         for y in range(ny):
             flat[pl.ds(y, ns, stride=ny), :] = value[:, y * nz : (y + 1) * nz]

time: 53.1 us -> 50.4 us (0.949)
  Pallas kernels: 18.5 us -> 15.7 us
    pallas_call x2, Pallas kernels: 7.7 us -> 6.19 us  [step_call(): pl.pallas_call(kernel, in_specs=in_specs, out_specs=[pl.BlockSpec(memory_...]
    pallas_call x1, Pallas kernels: 7.35 us -> 6.04 us  [start(): pl.pallas_call(functools.partial(start_kernel, shape, nk), in_specs=[pl.B...]
where the time goes in v4:
time: 50.4 us; the launch traced here: 50.2 us
  waiting for transfers between devices  17.1 us (34%)
  starting transfers between devices  16.6 us (33%)
  Pallas kernels  15.7 us (31%)
  between operations  0.75 us (1%)
    ppermute x8, starting transfers between devices, exchange(): got[axis].append(lax.ppermute(face, axis, pairs))  11.2 us
    ppermute x4, waiting for transfers between devices, swapped(): lax.ppermute(value, axis, [(i, i ^ stride) for i in range(size)])  9.99 us
    ppermute x8, waiting for transfers between devices, exchange(): got[axis].append(lax.ppermute(face, axis, pairs))  7.07 us
    pallas_call x2, Pallas kernels, step_call(): pl.pallas_call(kernel, in_specs=in_specs, out_specs=[pl.BlockSpec(memory_...  6.19 us
    pallas_call x1, Pallas kernels, start(): pl.pallas_call(functools.partial(start_kernel, shape, nk), in_specs=[pl.B...  6.04 us
    ppermute x4, starting transfers between devices, swapped(): lax.ppermute(value, axis, [(i, i ^ stride) for i in range(size)])  5.43 us
    pallas_call x1, Pallas kernels, finish(): pl.pallas_call(functools.partial(finish_kernel, shape, nk, inverse_rows),...  3.47 us
  transfers between devices with their start and end apart: 12, of which 8 were waited for; matrix products, arithmetic and copies ran while one was open for 0% of the time, Pallas kernels for 0%

profile of v4, /device:TPU:0, one launch (start us, length us, event | category | flops | bytes accessed | tf_op | source)
XLA Modules:
  0.0 50.2 jit_solution(11370081963450619968)
XLA Ops:
  0.7 6.0 %start.1 = (f32[32,8192]{1,0:T(8,128)S(1)}, f32[32,384]{1,0:T(8,128)S(1)}, f32[8,32,8,128]{3,2,1,0:T(8,128)S(1)}, f32[32,128]{1,0:T(8,128)S(1)}, bf16[256,1024]{...) custom-call(f32[32,128]{1,0:T(8,128)} %bitcast.5, ...), custom_call_target="tpu_custom_call" | custom-call | tf_op jit(solution)/shard_map/start/pallas_call | solution.py:230
  6.7 3.0 %collective-permute-start.2 = (f32[32,1408]{1,0:T(8,128)S(1)}, f32[32,1408]{1,0:T(8,128)S(1)}, u32[]{:S(2)}, u32[]{:S(2)}) collective-permute-start(f32[32,1408]{1,0:T(8,128)S(1)} %get-tuple-element.40), channel_id=1, source_target_pairs={{0,2},{2,0},{1,3},{3,1},{4,6},{6,4},{5,7},{7,5},{8,10},{10,8},{9,1... | collective-permute-start | bytes 540680 | tf_op jit(solution)/shard_map/ppermute | solution.py:146
  9.7 1.6 %collective-permute-start = (f32[32,1024]{1,0:T(8,128)S(1)}, f32[32,1024]{1,0:T(8,128)S(1)}, u32[]{:S(2)}, u32[]{:S(2)}) collective-permute-start(f32[32,1024]{1,0:T(8,128)S(1)} %get-tuple-element.38), channel_id=1, source_target_pairs={{0,4},{8,12},{4,0},{12,8},{1,5},{9,13},{5,1},{13,9},{2,6},{10,14},... | collective-permute-start | bytes 393224 | tf_op jit(solution)/shard_map/ppermute | solution.py:146
  11.3 0.7 %collective-permute-start.1 = (f32[32,1024]{1,0:T(8,128)S(1)}, f32[32,1024]{1,0:T(8,128)S(1)}, u32[]{:S(2)}, u32[]{:S(2)}) collective-permute-start(f32[32,1024]{1,0:T(8,128)S(1)} %get-tuple-element.39), channel_id=1, source_target_pairs={{4,8},{8,4},{5,9},{9,5},{6,10},{10,6},{7,11},{11,7},{20,24},{24,20... | collective-permute-start | bytes 393224 | tf_op jit(solution)/shard_map/ppermute | solution.py:146
  12.0 0.1 collective-permute-start.3
  12.1 1.2 %collective-permute-done.3.rest_3_ = f32[32,128]{1,0:T(8,128)S(1)} collective-permute-done((f32[32,128]{1,0:T(8,128)S(1)}, f32[32,128]{1,0:T(8,128)S(1)}, u32[]{:S(2)}, u32[]{:S(2)}) %collective-permute-start.3) | collective-permute-done | bytes 16416 | tf_op jit(solution)/shard_map/ppermute | solution.py:146
  13.2 1.5 %collective-permute-done.rest_0_ = f32[32,1024]{1,0:T(8,128)S(1)} collective-permute-done((f32[32,1024]{1,0:T(8,128)S(1)}, f32[32,1024]{1,0:T(8,128)S(1)}, u32[]{:S(2)}, u32[]{:S(2)}) %collective-permute-start) | collective-permute-done | bytes 131104 | tf_op jit(solution)/shard_map/ppermute | solution.py:146
  14.7 0.0 collective-permute-done.1.rest_1_
  14.7 2.8 %first_step.1 = (f32[32,8192]{1,0:T(8,128)S(1)}, f32[32,8192]{1,0:T(8,128)S(1)}, f32[32,384]{1,0:T(8,128)S(1)}, f32[32,1408]{1,0:T(8,128)S(1)}, f32[32,1024]{1,0...) custom-call(f32[32,8192]{1,0:T(8,128)S(1)} %get-tuple-element.34.analyte, ...), custom_call_target="tpu_custom_call" | custom-call | tf_op jit(solution)/shard_map/first_step/pallas_call | solution.py:433
  17.5 4.6 %collective-permute-start.4 = (f32[32,1408]{1,0:T(8,128)S(1)}, f32[32,1408]{1,0:T(8,128)S(1)}, u32[]{:S(2)}, u32[]{:S(2)}) collective-permute-start(f32[32,1408]{1,0:T(8,128)S(1)} %get-tuple-element.53), channel_id=1, source_target_pairs={{0,4},{8,12},{4,0},{12,8},{1,5},{9,13},{5,1},{13,9},{2,6},{10,14},... | collective-permute-start | bytes 540680 | tf_op jit(solution)/shard_map/ppermute | solution.py:146
  22.1 0.7 %collective-permute-start.5 = (f32[32,1024]{1,0:T(8,128)S(1)}, f32[32,1024]{1,0:T(8,128)S(1)}, u32[]{:S(2)}, u32[]{:S(2)}) collective-permute-start(f32[32,1024]{1,0:T(8,128)S(1)} %get-tuple-element.54), channel_id=1, source_target_pairs={{4,8},{8,4},{5,9},{9,5},{6,10},{10,6},{7,11},{11,7},{20,24},{24,20... | collective-permute-start | bytes 393224 | tf_op jit(solution)/shard_map/ppermute | solution.py:146
  22.8 0.6 %collective-permute-start.6 = (f32[32,1024]{1,0:T(8,128)S(1)}, f32[32,1024]{1,0:T(8,128)S(1)}, u32[]{:S(2)}, u32[]{:S(2)}) collective-permute-start(f32[32,1024]{1,0:T(8,128)S(1)} %get-tuple-element.55), channel_id=1, source_target_pairs={{0,2},{2,0},{1,3},{3,1},{4,6},{6,4},{5,7},{7,5},{8,10},{10,8},{9,1... | collective-permute-start | bytes 393224 | tf_op jit(solution)/shard_map/ppermute | solution.py:146
  23.4 1.2 %collective-permute-done.7.rest_11_ = f32[32,128]{1,0:T(8,128)S(1)} collective-permute-done((f32[32,128]{1,0:T(8,128)S(1)}, f32[32,128]{1,0:T(8,128)S(1)}, u32[]{:S(2)}, u32[]{:S(2)}) %collective-permute-start.7) | collective-permute-done | bytes 16416 | tf_op jit(solution)/shard_map/ppermute | solution.py:146
  24.6 3.2 %collective-permute-done.6.rest_10_ = f32[32,1024]{1,0:T(8,128)S(1)} collective-permute-done((f32[32,1024]{1,0:T(8,128)S(1)}, f32[32,1024]{1,0:T(8,128)S(1)}, u32[]{:S(2)}, u32[]{:S(2)}) %collective-permute-start.6) | collective-permute-done | bytes 131104 | tf_op jit(solution)/shard_map/ppermute | solution.py:146
  27.8 3.4 %second_step.1 = (bf16[64,8192]{1,0:T(8,128)(2,1)S(1)}, f32[32,8,8,128]{3,2,1,0:T(8,128)}, f32[40,128]{1,0:T(8,128)S(1)}, f32[96,128]{1,0:T(8,128)S(1)}) custom-call(f32[32,8192]{1,0:T(8,128)S(1)} %get-tuple-element.42.analyte, f32[32,8192]{1,0:T(8,128)S(1)} %get-tuple-element.43.bound, f32[8,8,128]{2,1,0:T(8,128)S(1)} %copy-done, ...), custom_call_target="tpu_custom_call" | custom-call | tf_op jit(solution)/shard_map/second_step/pallas_call | solution.py:433
  31.2 0.6 %collective-permute-start.8 = (f32[40,128]{1,0:T(8,128)S(1)}, f32[40,128]{1,0:T(8,128)S(1)}, u32[]{:S(2)}, u32[]{:S(2)}) collective-permute-start(f32[40,128]{1,0:T(8,128)S(1)} %get-tuple-element.57), channel_id=1, source_target_pairs={{0,2},{2,0},{1,3},{3,1},{4,6},{6,4},{5,7},{7,5},{8,10},{10,8},{9,1... | collective-permute-start | bytes 61448 | tf_op jit(solution)/shard_map/ppermute | solution.py:550
  31.8 3.2 %collective-permute-done.8 = f32[40,128]{1,0:T(8,128)S(1)} collective-permute-done((f32[40,128]{1,0:T(8,128)S(1)}, f32[40,128]{1,0:T(8,128)S(1)}, u32[]{:S(2)}, u32[]{:S(2)}) %collective-permute-start.8) | collective-permute-done | bytes 20512 | tf_op jit(solution)/shard_map/ppermute | solution.py:550
  35.1 3.2 %collective-permute-start.9 = (f32[40,128]{1,0:T(8,128)S(1)}, f32[40,128]{1,0:T(8,128)S(1)}, u32[]{:S(2)}, u32[]{:S(2)}) collective-permute-start(f32[40,128]{1,0:T(8,128)S(1)} %add.12), channel_id=1, source_target_pairs={{0,4},{4,0},{8,12},{12,8},{1,5},{5,1},{9,13},{13,9},{2,6},{6,2},{1... | collective-permute-start | bytes 61448 | tf_op jit(solution)/shard_map/ppermute | solution.py:550
  38.3 1.8 %collective-permute-done.9 = f32[40,128]{1,0:T(8,128)S(1)} collective-permute-done((f32[40,128]{1,0:T(8,128)S(1)}, f32[40,128]{1,0:T(8,128)S(1)}, u32[]{:S(2)}, u32[]{:S(2)}) %collective-permute-start.9) | collective-permute-done | bytes 20512 | tf_op jit(solution)/shard_map/ppermute | solution.py:550
  40.1 0.1 collective-permute-start.10
  40.2 1.2 %collective-permute-done.10 = f32[136,128]{1,0:T(8,128)S(1)} collective-permute-done((f32[136,128]{1,0:T(8,128)S(1)}, f32[136,128]{1,0:T(8,128)S(1)}, u32[]{:S(2)}, u32[]{:S(2)}) %collective-permute-start.10) | collective-permute-done | bytes 69664 | tf_op jit(solution)/shard_map/ppermute | solution.py:550
  41.4 1.5 %collective-permute-start.11 = (f32[136,128]{1,0:T(8,128)S(1)}, f32[136,128]{1,0:T(8,128)S(1)}, u32[]{:S(2)}, u32[]{:S(2)}) collective-permute-start(f32[136,128]{1,0:T(8,128)S(1)} %fusion), channel_id=1, source_target_pairs={{0,8},{4,12},{8,0},{12,4},{1,9},{5,13},{9,1},{13,5},{2,10},{6,14},... | collective-permute-start | bytes 208904 | tf_op jit(solution)/shard_map/ppermute | solution.py:550
  43.0 3.7 %collective-permute-done.11 = f32[136,128]{1,0:T(8,128)S(1)} collective-permute-done((f32[136,128]{1,0:T(8,128)S(1)}, f32[136,128]{1,0:T(8,128)S(1)}, u32[]{:S(2)}, u32[]{:S(2)}) %collective-permute-start.11) | collective-permute-done | bytes 69664 | tf_op jit(solution)/shard_map/ppermute | solution.py:550
  46.7 3.5 %finish.1 = (f32[32,8,8,128]{3,2,1,0:T(8,128)}, f32[32,32]{1,0:T(8,128)}, f32[32,128]{1,0:T(8,128)}) custom-call(f32[136,128]{1,0:T(8,128)S(1)} %add.15.totals, bf16[64,8192]{1,0:T(8,128)(2,1)S(1)} %get-tuple-element.59.snap, bf16[256,1024]{1,0:T(8,128)(2,1)S(1)} %get-tuple-element.45.rest_0_.refs_0_, ...), custom_call_target="tpu_custom_call" | custom-call | tf_op jit(solution)/shard_map/finish/pallas_call | solution.py:528
  (15 shorter events, 0.1 us)
Async XLA Ops:
  0.6 14.1 %copy-start.2 = (f32[3]{0:T(128)S(1)}, f32[3]{0:T(128)}, u32[]{:S(2)}) copy-start(f32[3]{0:T(128)} %capacity.3) | copy-start | bytes 40
  0.6 14.1 %copy-start.1 = (s32[8,8,128]{2,1,0:T(8,128)S(1)}, s32[8,8,128]{2,1,0:T(8,128)}, u32[]{:S(2)}) copy-start(s32[8,8,128]{2,1,0:T(8,128)} %zone_labels.3) | copy-start | bytes 98308
  0.7 14.1 %copy-start = (f32[8,8,128]{2,1,0:T(8,128)S(1)}, f32[8,8,128]{2,1,0:T(8,128)}, u32[]{:S(2)}) copy-start(f32[8,8,128]{2,1,0:T(8,128)} %velocity.3) | copy-start | bytes 98308
  6.7 8.0 %collective-permute-start.2 = (f32[32,1408]{1,0:T(8,128)S(1)}, f32[32,1408]{1,0:T(8,128)S(1)}, u32[]{:S(2)}, u32[]{:S(2)}) collective-permute-start(f32[32,1408]{1,0:T(8,128)S(1)} %get-tuple-element.40), channel_id=1, source_target_pairs={{0,2},{2,0},{1,3},{3,1},{4,6},{6,4},{5,7},{7,5},{8,10},{10,8},{9,1... | collective-permute-start | bytes 540680 | tf_op jit(solution)/shard_map/ppermute | solution.py:146
  9.7 5.0 %collective-permute-start = (f32[32,1024]{1,0:T(8,128)S(1)}, f32[32,1024]{1,0:T(8,128)S(1)}, u32[]{:S(2)}, u32[]{:S(2)}) collective-permute-start(f32[32,1024]{1,0:T(8,128)S(1)} %get-tuple-element.38), channel_id=1, source_target_pairs={{0,4},{8,12},{4,0},{12,8},{1,5},{9,13},{5,1},{13,9},{2,6},{10,14},... | collective-permute-start | bytes 393224 | tf_op jit(solution)/shard_map/ppermute | solution.py:146
  11.3 3.4 %collective-permute-start.1 = (f32[32,1024]{1,0:T(8,128)S(1)}, f32[32,1024]{1,0:T(8,128)S(1)}, u32[]{:S(2)}, u32[]{:S(2)}) collective-permute-start(f32[32,1024]{1,0:T(8,128)S(1)} %get-tuple-element.39), channel_id=1, source_target_pairs={{4,8},{8,4},{5,9},{9,5},{6,10},{10,6},{7,11},{11,7},{20,24},{24,20... | collective-permute-start | bytes 393224 | tf_op jit(solution)/shard_map/ppermute | solution.py:146
  12.0 1.2 %collective-permute-start.3 = (f32[32,128]{1,0:T(8,128)S(1)}, f32[32,128]{1,0:T(8,128)S(1)}, u32[]{:S(2)}, u32[]{:S(2)}) collective-permute-start(f32[32,128]{1,0:T(8,128)S(1)} %get-tuple-element.41), channel_id=1, source_target_pairs={{0,1},{1,0},{2,3},{3,2},{4,5},{5,4},{6,7},{7,6},{8,9},{9,8},{10,11... | collective-permute-start | bytes 49160 | tf_op jit(solution)/shard_map/ppermute | solution.py:146
  17.5 10.3 %collective-permute-start.4 = (f32[32,1408]{1,0:T(8,128)S(1)}, f32[32,1408]{1,0:T(8,128)S(1)}, u32[]{:S(2)}, u32[]{:S(2)}) collective-permute-start(f32[32,1408]{1,0:T(8,128)S(1)} %get-tuple-element.53), channel_id=1, source_target_pairs={{0,4},{8,12},{4,0},{12,8},{1,5},{9,13},{5,1},{13,9},{2,6},{10,14},... | collective-permute-start | bytes 540680 | tf_op jit(solution)/shard_map/ppermute | solution.py:146
  22.1 2.5 %collective-permute-start.5 = (f32[32,1024]{1,0:T(8,128)S(1)}, f32[32,1024]{1,0:T(8,128)S(1)}, u32[]{:S(2)}, u32[]{:S(2)}) collective-permute-start(f32[32,1024]{1,0:T(8,128)S(1)} %get-tuple-element.54), channel_id=1, source_target_pairs={{4,8},{8,4},{5,9},{9,5},{6,10},{10,6},{7,11},{11,7},{20,24},{24,20... | collective-permute-start | bytes 393224 | tf_op jit(solution)/shard_map/ppermute | solution.py:146
  22.8 5.0 %collective-permute-start.6 = (f32[32,1024]{1,0:T(8,128)S(1)}, f32[32,1024]{1,0:T(8,128)S(1)}, u32[]{:S(2)}, u32[]{:S(2)}) collective-permute-start(f32[32,1024]{1,0:T(8,128)S(1)} %get-tuple-element.55), channel_id=1, source_target_pairs={{0,2},{2,0},{1,3},{3,1},{4,6},{6,4},{5,7},{7,5},{8,10},{10,8},{9,1... | collective-permute-start | bytes 393224 | tf_op jit(solution)/shard_map/ppermute | solution.py:146
  23.4 1.2 %collective-permute-start.7 = (f32[32,128]{1,0:T(8,128)S(1)}, f32[32,128]{1,0:T(8,128)S(1)}, u32[]{:S(2)}, u32[]{:S(2)}) collective-permute-start(f32[32,128]{1,0:T(8,128)S(1)} %get-tuple-element.56), channel_id=1, source_target_pairs={{0,1},{1,0},{2,3},{3,2},{4,5},{5,4},{6,7},{7,6},{8,9},{9,8},{10,11... | collective-permute-start | bytes 49160 | tf_op jit(solution)/shard_map/ppermute | solution.py:146
  31.2 3.8 %collective-permute-start.8 = (f32[40,128]{1,0:T(8,128)S(1)}, f32[40,128]{1,0:T(8,128)S(1)}, u32[]{:S(2)}, u32[]{:S(2)}) collective-permute-start(f32[40,128]{1,0:T(8,128)S(1)} %get-tuple-element.57), channel_id=1, source_target_pairs={{0,2},{2,0},{1,3},{3,1},{4,6},{6,4},{5,7},{7,5},{8,10},{10,8},{9,1... | collective-permute-start | bytes 61448 | tf_op jit(solution)/shard_map/ppermute | solution.py:550
  35.1 5.0 %collective-permute-start.9 = (f32[40,128]{1,0:T(8,128)S(1)}, f32[40,128]{1,0:T(8,128)S(1)}, u32[]{:S(2)}, u32[]{:S(2)}) collective-permute-start(f32[40,128]{1,0:T(8,128)S(1)} %add.12), channel_id=1, source_target_pairs={{0,4},{4,0},{8,12},{12,8},{1,5},{5,1},{9,13},{13,9},{2,6},{6,2},{1... | collective-permute-start | bytes 61448 | tf_op jit(solution)/shard_map/ppermute | solution.py:550
  40.1 1.3 %collective-permute-start.10 = (f32[136,128]{1,0:T(8,128)S(1)}, f32[136,128]{1,0:T(8,128)S(1)}, u32[]{:S(2)}, u32[]{:S(2)}) collective-permute-start(f32[136,128]{1,0:T(8,128)S(1)} %pad_maximum_fusion), channel_id=1, source_target_pairs={{0,1},{1,0},{2,3},{3,2},{4,5},{5,4},{6,7},{7,6},{8,9},{9,8},{10,11... | collective-permute-start | bytes 208904 | tf_op jit(solution)/shard_map/ppermute | solution.py:550
  41.4 5.3 %collective-permute-start.11 = (f32[136,128]{1,0:T(8,128)S(1)}, f32[136,128]{1,0:T(8,128)S(1)}, u32[]{:S(2)}, u32[]{:S(2)}) collective-permute-start(f32[136,128]{1,0:T(8,128)S(1)} %fusion), channel_id=1, source_target_pairs={{0,8},{4,12},{8,0},{12,4},{1,9},{5,13},{9,1},{13,5},{2,10},{6,14},... | collective-permute-start | bytes 208904 | tf_op jit(solution)/shard_map/ppermute | solution.py:550
